TPU v7x, 256 devices: a whole 4x4x8 slice. The times are simulated.
256 devices in a mesh: segment: 4 (over x_lo, core), dp: 64 (over z, x_hi, y).
Axes of the slice: x: 4 (x_hi: 2, x_lo: 2; x = x_hi * 2 + x_lo), y: 4, z: 8, core: 2. Of those that a mesh axis runs over, the one named last changes fastest.
Arguments:
- latents: bfloat16 [128, 16, 16, 320], P('dp'), may hold values from -6 to 6
- cotangent: bfloat16 [128, 16, 16, 320], P('dp'), may hold values from -6 to 6
- bucket: int32 [128, 2], P('dp'), may hold values from 8 to 16, as said below
- timesteps: int32 [128], P('dp'), may hold values from 0 to 999
- w_enc: bfloat16 [4, 3, 3, 320, 320], P('segment'), may hold values from -0.109375 to 0.109375
- w_dec: bfloat16 [4, 3, 3, 320, 320], P('segment'), may hold values from -0.109375 to 0.109375
- w_time: bfloat16 [4, 2, 320, 320], P('segment'), may hold values from -0.3125 to 0.3125
Outputs:
- grad_enc: float32 [4, 3, 3, 320, 320], P('segment')
- grad_dec: float32 [4, 3, 3, 320, 320], P('segment')
Inputs may be any that keep to these rules, and one draw needn't show every extreme that they name: `bucket`: row b holds the height and width of the valid region at the start of microbatch b's 16 x 16 crop; in every draw some microbatch is 16 x 16 and another 16 // 2 x 16 // 2.
All inputs are finite; a program needn't handle non-finite values.
Results may differ from a plain program's by a relative error of at most 0.018.
Values may be sent and summed in bfloat16 or wider, within the bound.
No kernel may reach another device: no remote copies, remote signals or barrier semaphores. Data moves between devices by JAX's collectives and lax.ppermute only.
A program may use at most 128 MiB of HBM per device.

v0:
```python
import functools
import math

import jax
import jax.numpy as jnp
import numpy as np
from jax import lax
from jax.experimental import pallas as pl
from jax.experimental.pallas import tpu as pltpu
from jax.sharding import Mesh, PartitionSpec as P

G = 32
SIDE = 16
CELLS = SIDE * SIDE
C = 320
TAPS = 3 * C
F32 = jnp.float32
BF16 = jnp.bfloat16
VMEM_LIMIT = 30 * 1024 * 1024
ALL_VMEM = 60 * 1024 * 1024
LANES = 128
FLAT = 9 * C
TAIL = C - 2 * LANES
PACKED_USED = 2 * FLAT + FLAT // 2
PACKED = 64 * 120
STRIP = 240

NT = (((1,), (1,)), ((), ()))


def group_matrix():
    index = np.arange(C) // (C // G)
    return jnp.asarray((index[:, None] == index[None, :]).astype(np.float32), BF16)


def group_sums(columns, matrix):
    row = lax.broadcasted_iota(jnp.int32, (16, C), 0)
    stacked = jnp.zeros((16, C), F32)
    for at, column in enumerate(columns):
        high = column.astype(BF16).astype(F32)
        rest = column - high
        middle = rest.astype(BF16).astype(F32)
        low = (rest - middle).astype(BF16).astype(F32)
        for part, value in enumerate((high, middle, low)):
            stacked = jnp.where(row == 3 * at + part, value, stacked)
    sums = jnp.dot(stacked.astype(BF16), matrix, preferred_element_type=F32)
    return [
        sums[3 * at : 3 * at + 1] + sums[3 * at + 1 : 3 * at + 2] + sums[3 * at + 2 : 3 * at + 3]
        for at in range(len(columns))
    ]


def col_sum(values):
    return jnp.sum(values, axis=0, keepdims=True)


def column_index():
    return lax.broadcasted_iota(jnp.int32, (CELLS, C), 0) % SIDE


def shift_right(values, column):
    return jnp.where(column == 0, 0.0, pltpu.roll(values, 1, axis=0))


def shift_left(values, column):
    return jnp.where(column == SIDE - 1, 0.0, pltpu.roll(values, CELLS - 1, axis=0))


def clear_edges(padded):
    width = padded.shape[1]
    padded[0:SIDE, :] = jnp.zeros((SIDE, width), BF16)
    padded[SIDE + CELLS :, :] = jnp.zeros((SIDE, width), BF16)


def store_windows(padded, hidden, column):
    padded[SIDE : SIDE + CELLS, 0:C] = shift_right(hidden, column).astype(BF16)
    padded[SIDE : SIDE + CELLS, C : 2 * C] = hidden.astype(BF16)
    padded[SIDE : SIDE + CELLS, 2 * C : 3 * C] = shift_left(hidden, column).astype(BF16)


def norm_hidden(values, mask, temb, entries, matrix):
    mean = group_sums([col_sum(values * mask)], matrix)[0] / entries
    centered = values - mean
    variance = group_sums([col_sum(centered * centered * mask)], matrix)[0] / entries
    scale = lax.rsqrt(variance + 1e-05)
    normed = centered * scale
    shifted = normed + temb
    hidden = shifted / (1.0 + jnp.exp(-shifted)) * mask
    return normed, scale, hidden


def taps(kernel, row):
    return kernel[3 * row : 3 * row + 3].reshape(TAPS, C)


def conv(padded, kernel):
    total = None
    for row in range(3):
        part = jnp.dot(
            padded[row * SIDE : row * SIDE + CELLS, :], taps(kernel, row), preferred_element_type=F32
        )
        total = part if total is None else total + part
    return total


def conv_back(cot_padded, kernel, column):
    total = None
    for row in range(3):
        part = lax.dot_general(
            cot_padded[(2 - row) * SIDE : (2 - row) * SIDE + CELLS, :],
            taps(kernel, row),
            NT,
            preferred_element_type=F32,
        )
        total = part if total is None else total + part
    left, middle, right = total[:, 0:C], total[:, C : 2 * C], total[:, 2 * C : 3 * C]
    return shift_left(left, column) + middle + shift_right(right, column)


def norm_back(hidden_cot, normed, scale, temb, mask, entries, matrix):
    shifted = normed + temb
    gate = 1.0 / (1.0 + jnp.exp(-shifted))
    flow = hidden_cot * mask * (gate * (1.0 + shifted * (1.0 - gate)))
    plain, cross = group_sums([col_sum(flow), col_sum(flow * normed)], matrix)
    return scale * (flow - mask * (plain / entries + normed * (cross / entries)))


def mask_of(bucket_ref, core):
    row = lax.broadcasted_iota(jnp.int32, (CELLS, C), 0)
    inside = (row // SIDE < bucket_ref[core, 0]) & (row % SIDE < bucket_ref[core, 1])
    return inside.astype(F32)


def entries_of(bucket_ref, core):
    return (bucket_ref[core, 0] * bucket_ref[core, 1] * (C // G)).astype(F32)


class Setup:
    def __init__(self, core, bucket, embedding, time_ref, matrix):
        self.core = core
        self.column = column_index()
        self.mask = mask_of(bucket, core)
        self.entries = entries_of(bucket, core)
        self.matrix = matrix[...]
        self.embedding = embedding
        self.time_ref = time_ref

    def temb(self, k, side):
        rows = jnp.dot(self.embedding[...], self.time_ref[k, side], preferred_element_type=F32)
        at = lax.broadcasted_iota(jnp.int32, rows.shape, 0)
        return col_sum(jnp.where(at == self.core, rows, 0.0))


def fetch_pair(core, own, other, target, sems):
    copies = [
        pltpu.make_async_copy(own, target.at[core], sems.at[0]),
        pltpu.make_async_copy(other, target.at[1 - core], sems.at[1]),
    ]
    for copy in copies:
        copy.start()
    return copies


def wait_all(*groups):
    for copies in groups:
        for copy in copies:
            copy.wait()


def forward_block(setup, values, k, side, kernel, padded, out):
    normed_ref, scale_ref, hidden_ref = out
    normed, scale, hidden = norm_hidden(
        values, setup.mask, setup.temb(k, side), setup.entries, setup.matrix
    )
    normed_ref[k] = normed
    scale_ref[k] = jnp.broadcast_to(scale, (8, C))
    hidden_ref[k] = hidden.astype(BF16)
    if kernel is None:
        return None
    store_windows(padded, hidden, setup.column)
    return ((values + conv(padded, kernel)) * setup.mask).astype(BF16)


def encoder_pair(setup, value, w_enc, padded, out, inputs_ref):
    def block(k, value):
        inputs_ref[k] = value
        return forward_block(setup, value.astype(F32), k, 0, w_enc.at[k], padded, out)

    return lax.fori_loop(0, 2, block, value)


def decoder_pair(setup, value, w_dec, padded, out, inputs_ref, last):
    def block(step, value, conv_too=True):
        k = 1 - step
        summed = value.astype(F32) + inputs_ref[k].astype(F32)
        kernel = w_dec.at[k] if conv_too else None
        return forward_block(setup, summed, k, 1, kernel, padded, out)

    if last:
        return lax.fori_loop(0, 2, block, value)
    return block(1, block(0, value), conv_too=False)


def backward_pair(setup, value, side, upward, kernels, padded_cot, kept, cot_ref, skips, skip_in, last):
    normed_ref, scale_ref = kept

    def masked(k, value):
        residual = value.astype(F32) * setup.mask
        conv_cot = residual.astype(BF16)
        cot_ref[k] = conv_cot
        return residual, conv_cot

    def block(step, value):
        k = step if upward else 1 - step
        residual, conv_cot = masked(k, value)
        padded_cot[SIDE : SIDE + CELLS, :] = conv_cot
        hidden_cot = conv_back(padded_cot, kernels.at[k], setup.column)
        total = residual + norm_back(
            hidden_cot, normed_ref[k], scale_ref[k, 0:1], setup.temb(k, side), setup.mask,
            setup.entries, setup.matrix,
        )
        if skip_in is not None:
            total = total + skip_in[k].astype(F32)
        value = total.astype(BF16)
        if skips is not None:
            skips[k] = value
        return value

    if last:
        return lax.fori_loop(0, 2, block, value)
    masked(1 if upward else 0, block(0, value))
    return None


def phase_one(
    where, bucket, latents, time_own, time_other, enc_own, enc_other, emb, matrix,
    normed, scale, hidden, kept, sent, x, time_ref, w_enc, padded, sems,
):
    core = where[1]
    enc_copies = fetch_pair(core, enc_own, enc_other, w_enc, sems.at[0])
    time_copies = fetch_pair(core, time_own, time_other, time_ref, sems.at[1])
    x_copy = pltpu.make_async_copy(latents.at[core], x, sems.at[2, 0])
    x_copy.start()
    clear_edges(padded)
    wait_all([x_copy], time_copies, enc_copies)
    setup = Setup(core, bucket, emb, time_ref, matrix)
    sent[...] = encoder_pair(setup, x[...], w_enc, padded, (normed, scale, hidden), kept)


def phase_two(
    where, bucket, x, time_own, time_other, enc_own, enc_other, dec_own, dec_other, emb, matrix,
    e_normed, e_scale, e_hidden, d_normed, d_scale, d_hidden, sent,
    kept, time_ref, w_enc, w_dec, padded, sems,
):
    core = where[1]
    time_copies = fetch_pair(core, time_own, time_other, time_ref, sems.at[1])
    enc_copies = fetch_pair(core, enc_own, enc_other, w_enc, sems.at[0])
    dec_copies = fetch_pair(core, dec_own, dec_other, w_dec, sems.at[2])
    clear_edges(padded)
    wait_all(time_copies, enc_copies)
    setup = Setup(core, bucket, emb, time_ref, matrix)
    upper = encoder_pair(setup, x[...], w_enc, padded, (e_normed, e_scale, e_hidden), kept)
    wait_all(dec_copies)
    sent[...] = decoder_pair(
        setup, upper, w_dec, padded, (d_normed, d_scale, d_hidden), kept, True
    )


def phase_three(
    scaling, where, bucket, x, cotangent, time_own, time_other, dec_own, dec_other, kept, emb,
    matrix, d_hidden, cots, skips, sent,
    d_normed, d_scale, start, time_ref, w_dec, padded, padded_cot, sems,
):
    core = where[1]
    time_copies = fetch_pair(core, time_own, time_other, time_ref, sems.at[1])
    dec_copies = fetch_pair(core, dec_own, dec_other, w_dec, sems.at[0])
    start_copy = pltpu.make_async_copy(cotangent.at[core], start, sems.at[2, 0])
    start_copy.start()
    clear_edges(padded)
    clear_edges(padded_cot)
    wait_all(time_copies, dec_copies, [start_copy])
    setup = Setup(core, bucket, emb, time_ref, matrix)
    decoder_pair(setup, x[...], w_dec, padded, (d_normed, d_scale, d_hidden), kept, False)
    cot = (start[...].astype(F32) * scaling).astype(BF16)
    sent[...] = backward_pair(
        setup, cot, 1, True, w_dec, padded_cot, (d_normed, d_scale), cots, skips, None, True
    )


def phase_four(
    where, bucket, x, time_own, time_other, enc_own, enc_other, dec_own, dec_other, emb, matrix,
    d_normed, d_scale, e_normed, e_scale, d_cots, e_cots, sent,
    skips, time_ref, w_enc, w_dec, padded_cot, sems,
):
    core = where[1]
    time_copies = fetch_pair(core, time_own, time_other, time_ref, sems.at[1])
    dec_copies = fetch_pair(core, dec_own, dec_other, w_dec, sems.at[0])
    enc_copies = fetch_pair(core, enc_own, enc_other, w_enc, sems.at[2])
    clear_edges(padded_cot)
    wait_all(time_copies, dec_copies)
    setup = Setup(core, bucket, emb, time_ref, matrix)
    cot = backward_pair(
        setup, x[...], 1, True, w_dec, padded_cot, (d_normed, d_scale), d_cots, skips, None, True
    )
    wait_all(enc_copies)
    sent[...] = backward_pair(
        setup, cot, 0, False, w_enc, padded_cot, (e_normed, e_scale), e_cots, None, skips, True
    )


def store_packed(target, slot, row, values):
    first = row * TAPS
    target[slot, first : first + TAPS, :] = values[:, 0:LANES]
    target[slot, FLAT + first : FLAT + first + TAPS, :] = values[:, LANES : 2 * LANES]
    half = FLAT // 2
    pieces = ((0, TAPS // 2), (TAPS // 2, TAPS)) if row == 1 else ((0, TAPS),)
    for begin, end in pieces:
        side = 0 if first + end <= half else 1
        at = 2 * FLAT + first + begin - side * half
        target[slot, at : at + end - begin, side * TAIL : (side + 1) * TAIL] = values[
            begin:end, 2 * LANES : C
        ]


def store_gradients(core, hidden, cots, own, other, padded_cot, turned, pair):
    column = column_index()
    pair[:, PACKED_USED:, :] = jnp.zeros((2, PACKED - PACKED_USED, LANES), F32)

    def section(k, carry):
        values = hidden[k].astype(F32)
        padded_cot[SIDE : SIDE + CELLS, :] = cots[k]
        turned[0:C, :] = shift_right(values, column).T.astype(BF16)
        turned[C : 2 * C, :] = values.T.astype(BF16)
        turned[2 * C : 3 * C, :] = shift_left(values, column).T.astype(BF16)
        for row in range(3):
            part = jnp.dot(
                turned[...],
                padded_cot[(2 - row) * SIDE : (2 - row) * SIDE + CELLS, :],
                preferred_element_type=F32,
            )
            store_packed(pair, jnp.where(core == k, 0, 1), row, part)
        return carry

    lax.fori_loop(0, 2, section, 0)

    def copy(step, carry):
        begin = pl.multiple_of(step * STRIP, STRIP)
        own[pl.ds(begin, STRIP), :] = pair[0, pl.ds(begin, STRIP), :]
        other[pl.ds(begin, STRIP), :] = pair[1, pl.ds(begin, STRIP), :].astype(BF16)
        return carry

    lax.fori_loop(0, PACKED // STRIP, copy, 0)


def weight_phase(
    where, a_hidden, a_cots, b_hidden, b_cots, own, other, padded_cot, turned, pair, hidden, cots
):
    clear_edges(padded_cot)

    @pl.when(where[0] == 0)
    def _():
        hidden[...] = a_hidden[...]
        cots[...] = a_cots[...]

    @pl.when(where[0] != 0)
    def _():
        hidden[...] = b_hidden[...]
        cots[...] = b_cots[...]

    store_gradients(where[1], hidden, cots, own, other, padded_cot, turned, pair)


def phase_five(
    where, bucket, x, time_own, time_other, enc_own, enc_other, skips, emb, matrix,
    e_normed, e_scale, a_hidden, b_hidden, b_cots,
    own, other, padded_cot, turned, pair, hidden, cots, time_ref, w_enc, sems,
):
    clear_edges(padded_cot)
    core = where[1]
    time_copies = fetch_pair(core, time_own, time_other, time_ref, sems.at[1])
    enc_copies = fetch_pair(core, enc_own, enc_other, w_enc, sems.at[0])
    wait_all(time_copies, enc_copies)

    @pl.when(where[0] == 0)
    def _():
        hidden[...] = a_hidden[...]
        setup = Setup(core, bucket, emb, time_ref, matrix)
        backward_pair(
            setup, x[...], 0, False, w_enc, padded_cot, (e_normed, e_scale), cots, None, skips,
            False,
        )

    @pl.when(where[0] != 0)
    def _():
        hidden[...] = b_hidden[...]
        cots[...] = b_cots[...]

    store_gradients(core, hidden, cots, own, other, padded_cot, turned, pair)


def emit_chunks(total, me, kept, chunks):
    count = len(chunks) + 1
    rows = total.shape[0] // count
    for ahead in range(count):
        begin = pl.multiple_of(lax.rem(me + ahead, count) * rows, 8)
        part = total[pl.ds(begin, rows), :]
        if ahead == 0:
            kept[...] = part
        else:
            chunks[ahead - 1][...] = part.astype(BF16)


def place_chunks(target, me, chunks):
    count = len(chunks)
    rows = target.shape[0] // count
    for behind, chunk in enumerate(chunks):
        begin = pl.multiple_of(lax.rem(me + count - behind, count) * rows, 8)
        target[pl.ds(begin, rows), :] = chunk[...].astype(F32)


def core_add(own, other, out):
    def strip(step, carry):
        at = pl.ds(pl.multiple_of(step * 2 * STRIP, 2 * STRIP), 2 * STRIP)
        out[at, :] = (own[at, :] + other[at, :].astype(F32)).astype(BF16)
        return carry

    lax.fori_loop(0, PACKED // (2 * STRIP), strip, 0)


def sum_of(kept, received):
    value = kept[...]
    for part in received:
        value = value + part[...].astype(F32)
    return value


def block_sum(where, parts, kept, *rest):
    *chunks, total = rest
    value = parts[0].astype(F32)
    for at in range(1, parts.shape[0]):
        value = value + parts[at].astype(F32)
    total[...] = value
    emit_chunks(total, where[2], kept, chunks)


def last_sum(before, *rest):
    *received, out = rest
    out[...] = sum_of(before, received).astype(BF16)


def assemble(where, *rest):
    *chunks, out, total = rest
    place_chunks(total, where[2], chunks)
    value = total[...].astype(BF16)
    for at in range(out.shape[0]):
        out[at] = value


def unpack(packed, grad):
    half = FLAT // 2

    def strip(step, carry):
        begin = pl.multiple_of(step * 2 * STRIP, 2 * STRIP)
        for side in range(2):
            at = begin + side * half
            grad[pl.ds(at, 2 * STRIP), 0:LANES] = packed[pl.ds(at, 2 * STRIP), :].astype(F32)
            grad[pl.ds(at, 2 * STRIP), LANES : 2 * LANES] = packed[
                pl.ds(FLAT + at, 2 * STRIP), :
            ].astype(F32)
        tail = packed[pl.ds(2 * FLAT + begin, 2 * STRIP), :].astype(F32)
        grad[pl.ds(begin, 2 * STRIP), 2 * LANES : C] = tail[:, 0:TAIL]
        grad[pl.ds(begin + half, 2 * STRIP), 2 * LANES : C] = tail[:, TAIL : 2 * TAIL]
        return carry

    lax.fori_loop(0, half // (2 * STRIP), strip, 0)


def shape(dims, dtype):
    return jax.ShapeDtypeStruct(dims, dtype)


NORMED = ((2, CELLS, C), F32)
SCALE = ((2, 8, C), F32)
ACTS = ((2, CELLS, C), BF16)
ONE = ((CELLS, C), BF16)
PADDED = pltpu.VMEM((CELLS + 2 * SIDE, TAPS), BF16)
PADDED_COT = pltpu.VMEM((CELLS + 2 * SIDE, C), BF16)
TURNED = pltpu.VMEM((TAPS, CELLS), BF16)
OWN = ((PACKED, LANES), F32)
OTHER = ((PACKED, LANES), BF16)
WEIGHTS = pltpu.VMEM((2, 9, C, C), BF16)
TIMES = pltpu.VMEM((2, 2, C, C), BF16)
SEMS = pltpu.SemaphoreType.DMA((3, 2))


def call(body, spaces, outs, scratch, flops, name, vmem=VMEM_LIMIT):
    def run(*args):
        kinds = {"s": pltpu.SMEM, "h": pltpu.HBM, "v": pltpu.VMEM}
        moved = sum(a.size * a.dtype.itemsize for a in args) + sum(
            math.prod(d) * jnp.dtype(t).itemsize for d, t in outs
        )
        return pl.pallas_call(
            body,
            out_shape=tuple(shape(d, t) for d, t in outs),
            in_specs=[pl.BlockSpec(memory_space=kinds[space]) for space in spaces],
            out_specs=tuple(pl.BlockSpec(memory_space=pltpu.VMEM) for _ in outs),
            scratch_shapes=list(scratch),
            compiler_params=pltpu.CompilerParams(vmem_limit_bytes=vmem),
            cost_estimate=pl.CostEstimate(flops=flops, bytes_accessed=moved, transcendentals=0),
            name=name,
        )(*args)

    return run


CONV = 2 * CELLS * 9 * C * C


def time_embed(timesteps):
    half_width = C // 2
    frequencies = jnp.exp(
        -math.log(10000.0) * jnp.arange(half_width, dtype=F32) / half_width
    )
    angles = timesteps.astype(F32)[:, None] * frequencies[None, :]
    return jnp.concatenate([jnp.cos(angles), jnp.sin(angles)], axis=1).astype(BF16)


DP = ("z", "far", "y")


def to_other_core(array):
    return lax.ppermute(array, "core", [(0, 1), (1, 0)])


def ahead(value, axes, steps):
    count = lax.axis_size(axes)
    return lax.ppermute(value, axes, [(at, (at + steps) % count) for at in range(count)])


BLOCK = ("z_low", "far", "y")
LAYERS = "z_high"
DP = (LAYERS, *BLOCK)


def exchange(parts):
    return lax.all_to_all(parts, BLOCK, split_axis=0, concat_axis=0, tiled=True)


def core_sum(own, other):
    (pair,) = call(core_add, "vv", [((PACKED, LANES), BF16)], [], PACKED * LANES, "core_add", ALL_VMEM)(
        own, to_other_core(other)
    )
    return pair


def spread_parts(pair):
    count = lax.axis_size(BLOCK)
    return exchange(pair.reshape(count, PACKED // count, LANES))


def layer_sum(where, parts):
    count, rows, _ = parts.shape
    layers = lax.axis_size(LAYERS)
    part = (rows // layers, LANES)
    kept, *chunks = call(
        block_sum, "sv", [(part, F32)] + [(part, BF16)] * (layers - 1),
        [pltpu.VMEM((rows, LANES), F32)], PACKED * LANES, "block_sum",
    )(where, parts)
    received = [ahead(chunk, LAYERS, step + 1) for step, chunk in enumerate(chunks)]
    (mine,) = call(last_sum, "v" * layers, [(part, BF16)], [], rows * LANES, "last_sum")(
        kept, *received
    )
    received = [ahead(mine, LAYERS, step) for step in range(1, layers)]
    (copies,) = call(
        assemble, "s" + "v" * layers, [((count, rows, LANES), BF16)],
        [pltpu.VMEM((rows, LANES), F32)], PACKED * LANES, "assemble",
    )(where, mine, *received)
    return copies


def gradient(packed):
    (grad,) = call(unpack, "v", [((FLAT, C), F32)], [], PACKED * LANES, "unpack")(
        packed.reshape(PACKED, LANES)
    )
    return grad.reshape(1, 3, 3, C, C)


def local(latents, cotangent, bucket, timesteps, w_enc, w_dec, w_time):
    where = jnp.stack([lax.axis_index(axis) for axis in ("near", "core", LAYERS)])
    where = where.astype(jnp.int32)
    micro_count = latents.shape[0]
    loss_scale = float(micro_count * lax.axis_size(DP) * CELLS) ** (-0.5)

    enc = w_enc.reshape(9, C, C)
    dec = w_dec.reshape(9, C, C)
    times = w_time.reshape(2, C, C)
    enc = (enc, to_other_core(enc))
    times = (times, to_other_core(times))
    dec = (dec, to_other_core(dec))
    latents = latents.reshape(micro_count, CELLS, C)
    cotangent = cotangent.reshape(micro_count, CELLS, C)
    emb = jnp.pad(time_embed(timesteps), ((0, 16 - micro_count), (0, 0)))
    matrix = group_matrix()

    def up(value):
        return lax.ppermute(value, "near", [(0, 1)])

    def down(value):
        return lax.ppermute(value, "near", [(1, 0)])

    one = call(
        phase_one, "ss" + "h" * 5 + "vv", [NORMED, SCALE, ACTS, ACTS, ONE],
        [pltpu.VMEM(*ONE), TIMES, WEIGHTS, PADDED, SEMS], 2 * CONV, "one", ALL_VMEM,
    )
    a_normed, a_scale, a_hidden, a_kept, sent = one(
        where, bucket, latents, *times, *enc, emb, matrix
    )
    two = call(
        phase_two, "ssv" + "h" * 6 + "vv", [NORMED, SCALE, ACTS, NORMED, SCALE, ACTS, ONE],
        [pltpu.VMEM(*ACTS), TIMES, WEIGHTS, WEIGHTS, PADDED, SEMS], 4 * CONV, "two", ALL_VMEM,
    )
    be_normed, be_scale, be_hidden, bd_normed, bd_scale, bd_hidden, sent = two(
        where, bucket, up(sent), *times, *enc, *dec, emb, matrix
    )
    three = call(
        functools.partial(phase_three, loss_scale), "ssv" + "h" * 5 + "vvv",
        [ACTS, ACTS, ACTS, ONE],
        [
            pltpu.VMEM(*NORMED), pltpu.VMEM(*SCALE), pltpu.VMEM(*ONE), TIMES, WEIGHTS, PADDED,
            PADDED_COT, SEMS,
        ],
        3 * CONV, "three", ALL_VMEM,
    )
    ad_hidden, ad_cots, a_skips, sent = three(
        where, bucket, down(sent), cotangent, *times, *dec, a_kept, emb, matrix
    )
    four = call(
        phase_four, "ssv" + "h" * 6 + "v" * 6, [ACTS, ACTS, ONE],
        [pltpu.VMEM(*ACTS), TIMES, WEIGHTS, WEIGHTS, PADDED_COT, SEMS], 4 * CONV, "four", ALL_VMEM,
    )
    bd_cots, be_cots, sent = four(
        where, bucket, up(sent), *times, *enc, *dec, emb, matrix,
        bd_normed, bd_scale, be_normed, be_scale,
    )
    received = down(sent)
    work = [PADDED_COT, TURNED, pltpu.VMEM((2, PACKED, LANES), F32), pltpu.VMEM(*ACTS), pltpu.VMEM(*ACTS)]
    weights = call(weight_phase, "svvvv", [OWN, OTHER], work, 2 * CONV, "weights", ALL_VMEM)
    dec_pair = core_sum(*weights(where, ad_hidden, ad_cots, bd_hidden, bd_cots))
    received, dec_pair = lax.optimization_barrier((received, dec_pair))
    dec_parts = spread_parts(dec_pair)
    five = call(
        phase_five, "ssv" + "h" * 4 + "v" * 8, [OWN, OTHER], [*work, TIMES, WEIGHTS, SEMS],
        3 * CONV, "five", ALL_VMEM,
    )
    enc_grads = five(
        where, bucket, received, *times, *enc, a_skips, emb, matrix, a_normed, a_scale, a_hidden,
        be_hidden, be_cots,
    )

    enc_parts = spread_parts(core_sum(*enc_grads))
    dec_copies = exchange(layer_sum(where, dec_parts))
    enc_copies = exchange(layer_sum(where, enc_parts))
    return gradient(enc_copies), gradient(dec_copies)


def solution(mesh):
    segments, dp = mesh.shape["segment"], mesh.shape["dp"]
    near, far, rows = segments // 2, 2, 4
    split = Mesh(
        mesh.devices.reshape(near, 2, dp // (2 * far * rows), 2, far, rows),
        ("near", "core", *DP),
    )
    section, micro = ("near", "core"), DP
    placed = (
        P(micro, None, None, None),
        P(micro, None, None, None),
        P(micro, None),
        P(micro),
        P(section, None, None, None, None),
        P(section, None, None, None, None),
        P(section, None, None, None),
    )
    grads = P(section, None, None, None, None)
    return jax.shard_map(
        local, mesh=split, in_specs=placed, out_specs=(grads, grads), check_vma=False
    )
```

profile of v0, /device:TPU:2, one launch (start us, length us, event | category | flops | bytes accessed | tf_op | source)
XLA Modules:
  0.0 255.3 jit_solution(10121050445457978706)
XLA Ops:
  3.4 5.4 %collective-permute-done.time_other = bf16[2,320,320]{2,1,0:T(8,128)(2,1)S(1)} collective-permute-done((bf16[2,320,320]{2,1,0:T(8,128)(2,1)}, bf16[2,320,320]{2,1,0:T(8,128)(2,1)S(1)}, u32[]{:S(2)}, u32[]{:S(2)}) %collective-permute-start) | collective-permute-done | bytes 409632 | tf_op jit(solution)/shard_map/ppermute | solution.py:532
  10.3 7.7 %one.1 = (f32[2,256,320]{2,1,0:T(8,128)}, f32[2,8,320]{2,1,0:T(8,128)}, bf16[2,256,320]{2,1,0:T(8,128)(2,1)}, bf16[2,256,320]{2,1,0:T(8,128)(2,1)}, bf16[256,320]{1,0:T(8,128)(2,1)}) custom-call(s32[3]{0:T(128)} %pad_add_fusion.where, s32[2,2]{1,0:T(2,128)} %bucket.9, bf16[2,256,320]{2,1,0:T(8,128)(2,1)} %bitcast.34, bf16[2,320,320]{2,1,0:T(8,128)(2,1)} %bitcast.25, ...), custom_call_target="tpu_custom_call" | custom-call | flops 943718400 | bytes 6543388 | tf_op jit(solution)/shard_map/one/pallas_call | solution.py:502
  19.3 7.8 %collective-permute-done.2.x = bf16[256,320]{1,0:T(8,128)(2,1)S(1)} collective-permute-done((bf16[256,320]{1,0:T(8,128)(2,1)}, bf16[256,320]{1,0:T(8,128)(2,1)S(1)}, u32[]{:S(2)}, u32[]{:S(2)}) %collective-permute-start.2) | collective-permute-done | bytes 163872 | tf_op jit(solution)/shard_map/ppermute | solution.py:606
  27.8 11.1 %two.1 = (f32[2,256,320]{2,1,0:T(8,128)}, f32[2,8,320]{2,1,0:T(8,128)}, bf16[2,256,320]{2,1,0:T(8,128)(2,1)}, f32[2,256,320]{2,1,0:T(8,128)}, f32[2,8,320]{2,1,0...) custom-call(s32[3]{0:T(128)} %pad_add_fusion.where, s32[2,2]{1,0:T(2,128)} %bucket.9, ...), custom_call_target="tpu_custom_call" | custom-call | flops 1887436800 | bytes 10741788 | tf_op jit(solution)/shard_map/two/pallas_call | solution.py:502
  40.4 4.0 %collective-permute-done.4.x = bf16[256,320]{1,0:T(8,128)(2,1)S(1)} collective-permute-done((bf16[256,320]{1,0:T(8,128)(2,1)}, bf16[256,320]{1,0:T(8,128)(2,1)S(1)}, u32[]{:S(2)}, u32[]{:S(2)}) %collective-permute-start.4) | collective-permute-done | bytes 163872 | tf_op jit(solution)/shard_map/ppermute | solution.py:609
  45.1 10.1 %three.1 = (bf16[2,256,320]{2,1,0:T(8,128)(2,1)}, bf16[2,256,320]{2,1,0:T(8,128)(2,1)}, bf16[2,256,320]{2,1,0:T(8,128)(2,1)}, bf16[256,320]{1,0:T(8,128)(2,1)}) custom-call(s32[3]{0:T(128)} %pad_add_fusion.where, s32[2,2]{1,0:T(2,128)} %bucket.9, bf16[256,320]{1,0:T(8,128)(2,1)} %copy-done.7, bf16[2,256,320]{2,1,0:T(8,128)(2,1)} %bitcast.35, ...), custom_call_target="tpu_custom_call" | custom-call | flops 1415577600 | bytes 6686748 | tf_op jit(solution)/shard_map/three/pallas_call | solution.py:502
  56.6 6.3 %collective-permute-done.5.x = bf16[256,320]{1,0:T(8,128)(2,1)S(1)} collective-permute-done((bf16[256,320]{1,0:T(8,128)(2,1)}, bf16[256,320]{1,0:T(8,128)(2,1)S(1)}, u32[]{:S(2)}, u32[]{:S(2)}) %collective-permute-start.5) | collective-permute-done | bytes 163872 | tf_op jit(solution)/shard_map/ppermute | solution.py:606
  63.6 11.2 %four.1 = (bf16[2,256,320]{2,1,0:T(8,128)(2,1)}, bf16[2,256,320]{2,1,0:T(8,128)(2,1)}, bf16[256,320]{1,0:T(8,128)(2,1)}) custom-call(s32[3]{0:T(128)} %pad_add_fusion.where, s32[2,2]{1,0:T(2,128)} %bucket.9, bf16[256,320]{1,0:T(8,128)(2,1)} %copy-done.10, bf16[2,320,320]{2,1,0:T(8,128)(2,1)} %bitcast.28, bf16[2,320,320]{2,1,0:T(8,128)(2,1)} %copy-done.5, ...), custom_call_target="tpu_custom_call" | custom-call | flops 1887436800 | bytes 10741788 | tf_op jit(solution)/shard_map/four/pallas_call | solution.py:502
  74.8 6.8 %weights.1 = (f32[7680,128]{1,0:T(8,128)}, bf16[7680,128]{1,0:T(8,128)(2,1)}) custom-call(s32[3]{0:T(128)} %pad_add_fusion.where, bf16[2,256,320]{2,1,0:T(8,128)(2,1)} %get-tuple-element.44.a_hidden, bf16[2,256,320]{2,1,0:T(8,128)(2,1)} %get-tuple-element.45.a_cots, bf16[2,256,320]{2,1,0:T(8,128)(2,1)} %get-tuple-element.46.b_hidden, ...), custom_call_target="tpu_custom_call" | custom-call | flops 943718400 | bytes 7208972 | tf_op jit(solution)/shard_map/weights/pallas_call | solution.py:502
  83.3 2.6 %collective-permute-done.7.other = bf16[7680,128]{1,0:T(8,128)(2,1)S(1)} collective-permute-done((bf16[7680,128]{1,0:T(8,128)(2,1)}, bf16[7680,128]{1,0:T(8,128)(2,1)S(1)}, u32[]{:S(2)}, u32[]{:S(2)}) %collective-permute-start.7) | collective-permute-done | bytes 1966112 | tf_op jit(solution)/shard_map/ppermute | solution.py:532
  87.2 4.5 %core_add.2 = bf16[7680,128]{1,0:T(8,128)(2,1)} custom-call(f32[7680,128]{1,0:T(8,128)} %get-tuple-element.48.own, bf16[7680,128]{1,0:T(8,128)(2,1)} %copy-done.6), custom_call_target="tpu_custom_call" | custom-call | flops 983040 | bytes 7864320 | tf_op jit(solution)/shard_map/core_add/pallas_call | solution.py:502
  92.3 7.5 %all-to-all-start.2 = ((bf16[16,480,128]{2,1,0:T(8,128)(2,1)}), bf16[16,480,128]{2,1,0:T(8,128)(2,1)S(1)}, u32[]{:S(2)}, u32[]{:S(2)}) async-start(bf16[16,480,128]{2,1,0:T(8,128)(2,1)} %bitcast.31), calls=%async_computation.2 | async-start | bytes 3932160 | tf_op jit(solution)/shard_map/all_to_all | solution.py:546
  99.8 9.9 %five.1 = (f32[7680,128]{1,0:T(8,128)}, bf16[7680,128]{1,0:T(8,128)(2,1)}) custom-call(s32[3]{0:T(128)} %pad_add_fusion.where, s32[2,2]{1,0:T(2,128)} %bucket.9, bf16[256,320]{1,0:T(8,128)(2,1)} %copy-done.8, bf16[2,320,320]{2,1,0:T(8,128)(2,1)} %bitcast.29, bf16[2,320,320]{2,1,0:T(8,128)(2,1)} %copy-done.5, bf16[9,320,320]{2,1,0:T(8,128)(2,1)} %bitcast.19, ...), custom_call_target="tpu_custom_call" | custom-call | flops 1415577600 | bytes 12769308 | tf_op jit(solution)/shard_map/five/pallas_call | solution.py:502
  109.9 4.3 %collective-permute-done.8.other = bf16[7680,128]{1,0:T(8,128)(2,1)} collective-permute-done((bf16[7680,128]{1,0:T(8,128)(2,1)}, bf16[7680,128]{1,0:T(8,128)(2,1)}, u32[]{:S(2)}, u32[]{:S(2)}) %collective-permute-start.8) | collective-permute-done | bytes 1966112 | tf_op jit(solution)/shard_map/ppermute | solution.py:532
  114.2 4.4 %core_add.3 = bf16[7680,128]{1,0:T(8,128)(2,1)} custom-call(f32[7680,128]{1,0:T(8,128)} %get-tuple-element.57.own, bf16[7680,128]{1,0:T(8,128)(2,1)} %collective-permute-done.8.other), custom_call_target="tpu_custom_call" | custom-call | flops 983040 | bytes 7864320 | tf_op jit(solution)/shard_map/core_add/pallas_call | solution.py:502
  118.6 9.8 %all-to-all-done.2.parts = bf16[16,480,128]{2,1,0:T(8,128)(2,1)S(1)} async-done(((bf16[16,480,128]{2,1,0:T(8,128)(2,1)}), bf16[16,480,128]{2,1,0:T(8,128)(2,1)S(1)}, u32[]{:S(2)}, u32[]{:S(2)}) %all-to-all-start.2) | async-done | bytes 1966112 | tf_op jit(solution)/shard_map/all_to_all | solution.py:546
  129.7 4.9 %all-to-all-start = ((bf16[16,480,128]{2,1,0:T(8,128)(2,1)}), bf16[16,480,128]{2,1,0:T(8,128)(2,1)S(1)}, u32[]{:S(2)}, u32[]{:S(2)}) async-start(bf16[16,480,128]{2,1,0:T(8,128)(2,1)} %bitcast.30), calls=%async_computation | async-start | bytes 3932160 | tf_op jit(solution)/shard_map/all_to_all | solution.py:546
  137.1 3.4 %collective-permute-start.15 = (bf16[120,128]{1,0:T(8,128)(2,1)S(1)}, bf16[120,128]{1,0:T(8,128)(2,1)S(1)}, u32[]{:S(2)}, u32[]{:S(2)}) collective-permute-start(bf16[120,128]{1,0:T(8,128)(2,1)S(1)} %get-tuple-element.65), channel_id=1, source_target_pairs={{0,16},{16,32},{32,48},{48,0},{1,17},{17,33},{33,49},{49,1},{2,18}... | collective-permute-start | bytes 92168 | tf_op jit(solution)/shard_map/ppermute | solution.py:537
  140.4 4.5 %collective-permute-start.16 = (bf16[120,128]{1,0:T(8,128)(2,1)S(1)}, bf16[120,128]{1,0:T(8,128)(2,1)S(1)}, u32[]{:S(2)}, u32[]{:S(2)}) collective-permute-start(bf16[120,128]{1,0:T(8,128)(2,1)S(1)} %get-tuple-element.66), channel_id=1, source_target_pairs={{0,32},{16,48},{32,0},{48,16},{1,33},{17,49},{33,1},{49,17},{2,34}... | collective-permute-start | bytes 92168 | tf_op jit(solution)/shard_map/ppermute | solution.py:537
  144.9 2.7 %collective-permute-start.17 = (bf16[120,128]{1,0:T(8,128)(2,1)S(1)}, bf16[120,128]{1,0:T(8,128)(2,1)S(1)}, u32[]{:S(2)}, u32[]{:S(2)}) collective-permute-start(bf16[120,128]{1,0:T(8,128)(2,1)S(1)} %get-tuple-element.67), channel_id=1, source_target_pairs={{0,48},{16,0},{32,16},{48,32},{1,49},{17,1},{33,17},{49,33},{2,50}... | collective-permute-start | bytes 92168 | tf_op jit(solution)/shard_map/ppermute | solution.py:537
  147.6 14.9 %collective-permute-done.15.rest_0_ = bf16[120,128]{1,0:T(8,128)(2,1)S(1)} collective-permute-done((bf16[120,128]{1,0:T(8,128)(2,1)S(1)}, bf16[120,128]{1,0:T(8,128)(2,1)S(1)}, u32[]{:S(2)}, u32[]{:S(2)}) %collective-permute-start.15) | collective-permute-done | bytes 30752 | tf_op jit(solution)/shard_map/ppermute | solution.py:537
  164.7 4.2 %collective-permute-start.19 = (bf16[120,128]{1,0:T(8,128)(2,1)S(1)}, bf16[120,128]{1,0:T(8,128)(2,1)S(1)}, u32[]{:S(2)}, u32[]{:S(2)}) collective-permute-start(bf16[120,128]{1,0:T(8,128)(2,1)S(1)} %last_sum.3.rest_0_), channel_id=1, source_target_pairs={{0,32},{16,48},{32,0},{48,16},{1,33},{17,49},{33,1},{49,17},{2,34}... | collective-permute-start | bytes 92168 | tf_op jit(solution)/shard_map/ppermute | solution.py:537
  168.9 3.8 %collective-permute-done.19.rest_2_ = bf16[120,128]{1,0:T(8,128)(2,1)S(1)} collective-permute-done((bf16[120,128]{1,0:T(8,128)(2,1)S(1)}, bf16[120,128]{1,0:T(8,128)(2,1)S(1)}, u32[]{:S(2)}, u32[]{:S(2)}) %collective-permute-start.19) | collective-permute-done | bytes 30752 | tf_op jit(solution)/shard_map/ppermute | solution.py:537
  177.2 8.0 %all-to-all-start.3 = ((bf16[16,480,128]{2,1,0:T(8,128)(2,1)}), bf16[16,480,128]{2,1,0:T(8,128)(2,1)}, u32[]{:S(2)}, u32[]{:S(2)}) async-start(bf16[16,480,128]{2,1,0:T(8,128)(2,1)} %copy-done), calls=%async_computation.3 | async-start | bytes 3932160 | tf_op jit(solution)/shard_map/all_to_all | solution.py:546
  188.2 3.7 %collective-permute-start.11 = (bf16[120,128]{1,0:T(8,128)(2,1)S(1)}, bf16[120,128]{1,0:T(8,128)(2,1)S(1)}, u32[]{:S(2)}, u32[]{:S(2)}) collective-permute-start(bf16[120,128]{1,0:T(8,128)(2,1)S(1)} %get-tuple-element.62), channel_id=1, source_target_pairs={{0,48},{16,0},{32,16},{48,32},{1,49},{17,1},{33,17},{49,33},{2,50}... | collective-permute-start | bytes 92168 | tf_op jit(solution)/shard_map/ppermute | solution.py:537
  191.9 12.2 %collective-permute-done.9.rest_0_ = bf16[120,128]{1,0:T(8,128)(2,1)S(1)} collective-permute-done((bf16[120,128]{1,0:T(8,128)(2,1)S(1)}, bf16[120,128]{1,0:T(8,128)(2,1)S(1)}, u32[]{:S(2)}, u32[]{:S(2)}) %collective-permute-start.9) | collective-permute-done | bytes 30752 | tf_op jit(solution)/shard_map/ppermute | solution.py:537
  204.0 3.4 %collective-permute-done.10.rest_1_ = bf16[120,128]{1,0:T(8,128)(2,1)S(1)} collective-permute-done((bf16[120,128]{1,0:T(8,128)(2,1)S(1)}, bf16[120,128]{1,0:T(8,128)(2,1)S(1)}, u32[]{:S(2)}, u32[]{:S(2)}) %collective-permute-start.10) | collective-permute-done | bytes 30752 | tf_op jit(solution)/shard_map/ppermute | solution.py:537
  207.8 3.2 %collective-permute-start.13 = (bf16[120,128]{1,0:T(8,128)(2,1)S(1)}, bf16[120,128]{1,0:T(8,128)(2,1)S(1)}, u32[]{:S(2)}, u32[]{:S(2)}) collective-permute-start(bf16[120,128]{1,0:T(8,128)(2,1)S(1)} %last_sum.2.rest_0_), channel_id=1, source_target_pairs={{0,32},{16,48},{32,0},{48,16},{1,33},{17,49},{33,1},{49,17},{2,34}... | collective-permute-start | bytes 92168 | tf_op jit(solution)/shard_map/ppermute | solution.py:537
  211.0 2.7 %collective-permute-start.12 = (bf16[120,128]{1,0:T(8,128)(2,1)S(1)}, bf16[120,128]{1,0:T(8,128)(2,1)S(1)}, u32[]{:S(2)}, u32[]{:S(2)}) collective-permute-start(bf16[120,128]{1,0:T(8,128)(2,1)S(1)} %last_sum.2.rest_0_), channel_id=1, source_target_pairs={{0,16},{16,32},{32,48},{48,0},{1,17},{17,33},{33,49},{49,1},{2,18}... | collective-permute-start | bytes 92168 | tf_op jit(solution)/shard_map/ppermute | solution.py:537
  219.0 11.0 %all-to-all-start.1 = ((bf16[16,480,128]{2,1,0:T(8,128)(2,1)}), bf16[16,480,128]{2,1,0:T(8,128)(2,1)S(1)}, u32[]{:S(2)}, u32[]{:S(2)}) async-start(bf16[16,480,128]{2,1,0:T(8,128)(2,1)} %assemble.2), calls=%async_computation.1 | async-start | bytes 3932160 | tf_op jit(solution)/shard_map/all_to_all | solution.py:546
  230.0 4.1 %unpack.3 = f32[2880,320]{1,0:T(8,128)} custom-call(bf16[7680,128]{1,0:T(8,128)(2,1)} %bitcast.12.packed), custom_call_target="tpu_custom_call" | custom-call | flops 983040 | bytes 5652480 | tf_op jit(solution)/shard_map/unpack/pallas_call | solution.py:502
  234.1 18.6 %all-to-all-done.1 = bf16[16,480,128]{2,1,0:T(8,128)(2,1)S(1)} async-done(((bf16[16,480,128]{2,1,0:T(8,128)(2,1)}), bf16[16,480,128]{2,1,0:T(8,128)(2,1)S(1)}, u32[]{:S(2)}, u32[]{:S(2)}) %all-to-all-start.1) | async-done | bytes 1966112 | tf_op jit(solution)/shard_map/all_to_all | solution.py:546
  (63 shorter events, 35.9 us)
Async XLA Ops:
  0.6 8.2 %collective-permute-start.1 = (bf16[9,320,320]{2,1,0:T(8,128)(2,1)}, bf16[9,320,320]{2,1,0:T(8,128)(2,1)S(1)}, u32[]{:S(2)}, u32[]{:S(2)}) collective-permute-start(bf16[9,320,320]{2,1,0:T(8,128)(2,1)} %bitcast.15), channel_id=1, source_target_pairs={{0,64},{64,0},{1,65},{65,1},{2,66},{66,2},{3,67},{67,3},{4,68},{68... | collective-permute-start | bytes 5529608 | tf_op jit(solution)/shard_map/ppermute | solution.py:532
  0.7 18.6 %collective-permute-start.3 = (bf16[9,320,320]{2,1,0:T(8,128)(2,1)}, bf16[9,320,320]{2,1,0:T(8,128)(2,1)}, u32[]{:S(2)}, u32[]{:S(2)}) collective-permute-start(bf16[9,320,320]{2,1,0:T(8,128)(2,1)} %bitcast.20), channel_id=1, source_target_pairs={{0,64},{64,0},{1,65},{65,1},{2,66},{66,2},{3,67},{67,3},{4,68},{68... | collective-permute-start | bytes 5529608 | tf_op jit(solution)/shard_map/ppermute | solution.py:532
  1.2 7.6 %collective-permute-start = (bf16[2,320,320]{2,1,0:T(8,128)(2,1)}, bf16[2,320,320]{2,1,0:T(8,128)(2,1)S(1)}, u32[]{:S(2)}, u32[]{:S(2)}) collective-permute-start(bf16[2,320,320]{2,1,0:T(8,128)(2,1)} %bitcast.24), channel_id=1, source_target_pairs={{0,64},{64,0},{1,65},{65,1},{2,66},{66,2},{3,67},{67,3},{4,68},{68... | collective-permute-start | bytes 1228808 | tf_op jit(solution)/shard_map/ppermute | solution.py:532
  8.8 1.5 copy-start.4
  18.0 9.1 %collective-permute-start.2 = (bf16[256,320]{1,0:T(8,128)(2,1)}, bf16[256,320]{1,0:T(8,128)(2,1)S(1)}, u32[]{:S(2)}, u32[]{:S(2)}) collective-permute-start(bf16[256,320]{1,0:T(8,128)(2,1)} %get-tuple-element.35), channel_id=1, source_target_pairs={{0,128},{1,129},{2,130},{3,131},{4,132},{5,133},{6,134},{7,135},{8... | collective-permute-start | bytes 491528 | tf_op jit(solution)/shard_map/ppermute | solution.py:606
  38.8 5.5 %collective-permute-start.4 = (bf16[256,320]{1,0:T(8,128)(2,1)}, bf16[256,320]{1,0:T(8,128)(2,1)S(1)}, u32[]{:S(2)}, u32[]{:S(2)}) collective-permute-start(bf16[256,320]{1,0:T(8,128)(2,1)} %get-tuple-element.36), channel_id=1, source_target_pairs={{128,0},{129,1},{130,2},{131,3},{132,4},{133,5},{134,6},{135,7},{1... | collective-permute-start | bytes 491528 | tf_op jit(solution)/shard_map/ppermute | solution.py:609
  55.2 7.8 %collective-permute-start.5 = (bf16[256,320]{1,0:T(8,128)(2,1)}, bf16[256,320]{1,0:T(8,128)(2,1)S(1)}, u32[]{:S(2)}, u32[]{:S(2)}) collective-permute-start(bf16[256,320]{1,0:T(8,128)(2,1)} %get-tuple-element.38), channel_id=1, source_target_pairs={{0,128},{1,129},{2,130},{3,131},{4,132},{5,133},{6,134},{7,135},{8... | collective-permute-start | bytes 491528 | tf_op jit(solution)/shard_map/ppermute | solution.py:606
  74.8 6.9 %copy-start.11 = (bf16[256,320]{1,0:T(8,128)(2,1)S(1)}, bf16[256,320]{1,0:T(8,128)(2,1)}, u32[]{:S(2)}) copy-start(bf16[256,320]{1,0:T(8,128)(2,1)} %get-tuple-element.43) | copy-start | bytes 491524
  81.7 4.2 %collective-permute-start.7 = (bf16[7680,128]{1,0:T(8,128)(2,1)}, bf16[7680,128]{1,0:T(8,128)(2,1)S(1)}, u32[]{:S(2)}, u32[]{:S(2)}) collective-permute-start(bf16[7680,128]{1,0:T(8,128)(2,1)} %get-tuple-element.49), channel_id=1, source_target_pairs={{0,64},{64,0},{1,65},{65,1},{2,66},{66,2},{3,67},{67,3},{4,68},{68... | collective-permute-start | bytes 5898248 | tf_op jit(solution)/shard_map/ppermute | solution.py:532
  81.7 9.9 %collective-permute-start.6 = (bf16[256,320]{1,0:T(8,128)(2,1)S(1)}, bf16[256,320]{1,0:T(8,128)(2,1)S(1)}, u32[]{:S(2)}, u32[]{:S(2)}) collective-permute-start(bf16[256,320]{1,0:T(8,128)(2,1)S(1)} %copy-done.11), channel_id=1, source_target_pairs={{128,0},{129,1},{130,2},{131,3},{132,4},{133,5},{134,6},{135,7},{1... | collective-permute-start | bytes 491528 | tf_op jit(solution)/shard_map/ppermute | solution.py:609
  85.9 1.3 copy-start.6
  92.3 36.1 %all-to-all-start.2 = ((bf16[16,480,128]{2,1,0:T(8,128)(2,1)}), bf16[16,480,128]{2,1,0:T(8,128)(2,1)S(1)}, u32[]{:S(2)}, u32[]{:S(2)}) async-start(bf16[16,480,128]{2,1,0:T(8,128)(2,1)} %bitcast.31), calls=%async_computation.2 | async-start | bytes 3932160 | tf_op jit(solution)/shard_map/all_to_all | solution.py:546
  109.8 4.4 %collective-permute-start.8 = (bf16[7680,128]{1,0:T(8,128)(2,1)}, bf16[7680,128]{1,0:T(8,128)(2,1)}, u32[]{:S(2)}, u32[]{:S(2)}) collective-permute-start(bf16[7680,128]{1,0:T(8,128)(2,1)} %get-tuple-element.58), channel_id=1, source_target_pairs={{0,64},{64,0},{1,65},{65,1},{2,66},{66,2},{3,67},{67,3},{4,68},{68... | collective-permute-start | bytes 5898248 | tf_op jit(solution)/shard_map/ppermute | solution.py:532
  128.4 1.3 copy-start.1
  129.7 4.9 %copy-start.3 = (s32[3]{0:T(128)S(1)}, s32[3]{0:T(128)}, u32[]{:S(2)}) copy-start(s32[3]{0:T(128)} %pad_add_fusion.where) | copy-start | bytes 40
  129.7 47.5 %all-to-all-start = ((bf16[16,480,128]{2,1,0:T(8,128)(2,1)}), bf16[16,480,128]{2,1,0:T(8,128)(2,1)S(1)}, u32[]{:S(2)}, u32[]{:S(2)}) async-start(bf16[16,480,128]{2,1,0:T(8,128)(2,1)} %bitcast.30), calls=%async_computation | async-start | bytes 3932160 | tf_op jit(solution)/shard_map/all_to_all | solution.py:546
  134.6 1.5 copy-start.2
  137.1 25.5 %collective-permute-start.15 = (bf16[120,128]{1,0:T(8,128)(2,1)S(1)}, bf16[120,128]{1,0:T(8,128)(2,1)S(1)}, u32[]{:S(2)}, u32[]{:S(2)}) collective-permute-start(bf16[120,128]{1,0:T(8,128)(2,1)S(1)} %get-tuple-element.65), channel_id=1, source_target_pairs={{0,16},{16,32},{32,48},{48,0},{1,17},{17,33},{33,49},{49,1},{2,18}... | collective-permute-start | bytes 92168 | tf_op jit(solution)/shard_map/ppermute | solution.py:537
  140.4 23.3 %collective-permute-start.16 = (bf16[120,128]{1,0:T(8,128)(2,1)S(1)}, bf16[120,128]{1,0:T(8,128)(2,1)S(1)}, u32[]{:S(2)}, u32[]{:S(2)}) collective-permute-start(bf16[120,128]{1,0:T(8,128)(2,1)S(1)} %get-tuple-element.66), channel_id=1, source_target_pairs={{0,32},{16,48},{32,0},{48,16},{1,33},{17,49},{33,1},{49,17},{2,34}... | collective-permute-start | bytes 92168 | tf_op jit(solution)/shard_map/ppermute | solution.py:537
  144.9 18.8 %collective-permute-start.17 = (bf16[120,128]{1,0:T(8,128)(2,1)S(1)}, bf16[120,128]{1,0:T(8,128)(2,1)S(1)}, u32[]{:S(2)}, u32[]{:S(2)}) collective-permute-start(bf16[120,128]{1,0:T(8,128)(2,1)S(1)} %get-tuple-element.67), channel_id=1, source_target_pairs={{0,48},{16,0},{32,16},{48,32},{1,49},{17,1},{33,17},{49,33},{2,50}... | collective-permute-start | bytes 92168 | tf_op jit(solution)/shard_map/ppermute | solution.py:537
  163.8 5.1 %collective-permute-start.20 = (bf16[120,128]{1,0:T(8,128)(2,1)S(1)}, bf16[120,128]{1,0:T(8,128)(2,1)S(1)}, u32[]{:S(2)}, u32[]{:S(2)}) collective-permute-start(bf16[120,128]{1,0:T(8,128)(2,1)S(1)} %last_sum.3.rest_0_), channel_id=1, source_target_pairs={{0,48},{16,0},{32,16},{48,32},{1,49},{17,1},{33,17},{49,33},{2,50}... | collective-permute-start | bytes 92168 | tf_op jit(solution)/shard_map/ppermute | solution.py:537
  164.7 7.9 %collective-permute-start.19 = (bf16[120,128]{1,0:T(8,128)(2,1)S(1)}, bf16[120,128]{1,0:T(8,128)(2,1)S(1)}, u32[]{:S(2)}, u32[]{:S(2)}) collective-permute-start(bf16[120,128]{1,0:T(8,128)(2,1)S(1)} %last_sum.3.rest_0_), channel_id=1, source_target_pairs={{0,32},{16,48},{32,0},{48,16},{1,33},{17,49},{33,1},{49,17},{2,34}... | collective-permute-start | bytes 92168 | tf_op jit(solution)/shard_map/ppermute | solution.py:537
  168.9 6.3 %collective-permute-start.18 = (bf16[120,128]{1,0:T(8,128)(2,1)S(1)}, bf16[120,128]{1,0:T(8,128)(2,1)S(1)}, u32[]{:S(2)}, u32[]{:S(2)}) collective-permute-start(bf16[120,128]{1,0:T(8,128)(2,1)S(1)} %last_sum.3.rest_0_), channel_id=1, source_target_pairs={{0,16},{16,32},{32,48},{48,0},{1,17},{17,33},{33,49},{49,1},{2,18}... | collective-permute-start | bytes 92168 | tf_op jit(solution)/shard_map/ppermute | solution.py:537
  175.9 1.3 copy-start
  177.2 41.8 %all-to-all-start.3 = ((bf16[16,480,128]{2,1,0:T(8,128)(2,1)}), bf16[16,480,128]{2,1,0:T(8,128)(2,1)}, u32[]{:S(2)}, u32[]{:S(2)}) async-start(bf16[16,480,128]{2,1,0:T(8,128)(2,1)} %copy-done), calls=%async_computation.3 | async-start | bytes 3932160 | tf_op jit(solution)/shard_map/all_to_all | solution.py:546
  186.1 17.9 %collective-permute-start.9 = (bf16[120,128]{1,0:T(8,128)(2,1)S(1)}, bf16[120,128]{1,0:T(8,128)(2,1)S(1)}, u32[]{:S(2)}, u32[]{:S(2)}) collective-permute-start(bf16[120,128]{1,0:T(8,128)(2,1)S(1)} %get-tuple-element.60), channel_id=1, source_target_pairs={{0,16},{16,32},{32,48},{48,0},{1,17},{17,33},{33,49},{49,1},{2,18}... | collective-permute-start | bytes 92168 | tf_op jit(solution)/shard_map/ppermute | solution.py:537
  186.2 21.2 %collective-permute-start.10 = (bf16[120,128]{1,0:T(8,128)(2,1)S(1)}, bf16[120,128]{1,0:T(8,128)(2,1)S(1)}, u32[]{:S(2)}, u32[]{:S(2)}) collective-permute-start(bf16[120,128]{1,0:T(8,128)(2,1)S(1)} %get-tuple-element.61), channel_id=1, source_target_pairs={{0,32},{16,48},{32,0},{48,16},{1,33},{17,49},{33,1},{49,17},{2,34}... | collective-permute-start | bytes 92168 | tf_op jit(solution)/shard_map/ppermute | solution.py:537
  188.2 19.2 %collective-permute-start.11 = (bf16[120,128]{1,0:T(8,128)(2,1)S(1)}, bf16[120,128]{1,0:T(8,128)(2,1)S(1)}, u32[]{:S(2)}, u32[]{:S(2)}) collective-permute-start(bf16[120,128]{1,0:T(8,128)(2,1)S(1)} %get-tuple-element.62), channel_id=1, source_target_pairs={{0,48},{16,0},{32,16},{48,32},{1,49},{17,1},{33,17},{49,33},{2,50}... | collective-permute-start | bytes 92168 | tf_op jit(solution)/shard_map/ppermute | solution.py:537
  207.5 6.2 %collective-permute-start.14 = (bf16[120,128]{1,0:T(8,128)(2,1)S(1)}, bf16[120,128]{1,0:T(8,128)(2,1)S(1)}, u32[]{:S(2)}, u32[]{:S(2)}) collective-permute-start(bf16[120,128]{1,0:T(8,128)(2,1)S(1)} %last_sum.2.rest_0_), channel_id=1, source_target_pairs={{0,48},{16,0},{32,16},{48,32},{1,49},{17,1},{33,17},{49,33},{2,50}... | collective-permute-start | bytes 92168 | tf_op jit(solution)/shard_map/ppermute | solution.py:537
  207.8 7.8 %collective-permute-start.13 = (bf16[120,128]{1,0:T(8,128)(2,1)S(1)}, bf16[120,128]{1,0:T(8,128)(2,1)S(1)}, u32[]{:S(2)}, u32[]{:S(2)}) collective-permute-start(bf16[120,128]{1,0:T(8,128)(2,1)S(1)} %last_sum.2.rest_0_), channel_id=1, source_target_pairs={{0,32},{16,48},{32,0},{48,16},{1,33},{17,49},{33,1},{49,17},{2,34}... | collective-permute-start | bytes 92168 | tf_op jit(solution)/shard_map/ppermute | solution.py:537
  211.0 6.0 %collective-permute-start.12 = (bf16[120,128]{1,0:T(8,128)(2,1)S(1)}, bf16[120,128]{1,0:T(8,128)(2,1)S(1)}, u32[]{:S(2)}, u32[]{:S(2)}) collective-permute-start(bf16[120,128]{1,0:T(8,128)(2,1)S(1)} %last_sum.2.rest_0_), channel_id=1, source_target_pairs={{0,16},{16,32},{32,48},{48,0},{1,17},{17,33},{33,49},{49,1},{2,18}... | collective-permute-start | bytes 92168 | tf_op jit(solution)/shard_map/ppermute | solution.py:537
  219.0 33.7 %all-to-all-start.1 = ((bf16[16,480,128]{2,1,0:T(8,128)(2,1)}), bf16[16,480,128]{2,1,0:T(8,128)(2,1)S(1)}, u32[]{:S(2)}, u32[]{:S(2)}) async-start(bf16[16,480,128]{2,1,0:T(8,128)(2,1)} %assemble.2), calls=%async_computation.1 | async-start | bytes 3932160 | tf_op jit(solution)/shard_map/all_to_all | solution.py:546
  (5 other events, 3.5 us)
where the time goes:
time: 256 us; the launch traced here: 255 us
  waiting for transfers between devices  100 us (39%)
  Pallas kernels  76.9 us (30%)
  starting transfers between devices  65.7 us (26%)
  local copies, waits for them, and re-layouts  9.64 us (4%)
    pallas_call x16, Pallas kernels, run(): pl.pallas_call(body, out_shape=tuple((shape(d, t) for d, t in outs)), in_...  76.9 us
    ppermute x12, waiting for transfers between devices, ahead(): lax.ppermute(value, axes, [(at, (at + steps) % count) for at in range(cou...  41.4 us
    all_to_all x4, starting transfers between devices, exchange(): return lax.all_to_all(parts, BLOCK, split_axis=0, concat_axis=0, tiled=True)  31.4 us
    all_to_all x4, waiting for transfers between devices, exchange(): return lax.all_to_all(parts, BLOCK, split_axis=0, concat_axis=0, tiled=True)  28.4 us
    ppermute x12, starting transfers between devices, ahead(): lax.ppermute(value, axes, [(at, (at + steps) % count) for at in range(cou...  27.6 us
    ppermute x2, waiting for transfers between devices, up(): return lax.ppermute(value, 'near', [(0, 1)])  14.1 us
    ppermute x5, waiting for transfers between devices, to_other_core(): return lax.ppermute(array, 'core', [(0, 1), (1, 0)])  12.3 us
    unnamed x24, local copies, waits for them, and re-layouts  9.64 us
  transfers between devices with their start and end apart: 25, of which 16 were waited for; matrix products, arithmetic and copies ran while one was open for 1% of the time, Pallas kernels for 14%

commit v1 on v0

--- a/solution.py
+++ b/solution.py
@@ -398,26 +398,6 @@
     store_gradients(core, hidden, cots, own, other, padded_cot, turned, pair)
 
 
-def emit_chunks(total, me, kept, chunks):
-    count = len(chunks) + 1
-    rows = total.shape[0] // count
-    for ahead in range(count):
-        begin = pl.multiple_of(lax.rem(me + ahead, count) * rows, 8)
-        part = total[pl.ds(begin, rows), :]
-        if ahead == 0:
-            kept[...] = part
-        else:
-            chunks[ahead - 1][...] = part.astype(BF16)
-
-
-def place_chunks(target, me, chunks):
-    count = len(chunks)
-    rows = target.shape[0] // count
-    for behind, chunk in enumerate(chunks):
-        begin = pl.multiple_of(lax.rem(me + count - behind, count) * rows, 8)
-        target[pl.ds(begin, rows), :] = chunk[...].astype(F32)
-
-
 def core_add(own, other, out):
     def strip(step, carry):
         at = pl.ds(pl.multiple_of(step * 2 * STRIP, 2 * STRIP), 2 * STRIP)
@@ -427,52 +407,60 @@
     lax.fori_loop(0, PACKED // (2 * STRIP), strip, 0)
 
 
-def sum_of(kept, received):
-    value = kept[...]
-    for part in received:
-        value = value + part[...].astype(F32)
-    return value
-
-
-def block_sum(where, parts, kept, *rest):
-    *chunks, total = rest
+def added(parts):
     value = parts[0].astype(F32)
     for at in range(1, parts.shape[0]):
         value = value + parts[at].astype(F32)
-    total[...] = value
-    emit_chunks(total, where[2], kept, chunks)
-
-
-def last_sum(before, *rest):
-    *received, out = rest
-    out[...] = sum_of(before, received).astype(BF16)
-
-
-def assemble(where, *rest):
-    *chunks, out, total = rest
-    place_chunks(total, where[2], chunks)
+    return value
+
+
+def block_sums(first, second, out):
+    rows = out.shape[2]
+    for which, parts in enumerate((first, second)):
+        value = added(parts)
+        for layer in range(out.shape[0]):
+            out[layer, which] = value[layer * rows : (layer + 1) * rows].astype(BF16)
+
+
+def layer_sums(parts, out):
+    value = added(parts).astype(BF16)
+    for layer in range(out.shape[0]):
+        out[layer] = value
+
+
+def assemble(parts, out, total):
+    layers, _, rows, _ = parts.shape
+    for which in range(2):
+        for layer in range(layers):
+            begin = (which * layers + layer) * rows
+            total[begin : begin + rows, :] = parts[layer, which].astype(F32)
     value = total[...].astype(BF16)
     for at in range(out.shape[0]):
         out[at] = value
 
 
-def unpack(packed, grad):
+def unpack(packed, first, second):
+    rows = packed.shape[1] // 2
+    size = 2 * STRIP
     half = FLAT // 2
 
     def strip(step, carry):
-        begin = pl.multiple_of(step * 2 * STRIP, 2 * STRIP)
-        for side in range(2):
-            at = begin + side * half
-            grad[pl.ds(at, 2 * STRIP), 0:LANES] = packed[pl.ds(at, 2 * STRIP), :].astype(F32)
-            grad[pl.ds(at, 2 * STRIP), LANES : 2 * LANES] = packed[
-                pl.ds(FLAT + at, 2 * STRIP), :
-            ].astype(F32)
-        tail = packed[pl.ds(2 * FLAT + begin, 2 * STRIP), :].astype(F32)
-        grad[pl.ds(begin, 2 * STRIP), 2 * LANES : C] = tail[:, 0:TAIL]
-        grad[pl.ds(begin + half, 2 * STRIP), 2 * LANES : C] = tail[:, TAIL : 2 * TAIL]
+        for which, grad in enumerate((first, second)):
+
+            def source(begin, which=which):
+                begin = begin + step * size
+                at = pl.multiple_of(which * rows + lax.rem(begin, rows), 16)
+                return packed[lax.div(begin, rows), pl.ds(at, size), :].astype(F32)
+
+            tail = source(2 * FLAT)
+            for side in range(2):
+                to = pl.ds(pl.multiple_of(step * size + side * half, 16), size)
+                grad[to, 0:LANES] = source(side * half)
+                grad[to, LANES : 2 * LANES] = source(FLAT + side * half)
+                grad[to, 2 * LANES : C] = tail[:, side * TAIL : (side + 1) * TAIL]
         return carry
 
-    lax.fori_loop(0, half // (2 * STRIP), strip, 0)
+    lax.fori_loop(0, half // size, strip, 0)
 
 
 def shape(dims, dtype):
@@ -532,22 +520,17 @@
     return lax.ppermute(array, "core", [(0, 1), (1, 0)])
 
 
-def ahead(value, axes, steps):
-    count = lax.axis_size(axes)
-    return lax.ppermute(value, axes, [(at, (at + steps) % count) for at in range(count)])
-
-
 BLOCK = ("z_low", "far", "y")
 LAYERS = "z_high"
 DP = (LAYERS, *BLOCK)
 
 
-def exchange(parts):
-    return lax.all_to_all(parts, BLOCK, split_axis=0, concat_axis=0, tiled=True)
+def exchange(parts, axes):
+    return lax.all_to_all(parts, axes, split_axis=0, concat_axis=0, tiled=True)
 
 
 def core_sum(own, other):
-    (pair,) = call(core_add, "vv", [((PACKED, LANES), BF16)], [], PACKED * LANES, "core_add", ALL_VMEM)(
+    (pair,) = call(core_add, "vv", [((PACKED, LANES), BF16)], [], PACKED * LANES, "core_add")(
         own, to_other_core(other)
     )
     return pair
@@ -555,38 +538,29 @@
 
 def spread_parts(pair):
     count = lax.axis_size(BLOCK)
-    return exchange(pair.reshape(count, PACKED // count, LANES))
-
-
-def layer_sum(where, parts):
-    count, rows, _ = parts.shape
+    return exchange(pair.reshape(count, PACKED // count, LANES), BLOCK)
+
+
+def gradients(first, second):
+    count, rows, _ = first.shape
     layers = lax.axis_size(LAYERS)
-    part = (rows // layers, LANES)
-    kept, *chunks = call(
-        block_sum, "sv", [(part, F32)] + [(part, BF16)] * (layers - 1),
-        [pltpu.VMEM((rows, LANES), F32)], PACKED * LANES, "block_sum",
-    )(where, parts)
-    received = [ahead(chunk, LAYERS, step + 1) for step, chunk in enumerate(chunks)]
-    (mine,) = call(last_sum, "v" * layers, [(part, BF16)], [], rows * LANES, "last_sum")(
-        kept, *received
-    )
-    received = [ahead(mine, LAYERS, step) for step in range(1, layers)]
+    cut = ((layers, 2, rows // layers, LANES), BF16)
+    (sums,) = call(block_sums, "vv", [cut], [], 2 * PACKED * LANES, "block_sums")(first, second)
+    (sums,) = call(layer_sums, "v", [cut], [], 2 * rows * LANES, "layer_sums")(
+        exchange(sums, LAYERS)
+    )
     (copies,) = call(
-        assemble, "s" + "v" * layers, [((count, rows, LANES), BF16)],
-        [pltpu.VMEM((rows, LANES), F32)], PACKED * LANES, "assemble",
-    )(where, mine, *received)
-    return copies
-
-
-def gradient(packed):
-    (grad,) = call(unpack, "v", [((FLAT, C), F32)], [], PACKED * LANES, "unpack")(
-        packed.reshape(PACKED, LANES)
-    )
-    return grad.reshape(1, 3, 3, C, C)
+        assemble, "v", [((count, 2 * rows, LANES), BF16)], [pltpu.VMEM((2 * rows, LANES), F32)],
+        2 * PACKED * LANES, "assemble",
+    )(exchange(sums, LAYERS))
+    grads = call(unpack, "v", [((FLAT, C), F32)] * 2, [], 2 * PACKED * LANES, "unpack")(
+        exchange(copies, BLOCK)
+    )
+    return tuple(grad.reshape(1, 3, 3, C, C) for grad in grads)
 
 
 def local(latents, cotangent, bucket, timesteps, w_enc, w_dec, w_time):
-    where = jnp.stack([lax.axis_index(axis) for axis in ("near", "core", LAYERS)])
+    where = jnp.stack([lax.axis_index(axis) for axis in ("near", "core")])
     where = where.astype(jnp.int32)
     micro_count = latents.shape[0]
     loss_scale = float(micro_count * lax.axis_size(DP) * CELLS) ** (-0.5)
@@ -594,8 +568,9 @@
     enc = w_enc.reshape(9, C, C)
     dec = w_dec.reshape(9, C, C)
     times = w_time.reshape(2, C, C)
+    times = (times, to_other_core(times))
     enc = (enc, to_other_core(enc))
-    times = (times, to_other_core(times))
+    dec, enc, times = lax.optimization_barrier((dec, enc, times))
     dec = (dec, to_other_core(dec))
     latents = latents.reshape(micro_count, CELLS, C)
     cotangent = cotangent.reshape(micro_count, CELLS, C)
@@ -617,7 +592,7 @@
     )
     two = call(
         phase_two, "ssv" + "h" * 6 + "vv", [NORMED, SCALE, ACTS, NORMED, SCALE, ACTS, ONE],
-        [pltpu.VMEM(*ACTS), TIMES, WEIGHTS, WEIGHTS, PADDED, SEMS], 4 * CONV, "two", ALL_VMEM,
+        [pltpu.VMEM(*ACTS), TIMES, WEIGHTS, WEIGHTS, PADDED, SEMS], 4 * CONV, "two",
     )
     be_normed, be_scale, be_hidden, bd_normed, bd_scale, bd_hidden, sent = two(
         where, bucket, up(sent), *times, *enc, *dec, emb, matrix
@@ -629,14 +604,14 @@
             pltpu.VMEM(*NORMED), pltpu.VMEM(*SCALE), pltpu.VMEM(*ONE), TIMES, WEIGHTS, PADDED,
             PADDED_COT, SEMS,
         ],
-        3 * CONV, "three", ALL_VMEM,
+        3 * CONV, "three",
     )
     ad_hidden, ad_cots, a_skips, sent = three(
         where, bucket, down(sent), cotangent, *times, *dec, a_kept, emb, matrix
     )
     four = call(
         phase_four, "ssv" + "h" * 6 + "v" * 6, [ACTS, ACTS, ONE],
-        [pltpu.VMEM(*ACTS), TIMES, WEIGHTS, WEIGHTS, PADDED_COT, SEMS], 4 * CONV, "four", ALL_VMEM,
+        [pltpu.VMEM(*ACTS), TIMES, WEIGHTS, WEIGHTS, PADDED_COT, SEMS], 4 * CONV, "four",
     )
     bd_cots, be_cots, sent = four(
         where, bucket, up(sent), *times, *enc, *dec, emb, matrix,
@@ -644,13 +619,13 @@
     )
     received = down(sent)
     work = [PADDED_COT, TURNED, pltpu.VMEM((2, PACKED, LANES), F32), pltpu.VMEM(*ACTS), pltpu.VMEM(*ACTS)]
-    weights = call(weight_phase, "svvvv", [OWN, OTHER], work, 2 * CONV, "weights", ALL_VMEM)
+    weights = call(weight_phase, "svvvv", [OWN, OTHER], work, 2 * CONV, "weights")
     dec_pair = core_sum(*weights(where, ad_hidden, ad_cots, bd_hidden, bd_cots))
     received, dec_pair = lax.optimization_barrier((received, dec_pair))
     dec_parts = spread_parts(dec_pair)
     five = call(
         phase_five, "ssv" + "h" * 4 + "v" * 8, [OWN, OTHER], [*work, TIMES, WEIGHTS, SEMS],
-        3 * CONV, "five", ALL_VMEM,
+        3 * CONV, "five",
     )
     enc_grads = five(
         where, bucket, received, *times, *enc, a_skips, emb, matrix, a_normed, a_scale, a_hidden,
@@ -658,9 +633,7 @@
     )
 
     enc_parts = spread_parts(core_sum(*enc_grads))
-    dec_copies = exchange(layer_sum(where, dec_parts))
-    enc_copies = exchange(layer_sum(where, enc_parts))
-    return gradient(enc_copies), gradient(dec_copies)
+    return gradients(enc_parts, dec_parts)
 
 
 def solution(mesh):

time: 256 us -> 231 us (0.902)
  blocking collectives: 0 us -> 106 us
  waiting for transfers between devices: 100 us -> 41.6 us
  starting transfers between devices: 65.7 us -> 14.2 us
  Pallas kernels: 76.9 us -> 52.6 us
    all_to_all x0 -> x4, blocking collectives: none -> 106 us  [exchange(): return lax.all_to_all(parts, axes, split_axis=0, concat_axis=0, tiled=True)]
    ppermute x12 -> x0, waiting for transfers between devices: 41.4 us -> none  [ahead(): lax.ppermute(value, axes, [(at, (at + steps) % count) for at in range(cou...]
    ppermute x12 -> x0, starting transfers between devices: 27.6 us -> none  [ahead(): lax.ppermute(value, axes, [(at, (at + steps) % count) for at in range(cou...]
    pallas_call x16 -> x12, Pallas kernels: 76.9 us -> 52.6 us  [run(): pl.pallas_call(body, out_shape=tuple((shape(d, t) for d, t in outs)), in_...]
    all_to_all x4 -> x1, starting transfers between devices: 31.4 us -> 7.55 us  [exchange(): return lax.all_to_all(parts, axes, split_axis=0, concat_axis=0, tiled=True)]
    all_to_all x4 -> x1, waiting for transfers between devices: 28.4 us -> 11.7 us  [exchange(): return lax.all_to_all(parts, axes, split_axis=0, concat_axis=0, tiled=True)]
    unnamed x24 -> x50, local copies, waits for them, and re-layouts: 9.64 us -> 11.5 us
  transfers between devices with their start and end apart: 25 -> 10, of which waited for: 16 -> 9; matrix products, arithmetic and copies ran while one was open for 1% -> 1% of each run, Pallas kernels for 14% -> 6%
where the time goes in v1:
time: 231 us; the launch traced here: 229 us
  blocking collectives  106 us (46%)
  Pallas kernels  52.6 us (23%)
  waiting for transfers between devices  41.6 us (18%)
  starting transfers between devices  14.2 us (6%)
  local copies, waits for them, and re-layouts  11.5 us (5%)
    all_to_all x4, blocking collectives, exchange(): return lax.all_to_all(parts, axes, split_axis=0, concat_axis=0, tiled=True)  106 us
    pallas_call x12, Pallas kernels, run(): pl.pallas_call(body, out_shape=tuple((shape(d, t) for d, t in outs)), in_...  52.6 us
    ppermute x2, waiting for transfers between devices, up(): return lax.ppermute(value, 'near', [(0, 1)])  14.1 us
    all_to_all x1, waiting for transfers between devices, exchange(): return lax.all_to_all(parts, axes, split_axis=0, concat_axis=0, tiled=True)  11.7 us
    unnamed x50, local copies, waits for them, and re-layouts  11.5 us
    ppermute x5, waiting for transfers between devices, to_other_core(): return lax.ppermute(array, 'core', [(0, 1), (1, 0)])  11.3 us
    all_to_all x1, starting transfers between devices, exchange(): return lax.all_to_all(parts, axes, split_axis=0, concat_axis=0, tiled=True)  7.55 us
  transfers between devices with their start and end apart: 10, of which 9 were waited for; matrix products, arithmetic and copies ran while one was open for 1% of the time, Pallas kernels for 6%

profile of v1, /device:TPU:2, one launch (start us, length us, event | category | flops | bytes accessed | tf_op | source)
XLA Modules:
  0.0 229.4 jit_solution(557376520906641988)
XLA Ops:
  1.2 4.4 %collective-permute-done.1.time_other = bf16[2,320,320]{2,1,0:T(8,128)(2,1)S(1)} collective-permute-done((bf16[2,320,320]{2,1,0:T(8,128)(2,1)}, bf16[2,320,320]{2,1,0:T(8,128)(2,1)S(1)}, u32[]{:S(2)}, u32[]{:S(2)}) %collective-permute-start.1) | collective-permute-done | bytes 409632 | tf_op jit(solution)/shard_map/ppermute | solution.py:520
  8.4 7.8 %one.1 = (f32[2,256,320]{2,1,0:T(8,128)}, f32[2,8,320]{2,1,0:T(8,128)}, bf16[2,256,320]{2,1,0:T(8,128)(2,1)}, bf16[2,256,320]{2,1,0:T(8,128)(2,1)}, bf16[256,320]{1,0:T(8,128)(2,1)}) custom-call(s32[2]{0:T(128)} %pad_add_fusion.where, s32[2,2]{1,0:T(2,128)} %bucket.9, bf16[2,256,320]{2,1,0:T(8,128)(2,1)} %bitcast.29, bf16[2,320,320]{2,1,0:T(8,128)(2,1)} %bitcast.21, ...), custom_call_target="tpu_custom_call" | custom-call | flops 943718400 | bytes 6543384 | tf_op jit(solution)/shard_map/one/pallas_call | solution.py:490
  16.2 1.3 collective-permute-start.2
  17.5 8.0 %collective-permute-done.2.x = bf16[256,320]{1,0:T(8,128)(2,1)S(1)} collective-permute-done((bf16[256,320]{1,0:T(8,128)(2,1)}, bf16[256,320]{1,0:T(8,128)(2,1)S(1)}, u32[]{:S(2)}, u32[]{:S(2)}) %collective-permute-start.2) | collective-permute-done | bytes 163872 | tf_op jit(solution)/shard_map/ppermute | solution.py:581
  25.5 1.6 copy-done.1
  27.1 1.0 copy-done.5
  28.2 9.7 %two.1 = (f32[2,256,320]{2,1,0:T(8,128)S(1)}, f32[2,8,320]{2,1,0:T(8,128)S(1)}, bf16[2,256,320]{2,1,0:T(8,128)(2,1)S(1)}, f32[2,256,320]{2,1,0:T(8,128)S(1)}, f3...) custom-call(s32[2]{0:T(128)S(1)} %copy-done.24, s32[2,2]{1,0:T(2,128)S(1)} %copy-done.22, ...), custom_call_target="tpu_custom_call" | custom-call | flops 1887436800 | bytes 10741784 | tf_op jit(solution)/shard_map/two/pallas_call | solution.py:490
  37.9 1.6 collective-permute-start.4
  39.5 3.9 %collective-permute-done.4.x = bf16[256,320]{1,0:T(8,128)(2,1)S(1)} collective-permute-done((bf16[256,320]{1,0:T(8,128)(2,1)S(1)}, bf16[256,320]{1,0:T(8,128)(2,1)S(1)}, u32[]{:S(2)}, u32[]{:S(2)}) %collective-permute-start.4) | collective-permute-done | bytes 163872 | tf_op jit(solution)/shard_map/ppermute | solution.py:584
  43.3 8.5 %three.1 = (bf16[2,256,320]{2,1,0:T(8,128)(2,1)S(1)}, bf16[2,256,320]{2,1,0:T(8,128)(2,1)S(1)}, bf16[2,256,320]{2,1,0:T(8,128)(2,1)S(1)}, bf16[256,320]{1,0:T(8,128)(2,1)S(1)}) custom-call(s32[2]{0:T(128)S(1)} %copy-done.24, s32[2,2]{1,0:T(2,128)S(1)} %copy-done.22, bf16[256,320]{1,0:T(8,128)(2,1)S(1)} %collective-permute-done.4.x, ...), custom_call_target="tpu_custom_call" | custom-call | flops 1415577600 | bytes 6686744 | tf_op jit(solution)/shard_map/three/pallas_call | solution.py:490
  52.7 1.5 collective-permute-start.5
  54.1 6.1 %collective-permute-done.5.x = bf16[256,320]{1,0:T(8,128)(2,1)S(1)} collective-permute-done((bf16[256,320]{1,0:T(8,128)(2,1)S(1)}, bf16[256,320]{1,0:T(8,128)(2,1)S(1)}, u32[]{:S(2)}, u32[]{:S(2)}) %collective-permute-start.5) | collective-permute-done | bytes 163872 | tf_op jit(solution)/shard_map/ppermute | solution.py:581
  60.2 9.4 %four.1 = (bf16[2,256,320]{2,1,0:T(8,128)(2,1)S(1)}, bf16[2,256,320]{2,1,0:T(8,128)(2,1)S(1)}, bf16[256,320]{1,0:T(8,128)(2,1)S(1)}) custom-call(s32[2]{0:T(128)S(1)} %copy-done.24, s32[2,2]{1,0:T(2,128)S(1)} %copy-done.22, bf16[256,320]{1,0:T(8,128)(2,1)S(1)} %collective-permute-done.5.x, bf16[2,320,320]{2,1,0:T(8,128)(2,1)S(1)} %bitcast.24, ...), custom_call_target="tpu_custom_call" | custom-call | flops 1887436800 | bytes 10741784 | tf_op jit(solution)/shard_map/four/pallas_call | solution.py:490
  69.6 3.4 %weights.1 = (f32[7680,128]{1,0:T(8,128)S(1)}, bf16[7680,128]{1,0:T(8,128)(2,1)S(1)}) custom-call(s32[2]{0:T(128)S(1)} %copy-done.24, bf16[2,256,320]{2,1,0:T(8,128)(2,1)S(1)} %get-tuple-element.48.a_hidden, bf16[2,256,320]{2,1,0:T(8,128)(2,1)S(1)} %get-tuple-element.49.a_cots, bf16[2,256,320]{2,1,0:T(8,128)(2,1)S(1)} %get-tuple-element.50.b_hidden, ...), custom_call_target="tpu_custom_call" | custom-call | flops 943718400 | bytes 7208968 | tf_op jit(solution)/shard_map/weights/pallas_call | solution.py:490
  73.2 1.5 collective-permute-start.6
  74.6 2.5 %collective-permute-done.7.other = bf16[7680,128]{1,0:T(8,128)(2,1)S(1)} collective-permute-done((bf16[7680,128]{1,0:T(8,128)(2,1)S(1)}, bf16[7680,128]{1,0:T(8,128)(2,1)S(1)}, u32[]{:S(2)}, u32[]{:S(2)}) %collective-permute-start.7) | collective-permute-done | bytes 1966112 | tf_op jit(solution)/shard_map/ppermute | solution.py:520
  77.6 1.3 copy-done.7
  80.2 7.6 %all-to-all-start.1 = ((bf16[16,480,128]{2,1,0:T(8,128)(2,1)}), bf16[16,480,128]{2,1,0:T(8,128)(2,1)}, u32[]{:S(2)}, u32[]{:S(2)}) async-start(bf16[16,480,128]{2,1,0:T(8,128)(2,1)} %bitcast.26), calls=%async_computation.1 | async-start | bytes 3932160 | tf_op jit(solution)/shard_map/all_to_all | solution.py:529
  87.8 1.1 copy-done.9
  89.0 1.0 copy-done.11
  90.0 1.0 copy-done.13
  91.0 1.0 copy-done.15
  92.0 1.0 copy-done.17
  93.9 6.0 %five.1 = (f32[7680,128]{1,0:T(8,128)S(1)}, bf16[7680,128]{1,0:T(8,128)(2,1)S(1)}) custom-call(s32[2]{0:T(128)S(1)} %copy-done.24, s32[2,2]{1,0:T(2,128)S(1)} %copy-done.22, bf16[256,320]{1,0:T(8,128)(2,1)S(1)} %copy-done.21, bf16[2,320,320]{2,1,0:T(8,128)(2,1)S(1)} %bitcast.25, bf16[2,320,320]{2,1,0:T(8,128)(2,1)S(1)} %copy-done.6, ...), custom_call_target="tpu_custom_call" | custom-call | flops 1415577600 | bytes 12769304 | tf_op jit(solution)/shard_map/five/pallas_call | solution.py:490
  100.0 4.0 %collective-permute-done.8.other = bf16[7680,128]{1,0:T(8,128)(2,1)S(1)} collective-permute-done((bf16[7680,128]{1,0:T(8,128)(2,1)S(1)}, bf16[7680,128]{1,0:T(8,128)(2,1)S(1)}, u32[]{:S(2)}, u32[]{:S(2)}) %collective-permute-start.8) | collective-permute-done | bytes 1966112 | tf_op jit(solution)/shard_map/ppermute | solution.py:520
  104.4 11.7 %all-to-all-done.1.second = bf16[16,480,128]{2,1,0:T(8,128)(2,1)} async-done(((bf16[16,480,128]{2,1,0:T(8,128)(2,1)}), bf16[16,480,128]{2,1,0:T(8,128)(2,1)}, u32[]{:S(2)}, u32[]{:S(2)}) %all-to-all-start.1) | async-done | bytes 1966112 | tf_op jit(solution)/shard_map/all_to_all | solution.py:529
  116.1 31.0 %all_to_all.25.first = bf16[16,480,128]{2,1,0:T(8,128)(2,1)S(1)} all-to-all(bf16[16,480,128]{2,1,0:T(8,128)(2,1)S(1)} %bitcast.27), channel_id=1, replica_groups=mesh['near'=2,'core'=2,'z_high'=4,'z_low'=2,'far'=2,'y'=4] {'z_low','far..., dimensions={0} | all-to-all | bytes 3932160 | tf_op jit(solution)/shard_map/all_to_all | solution.py:529
  147.1 2.1 block_sums.1
  149.1 17.0 %all_to_all.26.parts = bf16[4,2,120,128]{3,2,1,0:T(8,128)(2,1)S(1)} all-to-all(bf16[4,2,120,128]{3,2,1,0:T(8,128)(2,1)S(1)} %block_sums.1), channel_id=1, replica_groups=mesh['near'=2,'core'=2,'z_high'=4,'z_low'=2,'far'=2,'y'=4] {'z_high'}, dimensions={0} | all-to-all | bytes 491520 | tf_op jit(solution)/shard_map/all_to_all | solution.py:529
  166.2 12.7 %all_to_all.27.parts = bf16[4,2,120,128]{3,2,1,0:T(8,128)(2,1)S(1)} all-to-all(bf16[4,2,120,128]{3,2,1,0:T(8,128)(2,1)S(1)} %layer_sums.1), channel_id=1, replica_groups=mesh['near'=2,'core'=2,'z_high'=4,'z_low'=2,'far'=2,'y'=4] {'z_high'}, dimensions={0} | all-to-all | bytes 491520 | tf_op jit(solution)/shard_map/all_to_all | solution.py:529
  179.3 45.7 %all_to_all.28.packed = bf16[16,960,128]{2,1,0:T(8,128)(2,1)S(1)} all-to-all(bf16[16,960,128]{2,1,0:T(8,128)(2,1)S(1)} %assemble.1), channel_id=1, replica_groups=mesh['near'=2,'core'=2,'z_high'=4,'z_low'=2,'far'=2,'y'=4] {'z_low','far..., dimensions={0} | all-to-all | bytes 7864320 | tf_op jit(solution)/shard_map/all_to_all | solution.py:529
  225.0 4.4 %unpack.1 = (f32[2880,320]{1,0:T(8,128)}, f32[2880,320]{1,0:T(8,128)}) custom-call(bf16[16,960,128]{2,1,0:T(8,128)(2,1)S(1)} %all_to_all.28.packed), custom_call_target="tpu_custom_call" | custom-call | flops 1966080 | bytes 11304960 | tf_op jit(solution)/shard_map/unpack/pallas_call | solution.py:490
  (59 shorter events, 7.9 us)
Async XLA Ops:
  0.6 5.5 %collective-permute-start = (bf16[9,320,320]{2,1,0:T(8,128)(2,1)}, bf16[9,320,320]{2,1,0:T(8,128)(2,1)}, u32[]{:S(2)}, u32[]{:S(2)}) collective-permute-start(bf16[9,320,320]{2,1,0:T(8,128)(2,1)} %bitcast.11), channel_id=1, source_target_pairs={{0,64},{64,0},{1,65},{65,1},{2,66},{66,2},{3,67},{67,3},{4,68},{68... | collective-permute-start | bytes 5529608 | tf_op jit(solution)/shard_map/ppermute | solution.py:520
  0.7 4.9 %collective-permute-start.1 = (bf16[2,320,320]{2,1,0:T(8,128)(2,1)}, bf16[2,320,320]{2,1,0:T(8,128)(2,1)S(1)}, u32[]{:S(2)}, u32[]{:S(2)}) collective-permute-start(bf16[2,320,320]{2,1,0:T(8,128)(2,1)} %bitcast.20), channel_id=1, source_target_pairs={{0,64},{64,0},{1,65},{65,1},{2,66},{66,2},{3,67},{67,3},{4,68},{68... | collective-permute-start | bytes 1228808 | tf_op jit(solution)/shard_map/ppermute | solution.py:520
  5.6 2.8 %copy-start.4 = (bf16[2,320,320]{2,1,0:T(8,128)(2,1)}, bf16[2,320,320]{2,1,0:T(8,128)(2,1)S(1)}, u32[]{:S(2)}) copy-start(bf16[2,320,320]{2,1,0:T(8,128)(2,1)S(1)} %collective-permute-done.1.time_other) | copy-start | bytes 1228804
  6.1 19.4 %collective-permute-start.3 = (bf16[9,320,320]{2,1,0:T(8,128)(2,1)}, bf16[9,320,320]{2,1,0:T(8,128)(2,1)}, u32[]{:S(2)}, u32[]{:S(2)}) collective-permute-start(bf16[9,320,320]{2,1,0:T(8,128)(2,1)} %bitcast.16), channel_id=1, source_target_pairs={{0,64},{64,0},{1,65},{65,1},{2,66},{66,2},{3,67},{67,3},{4,68},{68... | collective-permute-start | bytes 5529608 | tf_op jit(solution)/shard_map/ppermute | solution.py:520
  8.3 17.1 %copy-start = (bf16[1,3,3,320,320]{4,3,2,1,0:T(8,128)(2,1)S(1)}, bf16[1,3,3,320,320]{4,3,2,1,0:T(8,128)(2,1)}, u32[]{:S(2)}) copy-start(bf16[1,3,3,320,320]{4,3,2,1,0:T(8,128)(2,1)} %param.12) | copy-start | bytes 5529604
  8.4 17.1 %copy-start.3 = (bf16[1,2,320,320]{3,2,1,0:T(8,128)(2,1)S(1)}, bf16[1,2,320,320]{3,2,1,0:T(8,128)(2,1)}, u32[]{:S(2)}) copy-start(bf16[1,2,320,320]{3,2,1,0:T(8,128)(2,1)} %param.14) | copy-start | bytes 1228804
  8.4 17.1 %copy-start.8 = (bf16[320,320]{1,0:T(8,128)(2,1)S(1)}, bf16[320,320]{1,0:T(8,128)(2,1)}, u32[]{:S(2)}) copy-start(bf16[320,320]{1,0:T(8,128)(2,1)} %constant.20.clone.matrix) | copy-start | bytes 614404
  8.4 17.1 %copy-start.10 = (bf16[16,320]{1,0:T(8,128)(2,1)S(1)}, bf16[16,320]{1,0:T(8,128)(2,1)}, u32[]{:S(2)}) copy-start(bf16[16,320]{1,0:T(8,128)(2,1)} %fusion.2.emb) | copy-start | bytes 30724
  8.4 17.1 %copy-start.22 = (s32[2,2]{1,0:T(2,128)S(1)}, s32[2,2]{1,0:T(2,128)}, u32[]{:S(2)}) copy-start(s32[2,2]{1,0:T(2,128)} %bucket.9) | copy-start | bytes 52
  8.4 17.1 %copy-start.24 = (s32[2]{0:T(128)S(1)}, s32[2]{0:T(128)}, u32[]{:S(2)}) copy-start(s32[2]{0:T(128)} %pad_add_fusion.where) | copy-start | bytes 28
  8.4 35.0 %copy-start.18 = (bf16[2,16,16,320]{3,2,1,0:T(8,128)(2,1)S(1)}, bf16[2,16,16,320]{3,2,1,0:T(8,128)(2,1)}, u32[]{:S(2)}) copy-start(bf16[2,16,16,320]{3,2,1,0:T(8,128)(2,1)} %param.9) | copy-start | bytes 983044
  16.2 9.3 %collective-permute-start.2 = (bf16[256,320]{1,0:T(8,128)(2,1)}, bf16[256,320]{1,0:T(8,128)(2,1)S(1)}, u32[]{:S(2)}, u32[]{:S(2)}) collective-permute-start(bf16[256,320]{1,0:T(8,128)(2,1)} %get-tuple-element.38), channel_id=1, source_target_pairs={{0,128},{1,129},{2,130},{3,131},{4,132},{5,133},{6,134},{7,135},{8... | collective-permute-start | bytes 491528 | tf_op jit(solution)/shard_map/ppermute | solution.py:581
  25.5 1.6 copy-start.1
  27.1 1.0 copy-start.5
  28.2 15.2 %copy-start.2 = (bf16[1,3,3,320,320]{4,3,2,1,0:T(8,128)(2,1)S(1)}, bf16[1,3,3,320,320]{4,3,2,1,0:T(8,128)(2,1)}, u32[]{:S(2)}) copy-start(bf16[1,3,3,320,320]{4,3,2,1,0:T(8,128)(2,1)} %param.13) | copy-start | bytes 5529604
  28.2 15.2 %copy-start.19 = (bf16[2,256,320]{2,1,0:T(8,128)(2,1)S(1)}, bf16[2,256,320]{2,1,0:T(8,128)(2,1)}, u32[]{:S(2)}) copy-start(bf16[2,256,320]{2,1,0:T(8,128)(2,1)} %get-tuple-element.41.kept) | copy-start | bytes 983044
  37.9 14.0 %copy-start.12 = (bf16[2,256,320]{2,1,0:T(8,128)(2,1)}, bf16[2,256,320]{2,1,0:T(8,128)(2,1)S(1)}, u32[]{:S(2)}) copy-start(bf16[2,256,320]{2,1,0:T(8,128)(2,1)S(1)} %get-tuple-element.59.b_hidden) | copy-start | bytes 983044
  37.9 5.4 %collective-permute-start.4 = (bf16[256,320]{1,0:T(8,128)(2,1)S(1)}, bf16[256,320]{1,0:T(8,128)(2,1)S(1)}, u32[]{:S(2)}, u32[]{:S(2)}) collective-permute-start(bf16[256,320]{1,0:T(8,128)(2,1)S(1)} %get-tuple-element.40), channel_id=1, source_target_pairs={{128,0},{129,1},{130,2},{131,3},{132,4},{133,5},{134,6},{135,7},{1... | collective-permute-start | bytes 491528 | tf_op jit(solution)/shard_map/ppermute | solution.py:584
  52.7 7.6 %collective-permute-start.5 = (bf16[256,320]{1,0:T(8,128)(2,1)S(1)}, bf16[256,320]{1,0:T(8,128)(2,1)S(1)}, u32[]{:S(2)}, u32[]{:S(2)}) collective-permute-start(bf16[256,320]{1,0:T(8,128)(2,1)S(1)} %get-tuple-element.42), channel_id=1, source_target_pairs={{0,128},{1,129},{2,130},{3,131},{4,132},{5,133},{6,134},{7,135},{8... | collective-permute-start | bytes 491528 | tf_op jit(solution)/shard_map/ppermute | solution.py:581
  69.6 7.5 %copy-start.16 = (bf16[2,256,320]{2,1,0:T(8,128)(2,1)}, bf16[2,256,320]{2,1,0:T(8,128)(2,1)S(1)}, u32[]{:S(2)}) copy-start(bf16[2,256,320]{2,1,0:T(8,128)(2,1)S(1)} %get-tuple-element.60.b_cots) | copy-start | bytes 983044
  73.1 4.1 %collective-permute-start.7 = (bf16[7680,128]{1,0:T(8,128)(2,1)S(1)}, bf16[7680,128]{1,0:T(8,128)(2,1)S(1)}, u32[]{:S(2)}, u32[]{:S(2)}) collective-permute-start(bf16[7680,128]{1,0:T(8,128)(2,1)S(1)} %get-tuple-element.53), channel_id=1, source_target_pairs={{0,64},{64,0},{1,65},{65,1},{2,66},{66,2},{3,67},{67,3},{4,68},{68... | collective-permute-start | bytes 5898248 | tf_op jit(solution)/shard_map/ppermute | solution.py:520
  73.2 6.4 %collective-permute-start.6 = (bf16[256,320]{1,0:T(8,128)(2,1)S(1)}, bf16[256,320]{1,0:T(8,128)(2,1)S(1)}, u32[]{:S(2)}, u32[]{:S(2)}) collective-permute-start(bf16[256,320]{1,0:T(8,128)(2,1)S(1)} %get-tuple-element.47), channel_id=1, source_target_pairs={{128,0},{129,1},{130,2},{131,3},{132,4},{133,5},{134,6},{135,7},{1... | collective-permute-start | bytes 491528 | tf_op jit(solution)/shard_map/ppermute | solution.py:584
  77.6 1.3 copy-start.7
  78.8 9.0 %copy-start.6 = (bf16[2,320,320]{2,1,0:T(8,128)(2,1)S(1)}, bf16[2,320,320]{2,1,0:T(8,128)(2,1)}, u32[]{:S(2)}) copy-start(bf16[2,320,320]{2,1,0:T(8,128)(2,1)} %copy-done.4) | copy-start | bytes 1228804
  78.8 9.0 %copy-start.23 = (f32[2,8,320]{2,1,0:T(8,128)S(1)}, f32[2,8,320]{2,1,0:T(8,128)}, u32[]{:S(2)}) copy-start(f32[2,8,320]{2,1,0:T(8,128)} %get-tuple-element.57.e_scale) | copy-start | bytes 61444
  80.2 35.8 %all-to-all-start.1 = ((bf16[16,480,128]{2,1,0:T(8,128)(2,1)}), bf16[16,480,128]{2,1,0:T(8,128)(2,1)}, u32[]{:S(2)}, u32[]{:S(2)}) async-start(bf16[16,480,128]{2,1,0:T(8,128)(2,1)} %bitcast.26), calls=%async_computation.1 | async-start | bytes 3932160 | tf_op jit(solution)/shard_map/all_to_all | solution.py:529
  87.8 1.1 copy-start.9
  89.0 1.0 copy-start.11
  90.0 1.0 copy-start.13
  91.0 1.0 copy-start.15
  91.9 1.0 copy-start.17
  99.9 4.1 %collective-permute-start.8 = (bf16[7680,128]{1,0:T(8,128)(2,1)S(1)}, bf16[7680,128]{1,0:T(8,128)(2,1)S(1)}, u32[]{:S(2)}, u32[]{:S(2)}) collective-permute-start(bf16[7680,128]{1,0:T(8,128)(2,1)S(1)} %get-tuple-element.62), channel_id=1, source_target_pairs={{0,64},{64,0},{1,65},{65,1},{2,66},{66,2},{3,67},{67,3},{4,68},{68... | collective-permute-start | bytes 5898248 | tf_op jit(solution)/shard_map/ppermute | solution.py:520
  (3 other events, 2.4 us)

commit v2 on v1

--- a/solution.py
+++ b/solution.py
@@ -398,13 +398,16 @@
     store_gradients(core, hidden, cots, own, other, padded_cot, turned, pair)
 
 
-def core_add(own, other, out):
-    def strip(step, carry):
-        at = pl.ds(pl.multiple_of(step * 2 * STRIP, 2 * STRIP), 2 * STRIP)
-        out[at, :] = (own[at, :] + other[at, :].astype(F32)).astype(BF16)
+def core_add(first, first_other, second, second_other, out):
+    rows = out.shape[1] // 2
+
+    def part(at, carry):
+        source = pl.ds(pl.multiple_of(at * rows, 16), rows)
+        out[at, 0:rows] = (first[source, :] + first_other[source, :].astype(F32)).astype(BF16)
+        out[at, rows:] = (second[source, :] + second_other[source, :].astype(F32)).astype(BF16)
         return carry
 
-    lax.fori_loop(0, PACKED // (2 * STRIP), strip, 0)
+    lax.fori_loop(0, out.shape[0], part, 0)
 
 
 def added(parts):
@@ -414,12 +417,13 @@
     return value
 
 
-def block_sums(first, second, out):
+def block_sums(parts, out):
     rows = out.shape[2]
-    for which, parts in enumerate((first, second)):
-        value = added(parts)
+    value = added(parts)
+    for which in range(2):
         for layer in range(out.shape[0]):
-            out[layer, which] = value[layer * rows : (layer + 1) * rows].astype(BF16)
+            begin = (which * out.shape[0] + layer) * rows
+            out[layer, which] = value[begin : begin + rows].astype(BF16)
 
 
 def layer_sums(parts, out):
@@ -513,9 +517,6 @@
     return jnp.concatenate([jnp.cos(angles), jnp.sin(angles)], axis=1).astype(BF16)
 
 
-DP = ("z", "far", "y")
-
-
 def to_other_core(array):
     return lax.ppermute(array, "core", [(0, 1), (1, 0)])
 
@@ -529,23 +530,16 @@
     return lax.all_to_all(parts, axes, split_axis=0, concat_axis=0, tiled=True)
 
 
-def core_sum(own, other):
-    (pair,) = call(core_add, "vv", [((PACKED, LANES), BF16)], [], PACKED * LANES, "core_add")(
-        own, to_other_core(other)
-    )
-    return pair
-
-
-def spread_parts(pair):
-    count = lax.axis_size(BLOCK)
-    return exchange(pair.reshape(count, PACKED // count, LANES), BLOCK)
-
-
 def gradients(first, second):
-    count, rows, _ = first.shape
-    layers = lax.axis_size(LAYERS)
+    count, layers = lax.axis_size(BLOCK), lax.axis_size(LAYERS)
+    rows = PACKED // count
+    (pair,) = call(
+        core_add, "vvvv", [((count, 2 * rows, LANES), BF16)], [], 2 * PACKED * LANES, "core_add"
+    )(*first, *second)
     cut = ((layers, 2, rows // layers, LANES), BF16)
-    (sums,) = call(block_sums, "vv", [cut], [], 2 * PACKED * LANES, "block_sums")(first, second)
+    (sums,) = call(block_sums, "v", [cut], [], 2 * PACKED * LANES, "block_sums")(
+        exchange(pair, BLOCK)
+    )
     (sums,) = call(layer_sums, "v", [cut], [], 2 * rows * LANES, "layer_sums")(
         exchange(sums, LAYERS)
     )
@@ -570,11 +564,11 @@
     times = w_time.reshape(2, C, C)
     times = (times, to_other_core(times))
     enc = (enc, to_other_core(enc))
-    dec, enc, times = lax.optimization_barrier((dec, enc, times))
+    emb = jnp.pad(time_embed(timesteps), ((0, 16 - micro_count), (0, 0)))
+    dec, enc, times, emb, where = lax.optimization_barrier((dec, enc, times, emb, where))
     dec = (dec, to_other_core(dec))
     latents = latents.reshape(micro_count, CELLS, C)
     cotangent = cotangent.reshape(micro_count, CELLS, C)
-    emb = jnp.pad(time_embed(timesteps), ((0, 16 - micro_count), (0, 0)))
     matrix = group_matrix()
 
     def up(value):
@@ -585,7 +579,7 @@
 
     one = call(
         phase_one, "ss" + "h" * 5 + "vv", [NORMED, SCALE, ACTS, ACTS, ONE],
-        [pltpu.VMEM(*ONE), TIMES, WEIGHTS, PADDED, SEMS], 2 * CONV, "one", ALL_VMEM,
+        [pltpu.VMEM(*ONE), TIMES, WEIGHTS, PADDED, SEMS], 2 * CONV, "one",
     )
     a_normed, a_scale, a_hidden, a_kept, sent = one(
         where, bucket, latents, *times, *enc, emb, matrix
@@ -620,20 +614,18 @@
     received = down(sent)
     work = [PADDED_COT, TURNED, pltpu.VMEM((2, PACKED, LANES), F32), pltpu.VMEM(*ACTS), pltpu.VMEM(*ACTS)]
     weights = call(weight_phase, "svvvv", [OWN, OTHER], work, 2 * CONV, "weights")
-    dec_pair = core_sum(*weights(where, ad_hidden, ad_cots, bd_hidden, bd_cots))
-    received, dec_pair = lax.optimization_barrier((received, dec_pair))
-    dec_parts = spread_parts(dec_pair)
+    own_dec, other_dec = weights(where, ad_hidden, ad_cots, bd_hidden, bd_cots)
+    dec_pair = (own_dec, to_other_core(other_dec))
     five = call(
         phase_five, "ssv" + "h" * 4 + "v" * 8, [OWN, OTHER], [*work, TIMES, WEIGHTS, SEMS],
         3 * CONV, "five",
     )
-    enc_grads = five(
+    own_enc, other_enc = five(
         where, bucket, received, *times, *enc, a_skips, emb, matrix, a_normed, a_scale, a_hidden,
         be_hidden, be_cots,
     )
 
-    enc_parts = spread_parts(core_sum(*enc_grads))
-    return gradients(enc_parts, dec_parts)
+    return gradients((own_enc, to_other_core(other_enc)), dec_pair)
 
 
 def solution(mesh):

time: 231 us -> 221 us (0.957)
  blocking collectives: 106 us -> 136 us
  waiting for transfers between devices: 41.6 us -> 25.3 us
  Pallas kernels: 52.6 us -> 44.8 us
  starting transfers between devices: 14.2 us -> 7.19 us
  local copies, waits for them, and re-layouts: 11.5 us -> 5.29 us
    all_to_all x4, blocking collectives: 106 us -> 136 us  [exchange(): return lax.all_to_all(parts, axes, split_axis=0, concat_axis=0, tiled=True)]
    all_to_all x1 -> x0, waiting for transfers between devices: 11.7 us -> none  [exchange(): return lax.all_to_all(parts, axes, split_axis=0, concat_axis=0, tiled=True)]
    pallas_call x12 -> x11, Pallas kernels: 52.6 us -> 44.8 us  [run(): pl.pallas_call(body, out_shape=tuple((shape(d, t) for d, t in outs)), in_...]
    all_to_all x1 -> x0, starting transfers between devices: 7.55 us -> none  [exchange(): return lax.all_to_all(parts, axes, split_axis=0, concat_axis=0, tiled=True)]
    unnamed x50 -> x22, local copies, waits for them, and re-layouts: 11.5 us -> 5.29 us
    ppermute x5, waiting for transfers between devices: 11.3 us -> 7.38 us  [to_other_core(): return lax.ppermute(array, 'core', [(0, 1), (1, 0)])]
  transfers between devices with their start and end apart: 10 -> 9, of which waited for: 9 -> 5; matrix products, arithmetic and copies ran while one was open for 1% -> 0% of each run, Pallas kernels for 6% -> 6%
where the time goes in v2:
time: 221 us
  blocking collectives  136 us (62%)
  Pallas kernels  44.8 us (20%)
  waiting for transfers between devices  25.3 us (11%)
  starting transfers between devices  7.19 us (3%)
  local copies, waits for them, and re-layouts  5.29 us (2%)
    all_to_all x4, blocking collectives, exchange(): return lax.all_to_all(parts, axes, split_axis=0, concat_axis=0, tiled=True)  136 us
    pallas_call x11, Pallas kernels, run(): pl.pallas_call(body, out_shape=tuple((shape(d, t) for d, t in outs)), in_...  44.8 us
    ppermute x2, waiting for transfers between devices, up(): return lax.ppermute(value, 'near', [(0, 1)])  13.9 us
    ppermute x5, waiting for transfers between devices, to_other_core(): return lax.ppermute(array, 'core', [(0, 1), (1, 0)])  7.38 us
    unnamed x22, local copies, waits for them, and re-layouts  5.29 us
  transfers between devices with their start and end apart: 9, of which 5 were waited for; matrix products, arithmetic and copies ran while one was open for 0% of the time, Pallas kernels for 6%

profile of v2, /device:TPU:2, one launch (start us, length us, event | category | flops | bytes accessed | tf_op | source)
XLA Modules:
  0.0 220.8 jit_solution(7206063064313723666)
XLA Ops:
  0.7 0.5 collective-permute-start.1
  1.2 0.7 convert_element_type.6
  2.2 3.8 %collective-permute-done.1.time_other = bf16[2,320,320]{2,1,0:T(8,128)(2,1)S(1)} collective-permute-done((bf16[2,320,320]{2,1,0:T(8,128)(2,1)}, bf16[2,320,320]{2,1,0:T(8,128)(2,1)S(1)}, u32[]{:S(2)}, u32[]{:S(2)}) %collective-permute-start.1) | collective-permute-done | bytes 409632 | tf_op jit(solution)/shard_map/ppermute | solution.py:521
  6.0 0.1 collective-permute-start.3
  6.1 1.6 copy-done
  7.7 1.0 copy-done.3
  8.8 0.9 copy-done.5
  9.7 1.0 copy-done.7
  10.7 0.7 copy-done.9
  11.4 5.4 %one.1 = (f32[2,256,320]{2,1,0:T(8,128)S(1)}, f32[2,8,320]{2,1,0:T(8,128)S(1)}, bf16[2,256,320]{2,1,0:T(8,128)(2,1)S(1)}, bf16[2,256,320]{2,1,0:T(8,128)(2,1)S(1)}, bf16[256,320]{1,0:T(8,128)(2,1)S(1)}) custom-call(s32[2]{0:T(128)S(1)} %pad_add_fusion.where, s32[2,2]{1,0:T(2,128)S(1)} %copy-done.9, bf16[2,256,320]{2,1,0:T(8,128)(2,1)S(1)} %bitcast.24, ...), custom_call_target="tpu_custom_call" | custom-call | flops 943718400 | bytes 6543384 | tf_op jit(solution)/shard_map/one/pallas_call | solution.py:494
  16.8 1.4 collective-permute-start.2
  18.2 7.8 %collective-permute-done.2.x = bf16[256,320]{1,0:T(8,128)(2,1)S(1)} collective-permute-done((bf16[256,320]{1,0:T(8,128)(2,1)S(1)}, bf16[256,320]{1,0:T(8,128)(2,1)S(1)}, u32[]{:S(2)}, u32[]{:S(2)}) %collective-permute-start.2) | collective-permute-done | bytes 163872 | tf_op jit(solution)/shard_map/ppermute | solution.py:575
  26.0 9.0 %two.1 = (f32[2,256,320]{2,1,0:T(8,128)S(1)}, f32[2,8,320]{2,1,0:T(8,128)S(1)}, bf16[2,256,320]{2,1,0:T(8,128)(2,1)S(1)}, f32[2,256,320]{2,1,0:T(8,128)S(1)}, f3...) custom-call(s32[2]{0:T(128)S(1)} %pad_add_fusion.where, ...), custom_call_target="tpu_custom_call" | custom-call | flops 1887436800 | bytes 10741784 | tf_op jit(solution)/shard_map/two/pallas_call | solution.py:494
  35.1 1.5 collective-permute-start.4
  36.5 4.0 %collective-permute-done.4.x = bf16[256,320]{1,0:T(8,128)(2,1)S(1)} collective-permute-done((bf16[256,320]{1,0:T(8,128)(2,1)S(1)}, bf16[256,320]{1,0:T(8,128)(2,1)S(1)}, u32[]{:S(2)}, u32[]{:S(2)}) %collective-permute-start.4) | collective-permute-done | bytes 163872 | tf_op jit(solution)/shard_map/ppermute | solution.py:578
  40.5 7.5 %three.1 = (bf16[2,256,320]{2,1,0:T(8,128)(2,1)S(1)}, bf16[2,256,320]{2,1,0:T(8,128)(2,1)S(1)}, bf16[2,256,320]{2,1,0:T(8,128)(2,1)S(1)}, bf16[256,320]{1,0:T(8,128)(2,1)S(1)}) custom-call(s32[2]{0:T(128)S(1)} %pad_add_fusion.where, s32[2,2]{1,0:T(2,128)S(1)} %copy-done.9, bf16[256,320]{1,0:T(8,128)(2,1)S(1)} %collective-permute-done.4.x, ...), custom_call_target="tpu_custom_call" | custom-call | flops 1415577600 | bytes 6686744 | tf_op jit(solution)/shard_map/three/pallas_call | solution.py:494
  48.0 1.5 collective-permute-start.5
  49.5 6.1 %collective-permute-done.5.x = bf16[256,320]{1,0:T(8,128)(2,1)S(1)} collective-permute-done((bf16[256,320]{1,0:T(8,128)(2,1)S(1)}, bf16[256,320]{1,0:T(8,128)(2,1)S(1)}, u32[]{:S(2)}, u32[]{:S(2)}) %collective-permute-start.5) | collective-permute-done | bytes 163872 | tf_op jit(solution)/shard_map/ppermute | solution.py:575
  55.6 8.7 %four.1 = (bf16[2,256,320]{2,1,0:T(8,128)(2,1)S(1)}, bf16[2,256,320]{2,1,0:T(8,128)(2,1)S(1)}, bf16[256,320]{1,0:T(8,128)(2,1)S(1)}) custom-call(s32[2]{0:T(128)S(1)} %pad_add_fusion.where, s32[2,2]{1,0:T(2,128)S(1)} %copy-done.9, bf16[256,320]{1,0:T(8,128)(2,1)S(1)} %collective-permute-done.5.x, bf16[2,320,320]{2,1,0:T(8,128)(2,1)S(1)} %bitcast.22, ...), custom_call_target="tpu_custom_call" | custom-call | flops 1887436800 | bytes 10741784 | tf_op jit(solution)/shard_map/four/pallas_call | solution.py:494
  64.3 1.5 collective-permute-start.6
  65.8 3.4 %weights.1 = (f32[7680,128]{1,0:T(8,128)S(1)}, bf16[7680,128]{1,0:T(8,128)(2,1)S(1)}) custom-call(s32[2]{0:T(128)S(1)} %pad_add_fusion.where, bf16[2,256,320]{2,1,0:T(8,128)(2,1)S(1)} %get-tuple-element.58.a_hidden, bf16[2,256,320]{2,1,0:T(8,128)(2,1)S(1)} %get-tuple-element.59.a_cots, bf16[2,256,320]{2,1,0:T(8,128)(2,1)S(1)} %get-tuple-element.60.b_hidden, ...), custom_call_target="tpu_custom_call" | custom-call | flops 943718400 | bytes 7208968 | tf_op jit(solution)/shard_map/weights/pallas_call | solution.py:494
  69.3 4.7 %five.1 = (f32[7680,128]{1,0:T(8,128)S(1)}, bf16[7680,128]{1,0:T(8,128)(2,1)S(1)}) custom-call(s32[2]{0:T(128)S(1)} %pad_add_fusion.where, s32[2,2]{1,0:T(2,128)S(1)} %copy-done.10, bf16[256,320]{1,0:T(8,128)(2,1)S(1)} %collective-permute-done.6.x, bf16[2,320,320]{2,1,0:T(8,128)(2,1)S(1)} %bitcast.23, ...), custom_call_target="tpu_custom_call" | custom-call | flops 1415577600 | bytes 12769304 | tf_op jit(solution)/shard_map/five/pallas_call | solution.py:494
  74.1 0.6 collective-permute-start.7
  74.6 3.6 %collective-permute-done.7.first_other = bf16[7680,128]{1,0:T(8,128)(2,1)S(1)} collective-permute-done((bf16[7680,128]{1,0:T(8,128)(2,1)S(1)}, bf16[7680,128]{1,0:T(8,128)(2,1)S(1)}, u32[]{:S(2)}, u32[]{:S(2)}) %collective-permute-start.7) | collective-permute-done | bytes 1966112 | tf_op jit(solution)/shard_map/ppermute | solution.py:521
  78.2 0.8 core_add.1
  79.0 57.0 %all_to_all.20.parts = bf16[16,960,128]{2,1,0:T(8,128)(2,1)S(1)} all-to-all(bf16[16,960,128]{2,1,0:T(8,128)(2,1)S(1)} %core_add.1), channel_id=1, replica_groups=mesh['near'=2,'core'=2,'z_high'=4,'z_low'=2,'far'=2,'y'=4] {'z_low','far..., dimensions={0} | all-to-all | bytes 7864320 | tf_op jit(solution)/shard_map/all_to_all | solution.py:530
  136.0 0.5 block_sums.1
  136.5 17.0 %all_to_all.21.parts = bf16[4,2,120,128]{3,2,1,0:T(8,128)(2,1)S(1)} all-to-all(bf16[4,2,120,128]{3,2,1,0:T(8,128)(2,1)S(1)} %block_sums.1), channel_id=1, replica_groups=mesh['near'=2,'core'=2,'z_high'=4,'z_low'=2,'far'=2,'y'=4] {'z_high'}, dimensions={0} | all-to-all | bytes 491520 | tf_op jit(solution)/shard_map/all_to_all | solution.py:530
  153.6 13.0 %all_to_all.22.parts = bf16[4,2,120,128]{3,2,1,0:T(8,128)(2,1)S(1)} all-to-all(bf16[4,2,120,128]{3,2,1,0:T(8,128)(2,1)S(1)} %layer_sums.1), channel_id=1, replica_groups=mesh['near'=2,'core'=2,'z_high'=4,'z_low'=2,'far'=2,'y'=4] {'z_high'}, dimensions={0} | all-to-all | bytes 491520 | tf_op jit(solution)/shard_map/all_to_all | solution.py:530
  166.5 0.4 assemble.1
  166.9 49.5 %all_to_all.23.packed = bf16[16,960,128]{2,1,0:T(8,128)(2,1)S(1)} all-to-all(bf16[16,960,128]{2,1,0:T(8,128)(2,1)S(1)} %assemble.1), channel_id=1, replica_groups=mesh['near'=2,'core'=2,'z_high'=4,'z_low'=2,'far'=2,'y'=4] {'z_low','far..., dimensions={0} | all-to-all | bytes 7864320 | tf_op jit(solution)/shard_map/all_to_all | solution.py:530
  216.4 4.4 %unpack.1 = (f32[2880,320]{1,0:T(8,128)}, f32[2880,320]{1,0:T(8,128)}) custom-call(bf16[16,960,128]{2,1,0:T(8,128)(2,1)S(1)} %all_to_all.23.packed), custom_call_target="tpu_custom_call" | custom-call | flops 1966080 | bytes 11304960 | tf_op jit(solution)/shard_map/unpack/pallas_call | solution.py:494
  (28 shorter events, 0.5 us)
Async XLA Ops:
  0.6 5.3 %collective-permute-start = (bf16[9,320,320]{2,1,0:T(8,128)(2,1)}, bf16[9,320,320]{2,1,0:T(8,128)(2,1)S(1)}, u32[]{:S(2)}, u32[]{:S(2)}) collective-permute-start(bf16[9,320,320]{2,1,0:T(8,128)(2,1)} %bitcast.9), channel_id=1, source_target_pairs={{0,64},{64,0},{1,65},{65,1},{2,66},{66,2},{3,67},{67,3},{4,68},{68... | collective-permute-start | bytes 5529608 | tf_op jit(solution)/shard_map/ppermute | solution.py:521
  0.7 5.2 %collective-permute-start.1 = (bf16[2,320,320]{2,1,0:T(8,128)(2,1)}, bf16[2,320,320]{2,1,0:T(8,128)(2,1)S(1)}, u32[]{:S(2)}, u32[]{:S(2)}) collective-permute-start(bf16[2,320,320]{2,1,0:T(8,128)(2,1)} %bitcast.18), channel_id=1, source_target_pairs={{0,64},{64,0},{1,65},{65,1},{2,66},{66,2},{3,67},{67,3},{4,68},{68... | collective-permute-start | bytes 1228808 | tf_op jit(solution)/shard_map/ppermute | solution.py:521
  6.0 20.1 %collective-permute-start.3 = (bf16[9,320,320]{2,1,0:T(8,128)(2,1)}, bf16[9,320,320]{2,1,0:T(8,128)(2,1)S(1)}, u32[]{:S(2)}, u32[]{:S(2)}) collective-permute-start(bf16[9,320,320]{2,1,0:T(8,128)(2,1)} %bitcast.14), channel_id=1, source_target_pairs={{0,64},{64,0},{1,65},{65,1},{2,66},{66,2},{3,67},{67,3},{4,68},{68... | collective-permute-start | bytes 5529608 | tf_op jit(solution)/shard_map/ppermute | solution.py:521
  6.1 1.6 copy-start
  7.7 1.0 copy-start.3
  8.8 0.9 copy-start.5
  9.7 1.0 copy-start.7
  10.7 0.7 copy-start.9
  11.4 14.7 %copy-start.1 = (bf16[1,3,3,320,320]{4,3,2,1,0:T(8,128)(2,1)S(1)}, bf16[1,3,3,320,320]{4,3,2,1,0:T(8,128)(2,1)}, u32[]{:S(2)}) copy-start(bf16[1,3,3,320,320]{4,3,2,1,0:T(8,128)(2,1)} %param.12) | copy-start | bytes 5529604
  11.4 14.7 %copy-start.2 = (bf16[1,3,3,320,320]{4,3,2,1,0:T(8,128)(2,1)S(1)}, bf16[1,3,3,320,320]{4,3,2,1,0:T(8,128)(2,1)}, u32[]{:S(2)}) copy-start(bf16[1,3,3,320,320]{4,3,2,1,0:T(8,128)(2,1)} %param.13) | copy-start | bytes 5529604
  11.4 14.7 %copy-start.6 = (bf16[320,320]{1,0:T(8,128)(2,1)S(1)}, bf16[320,320]{1,0:T(8,128)(2,1)}, u32[]{:S(2)}) copy-start(bf16[320,320]{1,0:T(8,128)(2,1)} %constant.20.clone.matrix) | copy-start | bytes 614404
  16.8 23.7 %copy-start.8 = (bf16[2,16,16,320]{3,2,1,0:T(8,128)(2,1)S(1)}, bf16[2,16,16,320]{3,2,1,0:T(8,128)(2,1)}, u32[]{:S(2)}) copy-start(bf16[2,16,16,320]{3,2,1,0:T(8,128)(2,1)} %param.9) | copy-start | bytes 983044
  16.8 9.2 %collective-permute-start.2 = (bf16[256,320]{1,0:T(8,128)(2,1)S(1)}, bf16[256,320]{1,0:T(8,128)(2,1)S(1)}, u32[]{:S(2)}, u32[]{:S(2)}) collective-permute-start(bf16[256,320]{1,0:T(8,128)(2,1)S(1)} %get-tuple-element.40), channel_id=1, source_target_pairs={{0,128},{1,129},{2,130},{3,131},{4,132},{5,133},{6,134},{7,135},{8... | collective-permute-start | bytes 491528 | tf_op jit(solution)/shard_map/ppermute | solution.py:575
  35.1 5.4 %collective-permute-start.4 = (bf16[256,320]{1,0:T(8,128)(2,1)S(1)}, bf16[256,320]{1,0:T(8,128)(2,1)S(1)}, u32[]{:S(2)}, u32[]{:S(2)}) collective-permute-start(bf16[256,320]{1,0:T(8,128)(2,1)S(1)} %get-tuple-element.42), channel_id=1, source_target_pairs={{128,0},{129,1},{130,2},{131,3},{132,4},{133,5},{134,6},{135,7},{1... | collective-permute-start | bytes 491528 | tf_op jit(solution)/shard_map/ppermute | solution.py:578
  48.0 7.6 %collective-permute-start.5 = (bf16[256,320]{1,0:T(8,128)(2,1)S(1)}, bf16[256,320]{1,0:T(8,128)(2,1)S(1)}, u32[]{:S(2)}, u32[]{:S(2)}) collective-permute-start(bf16[256,320]{1,0:T(8,128)(2,1)S(1)} %get-tuple-element.44), channel_id=1, source_target_pairs={{0,128},{1,129},{2,130},{3,131},{4,132},{5,133},{6,134},{7,135},{8... | collective-permute-start | bytes 491528 | tf_op jit(solution)/shard_map/ppermute | solution.py:575
  55.6 13.7 %copy-start.4 = (bf16[1,2,320,320]{3,2,1,0:T(8,128)(2,1)S(1)}, bf16[1,2,320,320]{3,2,1,0:T(8,128)(2,1)}, u32[]{:S(2)}) copy-start(bf16[1,2,320,320]{3,2,1,0:T(8,128)(2,1)} %param.14) | copy-start | bytes 1228804
  55.6 13.7 %copy-start.10 = (s32[2,2]{1,0:T(2,128)S(1)}, s32[2,2]{1,0:T(2,128)}, u32[]{:S(2)}) copy-start(s32[2,2]{1,0:T(2,128)} %bucket.9) | copy-start | bytes 52
  64.3 5.0 %collective-permute-start.6 = (bf16[256,320]{1,0:T(8,128)(2,1)S(1)}, bf16[256,320]{1,0:T(8,128)(2,1)S(1)}, u32[]{:S(2)}, u32[]{:S(2)}) collective-permute-start(bf16[256,320]{1,0:T(8,128)(2,1)S(1)} %get-tuple-element.49), channel_id=1, source_target_pairs={{128,0},{129,1},{130,2},{131,3},{132,4},{133,5},{134,6},{135,7},{1... | collective-permute-start | bytes 491528 | tf_op jit(solution)/shard_map/ppermute | solution.py:578
  69.2 5.4 %collective-permute-start.8 = (bf16[7680,128]{1,0:T(8,128)(2,1)S(1)}, bf16[7680,128]{1,0:T(8,128)(2,1)S(1)}, u32[]{:S(2)}, u32[]{:S(2)}) collective-permute-start(bf16[7680,128]{1,0:T(8,128)(2,1)S(1)} %get-tuple-element.63), channel_id=1, source_target_pairs={{0,64},{64,0},{1,65},{65,1},{2,66},{66,2},{3,67},{67,3},{4,68},{68... | collective-permute-start | bytes 5898248 | tf_op jit(solution)/shard_map/ppermute | solution.py:521
  74.1 4.2 %collective-permute-start.7 = (bf16[7680,128]{1,0:T(8,128)(2,1)S(1)}, bf16[7680,128]{1,0:T(8,128)(2,1)S(1)}, u32[]{:S(2)}, u32[]{:S(2)}) collective-permute-start(bf16[7680,128]{1,0:T(8,128)(2,1)S(1)} %get-tuple-element.57), channel_id=1, source_target_pairs={{0,64},{64,0},{1,65},{65,1},{2,66},{66,2},{3,67},{67,3},{4,68},{68... | collective-permute-start | bytes 5898248 | tf_op jit(solution)/shard_map/ppermute | solution.py:521

commit v3 on v2

--- a/solution.py
+++ b/solution.py
@@ -417,27 +417,37 @@
     return value
 
 
-def block_sums(parts, out):
-    rows = out.shape[2]
-    value = added(parts)
+def block_sums(where, parts, kept, *rest):
+    *chunks, total = rest
+    layers = len(chunks) + 1
+    rows = kept.shape[1]
+    total[...] = added(parts)
     for which in range(2):
-        for layer in range(out.shape[0]):
-            begin = (which * out.shape[0] + layer) * rows
-            out[layer, which] = value[begin : begin + rows].astype(BF16)
-
-
-def layer_sums(parts, out):
-    value = added(parts).astype(BF16)
-    for layer in range(out.shape[0]):
-        out[layer] = value
-
-
-def assemble(parts, out, total):
-    layers, _, rows, _ = parts.shape
+        for ahead in range(layers):
+            at = which * layers + lax.rem(where[2] + ahead, layers)
+            value = total[pl.ds(pl.multiple_of(at * rows, 8), rows), :]
+            if ahead == 0:
+                kept[which] = value
+            else:
+                chunks[ahead - 1][which] = value.astype(BF16)
+
+
+def layer_sums(kept, *rest):
+    *received, out = rest
+    value = kept[...]
+    for part in received:
+        value = value + part[...].astype(F32)
+    out[...] = value.astype(BF16)
+
+
+def assemble(where, *rest):
+    *chunks, out, total = rest
+    layers = len(chunks)
+    rows = chunks[0].shape[1]
     for which in range(2):
-        for layer in range(layers):
-            begin = (which * layers + layer) * rows
-            total[begin : begin + rows, :] = parts[layer, which].astype(F32)
+        for behind, chunk in enumerate(chunks):
+            at = which * layers + lax.rem(where[2] + layers - behind, layers)
+            total[pl.ds(pl.multiple_of(at * rows, 8), rows), :] = chunk[which].astype(F32)
     value = total[...].astype(BF16)
     for at in range(out.shape[0]):
         out[at] = value
@@ -530,23 +540,32 @@
     return lax.all_to_all(parts, axes, split_axis=0, concat_axis=0, tiled=True)
 
 
-def gradients(first, second):
+def ahead(value, steps):
+    count = lax.axis_size(LAYERS)
+    return lax.ppermute(value, LAYERS, [(at, (at + steps) % count) for at in range(count)])
+
+
+def gradients(where, first, second):
     count, layers = lax.axis_size(BLOCK), lax.axis_size(LAYERS)
     rows = PACKED // count
     (pair,) = call(
         core_add, "vvvv", [((count, 2 * rows, LANES), BF16)], [], 2 * PACKED * LANES, "core_add"
     )(*first, *second)
-    cut = ((layers, 2, rows // layers, LANES), BF16)
-    (sums,) = call(block_sums, "v", [cut], [], 2 * PACKED * LANES, "block_sums")(
-        exchange(pair, BLOCK)
-    )
-    (sums,) = call(layer_sums, "v", [cut], [], 2 * rows * LANES, "layer_sums")(
-        exchange(sums, LAYERS)
-    )
+    cut = (2, rows // layers, LANES)
+    total = [pltpu.VMEM((2 * rows, LANES), F32)]
+    kept, *chunks = call(
+        block_sums, "sv", [(cut, F32)] + [(cut, BF16)] * (layers - 1), total, 2 * PACKED * LANES,
+        "block_sums",
+    )(where, exchange(pair, BLOCK))
+    received = [ahead(chunk, step + 1) for step, chunk in enumerate(chunks)]
+    (mine,) = call(
+        layer_sums, "v" * layers, [(cut, BF16)], [], 2 * rows * LANES, "layer_sums"
+    )(kept, *received)
+    received = [ahead(mine, step) for step in range(1, layers)]
     (copies,) = call(
-        assemble, "v", [((count, 2 * rows, LANES), BF16)], [pltpu.VMEM((2 * rows, LANES), F32)],
+        assemble, "s" + "v" * layers, [((count, 2 * rows, LANES), BF16)], total,
         2 * PACKED * LANES, "assemble",
-    )(exchange(sums, LAYERS))
+    )(where, mine, *received)
     grads = call(unpack, "v", [((FLAT, C), F32)] * 2, [], 2 * PACKED * LANES, "unpack")(
         exchange(copies, BLOCK)
     )
@@ -554,7 +573,7 @@
 
 
 def local(latents, cotangent, bucket, timesteps, w_enc, w_dec, w_time):
-    where = jnp.stack([lax.axis_index(axis) for axis in ("near", "core")])
+    where = jnp.stack([lax.axis_index(axis) for axis in ("near", "core", LAYERS)])
     where = where.astype(jnp.int32)
     micro_count = latents.shape[0]
     loss_scale = float(micro_count * lax.axis_size(DP) * CELLS) ** (-0.5)
@@ -625,7 +644,7 @@
         be_hidden, be_cots,
     )
 
-    return gradients((own_enc, to_other_core(other_enc)), dec_pair)
+    return gradients(where, (own_enc, to_other_core(other_enc)), dec_pair)
 
 
 def solution(mesh):

time: 221 us -> 222 us (level); the launches traced: 221 us -> 219 us
  blocking collectives: 136 us -> 107 us
  starting transfers between devices: 7.19 us -> 24 us
  waiting for transfers between devices: 25.3 us -> 35.1 us
    all_to_all x4 -> x2, blocking collectives: 136 us -> 107 us  [exchange(): return lax.all_to_all(parts, axes, split_axis=0, concat_axis=0, tiled=True)]
    ppermute x0 -> x6, starting transfers between devices: none -> 16.8 us  [ahead(): lax.ppermute(value, LAYERS, [(at, (at + steps) % count) for at in range(c...]
    ppermute x0 -> x6, waiting for transfers between devices: none -> 9.77 us  [ahead(): lax.ppermute(value, LAYERS, [(at, (at + steps) % count) for at in range(c...]
  transfers between devices with their start and end apart: 9 -> 15, of which waited for: 5 -> 9; matrix products, arithmetic and copies ran while one was open for 0% -> 0% of each run, Pallas kernels for 6% -> 6%
where the time goes in v3:
time: 222 us; the launch traced here: 219 us
  blocking collectives  107 us (48%)
  Pallas kernels  46.2 us (21%)
  waiting for transfers between devices  35.1 us (16%)
  starting transfers between devices  24 us (11%)
  local copies, waits for them, and re-layouts  5.3 us (2%)
    all_to_all x2, blocking collectives, exchange(): return lax.all_to_all(parts, axes, split_axis=0, concat_axis=0, tiled=True)  107 us
    pallas_call x11, Pallas kernels, run(): pl.pallas_call(body, out_shape=tuple((shape(d, t) for d, t in outs)), in_...  46.2 us
    ppermute x6, starting transfers between devices, ahead(): lax.ppermute(value, LAYERS, [(at, (at + steps) % count) for at in range(c...  16.8 us
    ppermute x2, waiting for transfers between devices, up(): return lax.ppermute(value, 'near', [(0, 1)])  13.9 us
    ppermute x6, waiting for transfers between devices, ahead(): lax.ppermute(value, LAYERS, [(at, (at + steps) % count) for at in range(c...  9.77 us
    ppermute x5, waiting for transfers between devices, to_other_core(): return lax.ppermute(array, 'core', [(0, 1), (1, 0)])  7.38 us
    unnamed x22, local copies, waits for them, and re-layouts  5.3 us
  transfers between devices with their start and end apart: 15, of which 9 were waited for; matrix products, arithmetic and copies ran while one was open for 0% of the time, Pallas kernels for 6%

profile of v3, /device:TPU:2, one launch (start us, length us, event | category | flops | bytes accessed | tf_op | source)
XLA Modules:
  0.0 219.3 jit_solution(4333656362455017879)
XLA Ops:
  2.2 3.8 %collective-permute-done.1.time_other = bf16[2,320,320]{2,1,0:T(8,128)(2,1)S(1)} collective-permute-done((bf16[2,320,320]{2,1,0:T(8,128)(2,1)}, bf16[2,320,320]{2,1,0:T(8,128)(2,1)S(1)}, u32[]{:S(2)}, u32[]{:S(2)}) %collective-permute-start.1) | collective-permute-done | bytes 409632 | tf_op jit(solution)/shard_map/ppermute | solution.py:531
  6.1 1.6 copy-done
  7.7 1.0 copy-done.3
  8.8 0.9 copy-done.5
  9.7 1.0 copy-done.7
  11.4 5.4 %one.1 = (f32[2,256,320]{2,1,0:T(8,128)S(1)}, f32[2,8,320]{2,1,0:T(8,128)S(1)}, bf16[2,256,320]{2,1,0:T(8,128)(2,1)S(1)}, bf16[2,256,320]{2,1,0:T(8,128)(2,1)S(1)}, bf16[256,320]{1,0:T(8,128)(2,1)S(1)}) custom-call(s32[3]{0:T(128)S(1)} %pad_add_fusion.where, s32[2,2]{1,0:T(2,128)S(1)} %copy-done.9, bf16[2,256,320]{2,1,0:T(8,128)(2,1)S(1)} %bitcast.25, ...), custom_call_target="tpu_custom_call" | custom-call | flops 943718400 | bytes 6543388 | tf_op jit(solution)/shard_map/one/pallas_call | solution.py:504
  16.8 1.4 collective-permute-start.2
  18.2 7.8 %collective-permute-done.2.x = bf16[256,320]{1,0:T(8,128)(2,1)S(1)} collective-permute-done((bf16[256,320]{1,0:T(8,128)(2,1)S(1)}, bf16[256,320]{1,0:T(8,128)(2,1)S(1)}, u32[]{:S(2)}, u32[]{:S(2)}) %collective-permute-start.2) | collective-permute-done | bytes 163872 | tf_op jit(solution)/shard_map/ppermute | solution.py:594
  26.0 9.0 %two.1 = (f32[2,256,320]{2,1,0:T(8,128)S(1)}, f32[2,8,320]{2,1,0:T(8,128)S(1)}, bf16[2,256,320]{2,1,0:T(8,128)(2,1)S(1)}, f32[2,256,320]{2,1,0:T(8,128)S(1)}, f3...) custom-call(s32[3]{0:T(128)S(1)} %pad_add_fusion.where, ...), custom_call_target="tpu_custom_call" | custom-call | flops 1887436800 | bytes 10741788 | tf_op jit(solution)/shard_map/two/pallas_call | solution.py:504
  35.1 1.5 collective-permute-start.4
  36.5 4.0 %collective-permute-done.4.x = bf16[256,320]{1,0:T(8,128)(2,1)S(1)} collective-permute-done((bf16[256,320]{1,0:T(8,128)(2,1)S(1)}, bf16[256,320]{1,0:T(8,128)(2,1)S(1)}, u32[]{:S(2)}, u32[]{:S(2)}) %collective-permute-start.4) | collective-permute-done | bytes 163872 | tf_op jit(solution)/shard_map/ppermute | solution.py:597
  40.5 7.5 %three.1 = (bf16[2,256,320]{2,1,0:T(8,128)(2,1)S(1)}, bf16[2,256,320]{2,1,0:T(8,128)(2,1)S(1)}, bf16[2,256,320]{2,1,0:T(8,128)(2,1)S(1)}, bf16[256,320]{1,0:T(8,128)(2,1)S(1)}) custom-call(s32[3]{0:T(128)S(1)} %pad_add_fusion.where, s32[2,2]{1,0:T(2,128)S(1)} %copy-done.9, bf16[256,320]{1,0:T(8,128)(2,1)S(1)} %collective-permute-done.4.x, ...), custom_call_target="tpu_custom_call" | custom-call | flops 1415577600 | bytes 6686748 | tf_op jit(solution)/shard_map/three/pallas_call | solution.py:504
  48.0 1.5 collective-permute-start.5
  49.5 6.1 %collective-permute-done.5.x = bf16[256,320]{1,0:T(8,128)(2,1)S(1)} collective-permute-done((bf16[256,320]{1,0:T(8,128)(2,1)S(1)}, bf16[256,320]{1,0:T(8,128)(2,1)S(1)}, u32[]{:S(2)}, u32[]{:S(2)}) %collective-permute-start.5) | collective-permute-done | bytes 163872 | tf_op jit(solution)/shard_map/ppermute | solution.py:594
  55.6 8.7 %four.1 = (bf16[2,256,320]{2,1,0:T(8,128)(2,1)S(1)}, bf16[2,256,320]{2,1,0:T(8,128)(2,1)S(1)}, bf16[256,320]{1,0:T(8,128)(2,1)S(1)}) custom-call(s32[3]{0:T(128)S(1)} %pad_add_fusion.where, s32[2,2]{1,0:T(2,128)S(1)} %copy-done.10, bf16[256,320]{1,0:T(8,128)(2,1)S(1)} %collective-permute-done.5.x, bf16[2,320,320]{2,1,0:T(8,128)(2,1)S(1)} %bitcast.23, ...), custom_call_target="tpu_custom_call" | custom-call | flops 1887436800 | bytes 10741788 | tf_op jit(solution)/shard_map/four/pallas_call | solution.py:504
  64.3 1.5 collective-permute-start.6
  65.8 3.4 %weights.1 = (f32[7680,128]{1,0:T(8,128)S(1)}, bf16[7680,128]{1,0:T(8,128)(2,1)S(1)}) custom-call(s32[3]{0:T(128)S(1)} %pad_add_fusion.where, bf16[2,256,320]{2,1,0:T(8,128)(2,1)S(1)} %get-tuple-element.62.a_hidden, bf16[2,256,320]{2,1,0:T(8,128)(2,1)S(1)} %get-tuple-element.63.a_cots, bf16[2,256,320]{2,1,0:T(8,128)(2,1)S(1)} %get-tuple-element.64.b_hidden, ...), custom_call_target="tpu_custom_call" | custom-call | flops 943718400 | bytes 7208972 | tf_op jit(solution)/shard_map/weights/pallas_call | solution.py:504
  69.3 4.7 %five.1 = (f32[7680,128]{1,0:T(8,128)S(1)}, bf16[7680,128]{1,0:T(8,128)(2,1)S(1)}) custom-call(s32[3]{0:T(128)S(1)} %pad_add_fusion.where, s32[2,2]{1,0:T(2,128)S(1)} %copy-done.10, bf16[256,320]{1,0:T(8,128)(2,1)S(1)} %collective-permute-done.6.x, bf16[2,320,320]{2,1,0:T(8,128)(2,1)S(1)} %bitcast.24, ...), custom_call_target="tpu_custom_call" | custom-call | flops 1415577600 | bytes 12769308 | tf_op jit(solution)/shard_map/five/pallas_call | solution.py:504
  74.6 3.6 %collective-permute-done.7.first_other = bf16[7680,128]{1,0:T(8,128)(2,1)S(1)} collective-permute-done((bf16[7680,128]{1,0:T(8,128)(2,1)S(1)}, bf16[7680,128]{1,0:T(8,128)(2,1)S(1)}, u32[]{:S(2)}, u32[]{:S(2)}) %collective-permute-start.7) | collective-permute-done | bytes 1966112 | tf_op jit(solution)/shard_map/ppermute | solution.py:531
  79.0 57.0 %all_to_all.10.parts = bf16[16,960,128]{2,1,0:T(8,128)(2,1)S(1)} all-to-all(bf16[16,960,128]{2,1,0:T(8,128)(2,1)S(1)} %core_add.1), channel_id=1, replica_groups=mesh['near'=2,'core'=2,'z_high'=4,'z_low'=2,'far'=2,'y'=4] {'z_low','far..., dimensions={0} | all-to-all | bytes 7864320 | tf_op jit(solution)/shard_map/all_to_all | solution.py:540
  136.0 1.4 block_sums.1
  137.4 3.4 %collective-permute-start.9 = (bf16[2,120,128]{2,1,0:T(8,128)(2,1)S(1)}, bf16[2,120,128]{2,1,0:T(8,128)(2,1)S(1)}, u32[]{:S(2)}, u32[]{:S(2)}) collective-permute-start(bf16[2,120,128]{2,1,0:T(8,128)(2,1)S(1)} %get-tuple-element.69), channel_id=1, source_target_pairs={{0,16},{16,32},{32,48},{48,0},{1,17},{17,33},{33,49},{49,1},{2,18}... | collective-permute-start | bytes 184328 | tf_op jit(solution)/shard_map/ppermute | solution.py:545
  140.8 4.5 %collective-permute-start.10 = (bf16[2,120,128]{2,1,0:T(8,128)(2,1)S(1)}, bf16[2,120,128]{2,1,0:T(8,128)(2,1)S(1)}, u32[]{:S(2)}, u32[]{:S(2)}) collective-permute-start(bf16[2,120,128]{2,1,0:T(8,128)(2,1)S(1)} %get-tuple-element.70), channel_id=1, source_target_pairs={{0,32},{16,48},{32,0},{48,16},{1,33},{17,49},{33,1},{49,17},{2,34}... | collective-permute-start | bytes 184328 | tf_op jit(solution)/shard_map/ppermute | solution.py:545
  145.3 2.6 %collective-permute-start.11 = (bf16[2,120,128]{2,1,0:T(8,128)(2,1)S(1)}, bf16[2,120,128]{2,1,0:T(8,128)(2,1)S(1)}, u32[]{:S(2)}, u32[]{:S(2)}) collective-permute-start(bf16[2,120,128]{2,1,0:T(8,128)(2,1)S(1)} %get-tuple-element.71), channel_id=1, source_target_pairs={{0,48},{16,0},{32,16},{48,32},{1,49},{17,1},{33,17},{49,33},{2,50}... | collective-permute-start | bytes 184328 | tf_op jit(solution)/shard_map/ppermute | solution.py:545
  147.9 1.6 collective-permute-done.10.rest_1_
  149.5 1.8 collective-permute-done.11.rest_2_
  151.3 3.7 %collective-permute-start.14 = (bf16[2,120,128]{2,1,0:T(8,128)(2,1)S(1)}, bf16[2,120,128]{2,1,0:T(8,128)(2,1)S(1)}, u32[]{:S(2)}, u32[]{:S(2)}) collective-permute-start(bf16[2,120,128]{2,1,0:T(8,128)(2,1)S(1)} %layer_sums.1.rest_0_), channel_id=1, source_target_pairs={{0,48},{16,0},{32,16},{48,32},{1,49},{17,1},{33,17},{49,33},{2,50}... | collective-permute-start | bytes 184328 | tf_op jit(solution)/shard_map/ppermute | solution.py:545
  155.0 2.1 collective-permute-start.13
  157.7 6.0 %collective-permute-done.13.rest_2_ = bf16[2,120,128]{2,1,0:T(8,128)(2,1)S(1)} collective-permute-done((bf16[2,120,128]{2,1,0:T(8,128)(2,1)S(1)}, bf16[2,120,128]{2,1,0:T(8,128)(2,1)S(1)}, u32[]{:S(2)}, u32[]{:S(2)}) %collective-permute-start.13) | collective-permute-done | bytes 61472 | tf_op jit(solution)/shard_map/ppermute | solution.py:545
  164.0 0.9 assemble.1
  164.9 49.9 %all_to_all.11.packed = bf16[16,960,128]{2,1,0:T(8,128)(2,1)S(1)} all-to-all(bf16[16,960,128]{2,1,0:T(8,128)(2,1)S(1)} %assemble.1), channel_id=1, replica_groups=mesh['near'=2,'core'=2,'z_high'=4,'z_low'=2,'far'=2,'y'=4] {'z_low','far..., dimensions={0} | all-to-all | bytes 7864320 | tf_op jit(solution)/shard_map/all_to_all | solution.py:540
  214.9 4.4 %unpack.1 = (f32[2880,320]{1,0:T(8,128)}, f32[2880,320]{1,0:T(8,128)}) custom-call(bf16[16,960,128]{2,1,0:T(8,128)(2,1)S(1)} %all_to_all.11.packed), custom_call_target="tpu_custom_call" | custom-call | flops 1966080 | bytes 11304960 | tf_op jit(solution)/shard_map/unpack/pallas_call | solution.py:504
  (38 shorter events, 4.9 us)
Async XLA Ops:
  0.6 5.3 %collective-permute-start = (bf16[9,320,320]{2,1,0:T(8,128)(2,1)}, bf16[9,320,320]{2,1,0:T(8,128)(2,1)S(1)}, u32[]{:S(2)}, u32[]{:S(2)}) collective-permute-start(bf16[9,320,320]{2,1,0:T(8,128)(2,1)} %bitcast.10), channel_id=1, source_target_pairs={{0,64},{64,0},{1,65},{65,1},{2,66},{66,2},{3,67},{67,3},{4,68},{68... | collective-permute-start | bytes 5529608 | tf_op jit(solution)/shard_map/ppermute | solution.py:531
  0.7 5.2 %collective-permute-start.1 = (bf16[2,320,320]{2,1,0:T(8,128)(2,1)}, bf16[2,320,320]{2,1,0:T(8,128)(2,1)S(1)}, u32[]{:S(2)}, u32[]{:S(2)}) collective-permute-start(bf16[2,320,320]{2,1,0:T(8,128)(2,1)} %bitcast.19), channel_id=1, source_target_pairs={{0,64},{64,0},{1,65},{65,1},{2,66},{66,2},{3,67},{67,3},{4,68},{68... | collective-permute-start | bytes 1228808 | tf_op jit(solution)/shard_map/ppermute | solution.py:531
  6.0 20.1 %collective-permute-start.3 = (bf16[9,320,320]{2,1,0:T(8,128)(2,1)}, bf16[9,320,320]{2,1,0:T(8,128)(2,1)S(1)}, u32[]{:S(2)}, u32[]{:S(2)}) collective-permute-start(bf16[9,320,320]{2,1,0:T(8,128)(2,1)} %bitcast.15), channel_id=1, source_target_pairs={{0,64},{64,0},{1,65},{65,1},{2,66},{66,2},{3,67},{67,3},{4,68},{68... | collective-permute-start | bytes 5529608 | tf_op jit(solution)/shard_map/ppermute | solution.py:531
  6.1 1.6 copy-start
  7.7 1.0 copy-start.3
  8.8 0.9 copy-start.5
  9.7 1.0 copy-start.7
  10.7 0.7 copy-start.9
  11.4 14.7 %copy-start.1 = (bf16[1,3,3,320,320]{4,3,2,1,0:T(8,128)(2,1)S(1)}, bf16[1,3,3,320,320]{4,3,2,1,0:T(8,128)(2,1)}, u32[]{:S(2)}) copy-start(bf16[1,3,3,320,320]{4,3,2,1,0:T(8,128)(2,1)} %param.12) | copy-start | bytes 5529604
  11.4 14.7 %copy-start.2 = (bf16[1,3,3,320,320]{4,3,2,1,0:T(8,128)(2,1)S(1)}, bf16[1,3,3,320,320]{4,3,2,1,0:T(8,128)(2,1)}, u32[]{:S(2)}) copy-start(bf16[1,3,3,320,320]{4,3,2,1,0:T(8,128)(2,1)} %param.13) | copy-start | bytes 5529604
  11.4 14.7 %copy-start.6 = (bf16[320,320]{1,0:T(8,128)(2,1)S(1)}, bf16[320,320]{1,0:T(8,128)(2,1)}, u32[]{:S(2)}) copy-start(bf16[320,320]{1,0:T(8,128)(2,1)} %constant.26.clone.matrix) | copy-start | bytes 614404
  16.8 23.7 %copy-start.8 = (bf16[2,16,16,320]{3,2,1,0:T(8,128)(2,1)S(1)}, bf16[2,16,16,320]{3,2,1,0:T(8,128)(2,1)}, u32[]{:S(2)}) copy-start(bf16[2,16,16,320]{3,2,1,0:T(8,128)(2,1)} %param.9) | copy-start | bytes 983044
  16.8 9.2 %collective-permute-start.2 = (bf16[256,320]{1,0:T(8,128)(2,1)S(1)}, bf16[256,320]{1,0:T(8,128)(2,1)S(1)}, u32[]{:S(2)}, u32[]{:S(2)}) collective-permute-start(bf16[256,320]{1,0:T(8,128)(2,1)S(1)} %get-tuple-element.44), channel_id=1, source_target_pairs={{0,128},{1,129},{2,130},{3,131},{4,132},{5,133},{6,134},{7,135},{8... | collective-permute-start | bytes 491528 | tf_op jit(solution)/shard_map/ppermute | solution.py:594
  35.1 20.6 %copy-start.10 = (s32[2,2]{1,0:T(2,128)S(1)}, s32[2,2]{1,0:T(2,128)}, u32[]{:S(2)}) copy-start(s32[2,2]{1,0:T(2,128)} %bucket.9) | copy-start | bytes 52
  35.1 5.4 %collective-permute-start.4 = (bf16[256,320]{1,0:T(8,128)(2,1)S(1)}, bf16[256,320]{1,0:T(8,128)(2,1)S(1)}, u32[]{:S(2)}, u32[]{:S(2)}) collective-permute-start(bf16[256,320]{1,0:T(8,128)(2,1)S(1)} %get-tuple-element.46), channel_id=1, source_target_pairs={{128,0},{129,1},{130,2},{131,3},{132,4},{133,5},{134,6},{135,7},{1... | collective-permute-start | bytes 491528 | tf_op jit(solution)/shard_map/ppermute | solution.py:597
  48.0 7.6 %collective-permute-start.5 = (bf16[256,320]{1,0:T(8,128)(2,1)S(1)}, bf16[256,320]{1,0:T(8,128)(2,1)S(1)}, u32[]{:S(2)}, u32[]{:S(2)}) collective-permute-start(bf16[256,320]{1,0:T(8,128)(2,1)S(1)} %get-tuple-element.48), channel_id=1, source_target_pairs={{0,128},{1,129},{2,130},{3,131},{4,132},{5,133},{6,134},{7,135},{8... | collective-permute-start | bytes 491528 | tf_op jit(solution)/shard_map/ppermute | solution.py:594
  55.6 13.7 %copy-start.4 = (bf16[1,2,320,320]{3,2,1,0:T(8,128)(2,1)S(1)}, bf16[1,2,320,320]{3,2,1,0:T(8,128)(2,1)}, u32[]{:S(2)}) copy-start(bf16[1,2,320,320]{3,2,1,0:T(8,128)(2,1)} %param.14) | copy-start | bytes 1228804
  64.3 5.0 %collective-permute-start.6 = (bf16[256,320]{1,0:T(8,128)(2,1)S(1)}, bf16[256,320]{1,0:T(8,128)(2,1)S(1)}, u32[]{:S(2)}, u32[]{:S(2)}) collective-permute-start(bf16[256,320]{1,0:T(8,128)(2,1)S(1)} %get-tuple-element.53), channel_id=1, source_target_pairs={{128,0},{129,1},{130,2},{131,3},{132,4},{133,5},{134,6},{135,7},{1... | collective-permute-start | bytes 491528 | tf_op jit(solution)/shard_map/ppermute | solution.py:597
  69.2 5.4 %collective-permute-start.8 = (bf16[7680,128]{1,0:T(8,128)(2,1)S(1)}, bf16[7680,128]{1,0:T(8,128)(2,1)S(1)}, u32[]{:S(2)}, u32[]{:S(2)}) collective-permute-start(bf16[7680,128]{1,0:T(8,128)(2,1)S(1)} %get-tuple-element.67), channel_id=1, source_target_pairs={{0,64},{64,0},{1,65},{65,1},{2,66},{66,2},{3,67},{67,3},{4,68},{68... | collective-permute-start | bytes 5898248 | tf_op jit(solution)/shard_map/ppermute | solution.py:531
  74.1 4.2 %collective-permute-start.7 = (bf16[7680,128]{1,0:T(8,128)(2,1)S(1)}, bf16[7680,128]{1,0:T(8,128)(2,1)S(1)}, u32[]{:S(2)}, u32[]{:S(2)}) collective-permute-start(bf16[7680,128]{1,0:T(8,128)(2,1)S(1)} %get-tuple-element.61), channel_id=1, source_target_pairs={{0,64},{64,0},{1,65},{65,1},{2,66},{66,2},{3,67},{67,3},{4,68},{68... | collective-permute-start | bytes 5898248 | tf_op jit(solution)/shard_map/ppermute | solution.py:531
  137.4 10.5 %collective-permute-start.9 = (bf16[2,120,128]{2,1,0:T(8,128)(2,1)S(1)}, bf16[2,120,128]{2,1,0:T(8,128)(2,1)S(1)}, u32[]{:S(2)}, u32[]{:S(2)}) collective-permute-start(bf16[2,120,128]{2,1,0:T(8,128)(2,1)S(1)} %get-tuple-element.69), channel_id=1, source_target_pairs={{0,16},{16,32},{32,48},{48,0},{1,17},{17,33},{33,49},{49,1},{2,18}... | collective-permute-start | bytes 184328 | tf_op jit(solution)/shard_map/ppermute | solution.py:545
  140.8 8.8 %collective-permute-start.10 = (bf16[2,120,128]{2,1,0:T(8,128)(2,1)S(1)}, bf16[2,120,128]{2,1,0:T(8,128)(2,1)S(1)}, u32[]{:S(2)}, u32[]{:S(2)}) collective-permute-start(bf16[2,120,128]{2,1,0:T(8,128)(2,1)S(1)} %get-tuple-element.70), channel_id=1, source_target_pairs={{0,32},{16,48},{32,0},{48,16},{1,33},{17,49},{33,1},{49,17},{2,34}... | collective-permute-start | bytes 184328 | tf_op jit(solution)/shard_map/ppermute | solution.py:545
  145.3 6.0 %collective-permute-start.11 = (bf16[2,120,128]{2,1,0:T(8,128)(2,1)S(1)}, bf16[2,120,128]{2,1,0:T(8,128)(2,1)S(1)}, u32[]{:S(2)}, u32[]{:S(2)}) collective-permute-start(bf16[2,120,128]{2,1,0:T(8,128)(2,1)S(1)} %get-tuple-element.71), channel_id=1, source_target_pairs={{0,48},{16,0},{32,16},{48,32},{1,49},{17,1},{33,17},{49,33},{2,50}... | collective-permute-start | bytes 184328 | tf_op jit(solution)/shard_map/ppermute | solution.py:545
  151.3 6.4 %collective-permute-start.14 = (bf16[2,120,128]{2,1,0:T(8,128)(2,1)S(1)}, bf16[2,120,128]{2,1,0:T(8,128)(2,1)S(1)}, u32[]{:S(2)}, u32[]{:S(2)}) collective-permute-start(bf16[2,120,128]{2,1,0:T(8,128)(2,1)S(1)} %layer_sums.1.rest_0_), channel_id=1, source_target_pairs={{0,48},{16,0},{32,16},{48,32},{1,49},{17,1},{33,17},{49,33},{2,50}... | collective-permute-start | bytes 184328 | tf_op jit(solution)/shard_map/ppermute | solution.py:545
  155.0 8.6 %collective-permute-start.13 = (bf16[2,120,128]{2,1,0:T(8,128)(2,1)S(1)}, bf16[2,120,128]{2,1,0:T(8,128)(2,1)S(1)}, u32[]{:S(2)}, u32[]{:S(2)}) collective-permute-start(bf16[2,120,128]{2,1,0:T(8,128)(2,1)S(1)} %layer_sums.1.rest_0_), channel_id=1, source_target_pairs={{0,32},{16,48},{32,0},{48,16},{1,33},{17,49},{33,1},{49,17},{2,34}... | collective-permute-start | bytes 184328 | tf_op jit(solution)/shard_map/ppermute | solution.py:545
  157.1 7.0 %collective-permute-start.12 = (bf16[2,120,128]{2,1,0:T(8,128)(2,1)S(1)}, bf16[2,120,128]{2,1,0:T(8,128)(2,1)S(1)}, u32[]{:S(2)}, u32[]{:S(2)}) collective-permute-start(bf16[2,120,128]{2,1,0:T(8,128)(2,1)S(1)} %layer_sums.1.rest_0_), channel_id=1, source_target_pairs={{0,16},{16,32},{32,48},{48,0},{1,17},{17,33},{33,49},{49,1},{2,18}... | collective-permute-start | bytes 184328 | tf_op jit(solution)/shard_map/ppermute | solution.py:545

commit v4 on v2

--- a/solution.py
+++ b/solution.py
@@ -521,9 +521,9 @@
     return lax.ppermute(array, "core", [(0, 1), (1, 0)])
 
 
-BLOCK = ("z_low", "far", "y")
-LAYERS = "z_high"
-DP = (LAYERS, *BLOCK)
+BLOCK = ("z_low", "y")
+LAYERS = ("z_high", "far")
+DP = ("z_high", "z_low", "far", "y")
 
 
 def exchange(parts, axes):

time: 221 us -> 232 us (1.050)
  blocking collectives: 136 us -> 146 us
    all_to_all x4, blocking collectives: 136 us -> 146 us  [exchange(): return lax.all_to_all(parts, axes, split_axis=0, concat_axis=0, tiled=True)]
where the time goes in v4:
time: 232 us; the launch traced here: 230 us
  blocking collectives  146 us (63%)
  Pallas kernels  44.6 us (19%)
  waiting for transfers between devices  25.3 us (11%)
  starting transfers between devices  7.19 us (3%)
  local copies, waits for them, and re-layouts  5.29 us (2%)
    all_to_all x4, blocking collectives, exchange(): return lax.all_to_all(parts, axes, split_axis=0, concat_axis=0, tiled=True)  146 us
    pallas_call x11, Pallas kernels, run(): pl.pallas_call(body, out_shape=tuple((shape(d, t) for d, t in outs)), in_...  44.6 us
    ppermute x2, waiting for transfers between devices, up(): return lax.ppermute(value, 'near', [(0, 1)])  13.9 us
    ppermute x5, waiting for transfers between devices, to_other_core(): return lax.ppermute(array, 'core', [(0, 1), (1, 0)])  7.38 us
    unnamed x22, local copies, waits for them, and re-layouts  5.29 us
  transfers between devices with their start and end apart: 9, of which 5 were waited for; matrix products, arithmetic and copies ran while one was open for 0% of the time, Pallas kernels for 6%

profile of v4, /device:TPU:2, one launch (start us, length us, event | category | flops | bytes accessed | tf_op | source)
XLA Modules:
  0.0 230.2 jit_solution(14860631087911900721)
XLA Ops:
  0.7 0.5 collective-permute-start.1
  1.2 0.7 convert_element_type.6
  2.2 3.8 %collective-permute-done.1.time_other = bf16[2,320,320]{2,1,0:T(8,128)(2,1)S(1)} collective-permute-done((bf16[2,320,320]{2,1,0:T(8,128)(2,1)}, bf16[2,320,320]{2,1,0:T(8,128)(2,1)S(1)}, u32[]{:S(2)}, u32[]{:S(2)}) %collective-permute-start.1) | collective-permute-done | bytes 409632 | tf_op jit(solution)/shard_map/ppermute | solution.py:521
  6.0 0.1 collective-permute-start.3
  6.1 1.6 copy-done
  7.7 1.0 copy-done.3
  8.8 0.9 copy-done.5
  9.7 1.0 copy-done.7
  10.7 0.7 copy-done.9
  11.4 5.4 %one.1 = (f32[2,256,320]{2,1,0:T(8,128)S(1)}, f32[2,8,320]{2,1,0:T(8,128)S(1)}, bf16[2,256,320]{2,1,0:T(8,128)(2,1)S(1)}, bf16[2,256,320]{2,1,0:T(8,128)(2,1)S(1)}, bf16[256,320]{1,0:T(8,128)(2,1)S(1)}) custom-call(s32[2]{0:T(128)S(1)} %pad_add_fusion.where, s32[2,2]{1,0:T(2,128)S(1)} %copy-done.9, bf16[2,256,320]{2,1,0:T(8,128)(2,1)S(1)} %bitcast.24, ...), custom_call_target="tpu_custom_call" | custom-call | flops 943718400 | bytes 6543384 | tf_op jit(solution)/shard_map/one/pallas_call | solution.py:494
  16.8 1.4 collective-permute-start.2
  18.2 7.8 %collective-permute-done.2.x = bf16[256,320]{1,0:T(8,128)(2,1)S(1)} collective-permute-done((bf16[256,320]{1,0:T(8,128)(2,1)S(1)}, bf16[256,320]{1,0:T(8,128)(2,1)S(1)}, u32[]{:S(2)}, u32[]{:S(2)}) %collective-permute-start.2) | collective-permute-done | bytes 163872 | tf_op jit(solution)/shard_map/ppermute | solution.py:575
  26.0 9.0 %two.1 = (f32[2,256,320]{2,1,0:T(8,128)S(1)}, f32[2,8,320]{2,1,0:T(8,128)S(1)}, bf16[2,256,320]{2,1,0:T(8,128)(2,1)S(1)}, f32[2,256,320]{2,1,0:T(8,128)S(1)}, f3...) custom-call(s32[2]{0:T(128)S(1)} %pad_add_fusion.where, ...), custom_call_target="tpu_custom_call" | custom-call | flops 1887436800 | bytes 10741784 | tf_op jit(solution)/shard_map/two/pallas_call | solution.py:494
  35.1 1.5 collective-permute-start.4
  36.5 4.0 %collective-permute-done.4.x = bf16[256,320]{1,0:T(8,128)(2,1)S(1)} collective-permute-done((bf16[256,320]{1,0:T(8,128)(2,1)S(1)}, bf16[256,320]{1,0:T(8,128)(2,1)S(1)}, u32[]{:S(2)}, u32[]{:S(2)}) %collective-permute-start.4) | collective-permute-done | bytes 163872 | tf_op jit(solution)/shard_map/ppermute | solution.py:578
  40.5 7.5 %three.1 = (bf16[2,256,320]{2,1,0:T(8,128)(2,1)S(1)}, bf16[2,256,320]{2,1,0:T(8,128)(2,1)S(1)}, bf16[2,256,320]{2,1,0:T(8,128)(2,1)S(1)}, bf16[256,320]{1,0:T(8,128)(2,1)S(1)}) custom-call(s32[2]{0:T(128)S(1)} %pad_add_fusion.where, s32[2,2]{1,0:T(2,128)S(1)} %copy-done.9, bf16[256,320]{1,0:T(8,128)(2,1)S(1)} %collective-permute-done.4.x, ...), custom_call_target="tpu_custom_call" | custom-call | flops 1415577600 | bytes 6686744 | tf_op jit(solution)/shard_map/three/pallas_call | solution.py:494
  48.0 1.5 collective-permute-start.5
  49.5 6.1 %collective-permute-done.5.x = bf16[256,320]{1,0:T(8,128)(2,1)S(1)} collective-permute-done((bf16[256,320]{1,0:T(8,128)(2,1)S(1)}, bf16[256,320]{1,0:T(8,128)(2,1)S(1)}, u32[]{:S(2)}, u32[]{:S(2)}) %collective-permute-start.5) | collective-permute-done | bytes 163872 | tf_op jit(solution)/shard_map/ppermute | solution.py:575
  55.6 8.7 %four.1 = (bf16[2,256,320]{2,1,0:T(8,128)(2,1)S(1)}, bf16[2,256,320]{2,1,0:T(8,128)(2,1)S(1)}, bf16[256,320]{1,0:T(8,128)(2,1)S(1)}) custom-call(s32[2]{0:T(128)S(1)} %pad_add_fusion.where, s32[2,2]{1,0:T(2,128)S(1)} %copy-done.9, bf16[256,320]{1,0:T(8,128)(2,1)S(1)} %collective-permute-done.5.x, bf16[2,320,320]{2,1,0:T(8,128)(2,1)S(1)} %bitcast.22, ...), custom_call_target="tpu_custom_call" | custom-call | flops 1887436800 | bytes 10741784 | tf_op jit(solution)/shard_map/four/pallas_call | solution.py:494
  64.3 1.5 collective-permute-start.6
  65.8 3.4 %weights.1 = (f32[7680,128]{1,0:T(8,128)S(1)}, bf16[7680,128]{1,0:T(8,128)(2,1)S(1)}) custom-call(s32[2]{0:T(128)S(1)} %pad_add_fusion.where, bf16[2,256,320]{2,1,0:T(8,128)(2,1)S(1)} %get-tuple-element.58.a_hidden, bf16[2,256,320]{2,1,0:T(8,128)(2,1)S(1)} %get-tuple-element.59.a_cots, bf16[2,256,320]{2,1,0:T(8,128)(2,1)S(1)} %get-tuple-element.60.b_hidden, ...), custom_call_target="tpu_custom_call" | custom-call | flops 943718400 | bytes 7208968 | tf_op jit(solution)/shard_map/weights/pallas_call | solution.py:494
  69.3 4.7 %five.1 = (f32[7680,128]{1,0:T(8,128)S(1)}, bf16[7680,128]{1,0:T(8,128)(2,1)S(1)}) custom-call(s32[2]{0:T(128)S(1)} %pad_add_fusion.where, s32[2,2]{1,0:T(2,128)S(1)} %copy-done.10, bf16[256,320]{1,0:T(8,128)(2,1)S(1)} %collective-permute-done.6.x, bf16[2,320,320]{2,1,0:T(8,128)(2,1)S(1)} %bitcast.23, ...), custom_call_target="tpu_custom_call" | custom-call | flops 1415577600 | bytes 12769304 | tf_op jit(solution)/shard_map/five/pallas_call | solution.py:494
  74.1 0.6 collective-permute-start.7
  74.6 3.6 %collective-permute-done.7.first_other = bf16[7680,128]{1,0:T(8,128)(2,1)S(1)} collective-permute-done((bf16[7680,128]{1,0:T(8,128)(2,1)S(1)}, bf16[7680,128]{1,0:T(8,128)(2,1)S(1)}, u32[]{:S(2)}, u32[]{:S(2)}) %collective-permute-start.7) | collective-permute-done | bytes 1966112 | tf_op jit(solution)/shard_map/ppermute | solution.py:521
  78.2 0.7 core_add.1
  78.9 52.6 %all_to_all.20.parts = bf16[8,1920,128]{2,1,0:T(8,128)(2,1)S(1)} all-to-all(bf16[8,1920,128]{2,1,0:T(8,128)(2,1)S(1)} %core_add.1), channel_id=1, replica_groups=mesh['near'=2,'core'=2,'z_high'=4,'z_low'=2,'far'=2,'y'=4] {'z_low','y'}, dimensions={0} | all-to-all | bytes 7864320 | tf_op jit(solution)/shard_map/all_to_all | solution.py:530
  131.5 0.5 block_sums.1
  132.0 23.3 %all_to_all.21.parts = bf16[8,2,120,128]{3,2,1,0:T(8,128)(2,1)S(1)} all-to-all(bf16[8,2,120,128]{3,2,1,0:T(8,128)(2,1)S(1)} %block_sums.1), channel_id=1, replica_groups=mesh['near'=2,'core'=2,'z_high'=4,'z_low'=2,'far'=2,'y'=4] {'z_high','far'}, dimensions={0} | all-to-all | bytes 983040 | tf_op jit(solution)/shard_map/all_to_all | solution.py:530
  155.4 19.6 %all_to_all.22.parts = bf16[8,2,120,128]{3,2,1,0:T(8,128)(2,1)S(1)} all-to-all(bf16[8,2,120,128]{3,2,1,0:T(8,128)(2,1)S(1)} %layer_sums.1), channel_id=1, replica_groups=mesh['near'=2,'core'=2,'z_high'=4,'z_low'=2,'far'=2,'y'=4] {'z_high','far'}, dimensions={0} | all-to-all | bytes 983040 | tf_op jit(solution)/shard_map/all_to_all | solution.py:530
  175.1 0.3 assemble.1
  175.3 50.5 %all_to_all.23.packed = bf16[8,1920,128]{2,1,0:T(8,128)(2,1)S(1)} all-to-all(bf16[8,1920,128]{2,1,0:T(8,128)(2,1)S(1)} %assemble.1), channel_id=1, replica_groups=mesh['near'=2,'core'=2,'z_high'=4,'z_low'=2,'far'=2,'y'=4] {'z_low','y'}, dimensions={0} | all-to-all | bytes 7864320 | tf_op jit(solution)/shard_map/all_to_all | solution.py:530
  225.8 4.4 %unpack.1 = (f32[2880,320]{1,0:T(8,128)}, f32[2880,320]{1,0:T(8,128)}) custom-call(bf16[8,1920,128]{2,1,0:T(8,128)(2,1)S(1)} %all_to_all.23.packed), custom_call_target="tpu_custom_call" | custom-call | flops 1966080 | bytes 11304960 | tf_op jit(solution)/shard_map/unpack/pallas_call | solution.py:494
  (28 shorter events, 0.6 us)
Async XLA Ops:
  0.6 5.3 %collective-permute-start = (bf16[9,320,320]{2,1,0:T(8,128)(2,1)}, bf16[9,320,320]{2,1,0:T(8,128)(2,1)S(1)}, u32[]{:S(2)}, u32[]{:S(2)}) collective-permute-start(bf16[9,320,320]{2,1,0:T(8,128)(2,1)} %bitcast.9), channel_id=1, source_target_pairs={{0,64},{64,0},{1,65},{65,1},{2,66},{66,2},{3,67},{67,3},{4,68},{68... | collective-permute-start | bytes 5529608 | tf_op jit(solution)/shard_map/ppermute | solution.py:521
  0.7 5.2 %collective-permute-start.1 = (bf16[2,320,320]{2,1,0:T(8,128)(2,1)}, bf16[2,320,320]{2,1,0:T(8,128)(2,1)S(1)}, u32[]{:S(2)}, u32[]{:S(2)}) collective-permute-start(bf16[2,320,320]{2,1,0:T(8,128)(2,1)} %bitcast.18), channel_id=1, source_target_pairs={{0,64},{64,0},{1,65},{65,1},{2,66},{66,2},{3,67},{67,3},{4,68},{68... | collective-permute-start | bytes 1228808 | tf_op jit(solution)/shard_map/ppermute | solution.py:521
  6.0 20.1 %collective-permute-start.3 = (bf16[9,320,320]{2,1,0:T(8,128)(2,1)}, bf16[9,320,320]{2,1,0:T(8,128)(2,1)S(1)}, u32[]{:S(2)}, u32[]{:S(2)}) collective-permute-start(bf16[9,320,320]{2,1,0:T(8,128)(2,1)} %bitcast.14), channel_id=1, source_target_pairs={{0,64},{64,0},{1,65},{65,1},{2,66},{66,2},{3,67},{67,3},{4,68},{68... | collective-permute-start | bytes 5529608 | tf_op jit(solution)/shard_map/ppermute | solution.py:521
  6.1 1.6 copy-start
  7.7 1.0 copy-start.3
  8.8 0.9 copy-start.5
  9.7 1.0 copy-start.7
  10.7 0.7 copy-start.9
  11.4 14.7 %copy-start.1 = (bf16[1,3,3,320,320]{4,3,2,1,0:T(8,128)(2,1)S(1)}, bf16[1,3,3,320,320]{4,3,2,1,0:T(8,128)(2,1)}, u32[]{:S(2)}) copy-start(bf16[1,3,3,320,320]{4,3,2,1,0:T(8,128)(2,1)} %param.12) | copy-start | bytes 5529604
  11.4 14.7 %copy-start.2 = (bf16[1,3,3,320,320]{4,3,2,1,0:T(8,128)(2,1)S(1)}, bf16[1,3,3,320,320]{4,3,2,1,0:T(8,128)(2,1)}, u32[]{:S(2)}) copy-start(bf16[1,3,3,320,320]{4,3,2,1,0:T(8,128)(2,1)} %param.13) | copy-start | bytes 5529604
  11.4 14.7 %copy-start.6 = (bf16[320,320]{1,0:T(8,128)(2,1)S(1)}, bf16[320,320]{1,0:T(8,128)(2,1)}, u32[]{:S(2)}) copy-start(bf16[320,320]{1,0:T(8,128)(2,1)} %constant.20.clone.matrix) | copy-start | bytes 614404
  16.8 23.7 %copy-start.8 = (bf16[2,16,16,320]{3,2,1,0:T(8,128)(2,1)S(1)}, bf16[2,16,16,320]{3,2,1,0:T(8,128)(2,1)}, u32[]{:S(2)}) copy-start(bf16[2,16,16,320]{3,2,1,0:T(8,128)(2,1)} %param.9) | copy-start | bytes 983044
  16.8 9.2 %collective-permute-start.2 = (bf16[256,320]{1,0:T(8,128)(2,1)S(1)}, bf16[256,320]{1,0:T(8,128)(2,1)S(1)}, u32[]{:S(2)}, u32[]{:S(2)}) collective-permute-start(bf16[256,320]{1,0:T(8,128)(2,1)S(1)} %get-tuple-element.40), channel_id=1, source_target_pairs={{0,128},{1,129},{2,130},{3,131},{4,132},{5,133},{6,134},{7,135},{8... | collective-permute-start | bytes 491528 | tf_op jit(solution)/shard_map/ppermute | solution.py:575
  35.1 5.4 %collective-permute-start.4 = (bf16[256,320]{1,0:T(8,128)(2,1)S(1)}, bf16[256,320]{1,0:T(8,128)(2,1)S(1)}, u32[]{:S(2)}, u32[]{:S(2)}) collective-permute-start(bf16[256,320]{1,0:T(8,128)(2,1)S(1)} %get-tuple-element.42), channel_id=1, source_target_pairs={{128,0},{129,1},{130,2},{131,3},{132,4},{133,5},{134,6},{135,7},{1... | collective-permute-start | bytes 491528 | tf_op jit(solution)/shard_map/ppermute | solution.py:578
  48.0 7.6 %collective-permute-start.5 = (bf16[256,320]{1,0:T(8,128)(2,1)S(1)}, bf16[256,320]{1,0:T(8,128)(2,1)S(1)}, u32[]{:S(2)}, u32[]{:S(2)}) collective-permute-start(bf16[256,320]{1,0:T(8,128)(2,1)S(1)} %get-tuple-element.44), channel_id=1, source_target_pairs={{0,128},{1,129},{2,130},{3,131},{4,132},{5,133},{6,134},{7,135},{8... | collective-permute-start | bytes 491528 | tf_op jit(solution)/shard_map/ppermute | solution.py:575
  55.6 13.7 %copy-start.4 = (bf16[1,2,320,320]{3,2,1,0:T(8,128)(2,1)S(1)}, bf16[1,2,320,320]{3,2,1,0:T(8,128)(2,1)}, u32[]{:S(2)}) copy-start(bf16[1,2,320,320]{3,2,1,0:T(8,128)(2,1)} %param.14) | copy-start | bytes 1228804
  55.6 13.7 %copy-start.10 = (s32[2,2]{1,0:T(2,128)S(1)}, s32[2,2]{1,0:T(2,128)}, u32[]{:S(2)}) copy-start(s32[2,2]{1,0:T(2,128)} %bucket.9) | copy-start | bytes 52
  64.3 5.0 %collective-permute-start.6 = (bf16[256,320]{1,0:T(8,128)(2,1)S(1)}, bf16[256,320]{1,0:T(8,128)(2,1)S(1)}, u32[]{:S(2)}, u32[]{:S(2)}) collective-permute-start(bf16[256,320]{1,0:T(8,128)(2,1)S(1)} %get-tuple-element.49), channel_id=1, source_target_pairs={{128,0},{129,1},{130,2},{131,3},{132,4},{133,5},{134,6},{135,7},{1... | collective-permute-start | bytes 491528 | tf_op jit(solution)/shard_map/ppermute | solution.py:578
  69.2 5.4 %collective-permute-start.8 = (bf16[7680,128]{1,0:T(8,128)(2,1)S(1)}, bf16[7680,128]{1,0:T(8,128)(2,1)S(1)}, u32[]{:S(2)}, u32[]{:S(2)}) collective-permute-start(bf16[7680,128]{1,0:T(8,128)(2,1)S(1)} %get-tuple-element.63), channel_id=1, source_target_pairs={{0,64},{64,0},{1,65},{65,1},{2,66},{66,2},{3,67},{67,3},{4,68},{68... | collective-permute-start | bytes 5898248 | tf_op jit(solution)/shard_map/ppermute | solution.py:521
  74.1 4.2 %collective-permute-start.7 = (bf16[7680,128]{1,0:T(8,128)(2,1)S(1)}, bf16[7680,128]{1,0:T(8,128)(2,1)S(1)}, u32[]{:S(2)}, u32[]{:S(2)}) collective-permute-start(bf16[7680,128]{1,0:T(8,128)(2,1)S(1)} %get-tuple-element.57), channel_id=1, source_target_pairs={{0,64},{64,0},{1,65},{65,1},{2,66},{66,2},{3,67},{67,3},{4,68},{68... | collective-permute-start | bytes 5898248 | tf_op jit(solution)/shard_map/ppermute | solution.py:521

commit v5 on v3

--- a/solution.py
+++ b/solution.py
@@ -458,23 +458,19 @@
     size = 2 * STRIP
     half = FLAT // 2
 
-    def strip(step, carry):
-        for which, grad in enumerate((first, second)):
-
-            def source(begin, which=which):
-                begin = begin + step * size
-                at = pl.multiple_of(which * rows + lax.rem(begin, rows), 16)
-                return packed[lax.div(begin, rows), pl.ds(at, size), :].astype(F32)
-
-            tail = source(2 * FLAT)
-            for side in range(2):
-                to = pl.ds(pl.multiple_of(step * size + side * half, 16), size)
-                grad[to, 0:LANES] = source(side * half)
-                grad[to, LANES : 2 * LANES] = source(FLAT + side * half)
-                grad[to, 2 * LANES : C] = tail[:, side * TAIL : (side + 1) * TAIL]
-        return carry
-
-    lax.fori_loop(0, half // size, strip, 0)
+    step = pl.program_id(0)
+    for which, grad in enumerate((first, second)):
+
+        def source(begin, which=which):
+            begin = begin + step * size
+            at = pl.multiple_of(which * rows + lax.rem(begin, rows), 16)
+            return packed[lax.div(begin, rows), pl.ds(at, size), :].astype(F32)
+
+        tail = source(2 * FLAT)
+        for side in range(2):
+            grad[side, :, 0:LANES] = source(side * half)
+            grad[side, :, LANES : 2 * LANES] = source(FLAT + side * half)
+            grad[side, :, 2 * LANES : C] = tail[:, side * TAIL : (side + 1) * TAIL]
 
 
 def shape(dims, dtype):
@@ -566,9 +562,18 @@
         assemble, "s" + "v" * layers, [((count, 2 * rows, LANES), BF16)], total,
         2 * PACKED * LANES, "assemble",
     )(where, mine, *received)
-    grads = call(unpack, "v", [((FLAT, C), F32)] * 2, [], 2 * PACKED * LANES, "unpack")(
-        exchange(copies, BLOCK)
-    )
+    packed = exchange(copies, BLOCK)
+    half = FLAT // 2
+    strip = pl.BlockSpec((2, 2 * STRIP, C), lambda step: (0, step, 0))
+    grads = pl.pallas_call(
+        unpack,
+        out_shape=(shape((2, half, C), F32),) * 2,
+        grid=(half // (2 * STRIP),),
+        in_specs=[pl.BlockSpec(packed.shape, lambda step: (0, 0, 0))],
+        out_specs=(strip, strip),
+        compiler_params=pltpu.CompilerParams(vmem_limit_bytes=VMEM_LIMIT),
+        name="unpack",
+    )(packed)
     return tuple(grad.reshape(1, 3, 3, C, C) for grad in grads)
 
 

time: 222 us -> 221 us (level)
    pallas_call x11 -> x10, Pallas kernels: 46.2 us -> 41.8 us  [run(): pl.pallas_call(body, out_shape=tuple((shape(d, t) for d, t in outs)), in_...]
    pallas_call x0 -> x1, Pallas kernels: none -> 3.73 us  [gradients(): pl.pallas_call(unpack, out_shape=(shape((2, half, C), F32),) * 2, grid=(h...]
where the time goes in v5:
time: 221 us; the launch traced here: 219 us
  blocking collectives  107 us (48%)
  Pallas kernels  45.5 us (21%)
  waiting for transfers between devices  35.1 us (16%)
  starting transfers between devices  24 us (11%)
  local copies, waits for them, and re-layouts  5.3 us (2%)
    all_to_all x2, blocking collectives, exchange(): return lax.all_to_all(parts, axes, split_axis=0, concat_axis=0, tiled=True)  107 us
    pallas_call x10, Pallas kernels, run(): pl.pallas_call(body, out_shape=tuple((shape(d, t) for d, t in outs)), in_...  41.8 us
    ppermute x6, starting transfers between devices, ahead(): lax.ppermute(value, LAYERS, [(at, (at + steps) % count) for at in range(c...  16.8 us
    ppermute x2, waiting for transfers between devices, up(): return lax.ppermute(value, 'near', [(0, 1)])  13.9 us
    ppermute x6, waiting for transfers between devices, ahead(): lax.ppermute(value, LAYERS, [(at, (at + steps) % count) for at in range(c...  9.77 us
    ppermute x5, waiting for transfers between devices, to_other_core(): return lax.ppermute(array, 'core', [(0, 1), (1, 0)])  7.38 us
    unnamed x22, local copies, waits for them, and re-layouts  5.3 us
  transfers between devices with their start and end apart: 15, of which 9 were waited for; matrix products, arithmetic and copies ran while one was open for 0% of the time, Pallas kernels for 6%

profile of v5, /device:TPU:2, one launch (start us, length us, event | category | flops | bytes accessed | tf_op | source)
XLA Modules:
  0.0 218.6 jit_solution(5637883376374096295)
XLA Ops:
  2.2 3.8 %collective-permute-done.1.time_other = bf16[2,320,320]{2,1,0:T(8,128)(2,1)S(1)} collective-permute-done((bf16[2,320,320]{2,1,0:T(8,128)(2,1)}, bf16[2,320,320]{2,1,0:T(8,128)(2,1)S(1)}, u32[]{:S(2)}, u32[]{:S(2)}) %collective-permute-start.1) | collective-permute-done | bytes 409632 | tf_op jit(solution)/shard_map/ppermute | solution.py:527
  6.1 1.6 copy-done
  7.7 1.0 copy-done.3
  8.8 0.9 copy-done.5
  9.7 1.0 copy-done.7
  11.4 5.4 %one.1 = (f32[2,256,320]{2,1,0:T(8,128)S(1)}, f32[2,8,320]{2,1,0:T(8,128)S(1)}, bf16[2,256,320]{2,1,0:T(8,128)(2,1)S(1)}, bf16[2,256,320]{2,1,0:T(8,128)(2,1)S(1)}, bf16[256,320]{1,0:T(8,128)(2,1)S(1)}) custom-call(s32[3]{0:T(128)S(1)} %pad_add_fusion.where, s32[2,2]{1,0:T(2,128)S(1)} %copy-done.9, bf16[2,256,320]{2,1,0:T(8,128)(2,1)S(1)} %bitcast.25, ...), custom_call_target="tpu_custom_call" | custom-call | flops 943718400 | bytes 6543388 | tf_op jit(solution)/shard_map/one/pallas_call | solution.py:500
  16.8 1.4 collective-permute-start.2
  18.2 7.8 %collective-permute-done.2.x = bf16[256,320]{1,0:T(8,128)(2,1)S(1)} collective-permute-done((bf16[256,320]{1,0:T(8,128)(2,1)S(1)}, bf16[256,320]{1,0:T(8,128)(2,1)S(1)}, u32[]{:S(2)}, u32[]{:S(2)}) %collective-permute-start.2) | collective-permute-done | bytes 163872 | tf_op jit(solution)/shard_map/ppermute | solution.py:599
  26.0 9.0 %two.1 = (f32[2,256,320]{2,1,0:T(8,128)S(1)}, f32[2,8,320]{2,1,0:T(8,128)S(1)}, bf16[2,256,320]{2,1,0:T(8,128)(2,1)S(1)}, f32[2,256,320]{2,1,0:T(8,128)S(1)}, f3...) custom-call(s32[3]{0:T(128)S(1)} %pad_add_fusion.where, ...), custom_call_target="tpu_custom_call" | custom-call | flops 1887436800 | bytes 10741788 | tf_op jit(solution)/shard_map/two/pallas_call | solution.py:500
  35.1 1.5 collective-permute-start.4
  36.5 4.0 %collective-permute-done.4.x = bf16[256,320]{1,0:T(8,128)(2,1)S(1)} collective-permute-done((bf16[256,320]{1,0:T(8,128)(2,1)S(1)}, bf16[256,320]{1,0:T(8,128)(2,1)S(1)}, u32[]{:S(2)}, u32[]{:S(2)}) %collective-permute-start.4) | collective-permute-done | bytes 163872 | tf_op jit(solution)/shard_map/ppermute | solution.py:602
  40.5 7.5 %three.1 = (bf16[2,256,320]{2,1,0:T(8,128)(2,1)S(1)}, bf16[2,256,320]{2,1,0:T(8,128)(2,1)S(1)}, bf16[2,256,320]{2,1,0:T(8,128)(2,1)S(1)}, bf16[256,320]{1,0:T(8,128)(2,1)S(1)}) custom-call(s32[3]{0:T(128)S(1)} %pad_add_fusion.where, s32[2,2]{1,0:T(2,128)S(1)} %copy-done.9, bf16[256,320]{1,0:T(8,128)(2,1)S(1)} %collective-permute-done.4.x, ...), custom_call_target="tpu_custom_call" | custom-call | flops 1415577600 | bytes 6686748 | tf_op jit(solution)/shard_map/three/pallas_call | solution.py:500
  48.0 1.5 collective-permute-start.5
  49.5 6.1 %collective-permute-done.5.x = bf16[256,320]{1,0:T(8,128)(2,1)S(1)} collective-permute-done((bf16[256,320]{1,0:T(8,128)(2,1)S(1)}, bf16[256,320]{1,0:T(8,128)(2,1)S(1)}, u32[]{:S(2)}, u32[]{:S(2)}) %collective-permute-start.5) | collective-permute-done | bytes 163872 | tf_op jit(solution)/shard_map/ppermute | solution.py:599
  55.6 8.7 %four.1 = (bf16[2,256,320]{2,1,0:T(8,128)(2,1)S(1)}, bf16[2,256,320]{2,1,0:T(8,128)(2,1)S(1)}, bf16[256,320]{1,0:T(8,128)(2,1)S(1)}) custom-call(s32[3]{0:T(128)S(1)} %pad_add_fusion.where, s32[2,2]{1,0:T(2,128)S(1)} %copy-done.10, bf16[256,320]{1,0:T(8,128)(2,1)S(1)} %collective-permute-done.5.x, bf16[2,320,320]{2,1,0:T(8,128)(2,1)S(1)} %bitcast.23, ...), custom_call_target="tpu_custom_call" | custom-call | flops 1887436800 | bytes 10741788 | tf_op jit(solution)/shard_map/four/pallas_call | solution.py:500
  64.3 1.5 collective-permute-start.6
  65.8 3.4 %weights.1 = (f32[7680,128]{1,0:T(8,128)S(1)}, bf16[7680,128]{1,0:T(8,128)(2,1)S(1)}) custom-call(s32[3]{0:T(128)S(1)} %pad_add_fusion.where, bf16[2,256,320]{2,1,0:T(8,128)(2,1)S(1)} %get-tuple-element.62.a_hidden, bf16[2,256,320]{2,1,0:T(8,128)(2,1)S(1)} %get-tuple-element.63.a_cots, bf16[2,256,320]{2,1,0:T(8,128)(2,1)S(1)} %get-tuple-element.64.b_hidden, ...), custom_call_target="tpu_custom_call" | custom-call | flops 943718400 | bytes 7208972 | tf_op jit(solution)/shard_map/weights/pallas_call | solution.py:500
  69.3 4.7 %five.1 = (f32[7680,128]{1,0:T(8,128)S(1)}, bf16[7680,128]{1,0:T(8,128)(2,1)S(1)}) custom-call(s32[3]{0:T(128)S(1)} %pad_add_fusion.where, s32[2,2]{1,0:T(2,128)S(1)} %copy-done.10, bf16[256,320]{1,0:T(8,128)(2,1)S(1)} %collective-permute-done.6.x, bf16[2,320,320]{2,1,0:T(8,128)(2,1)S(1)} %bitcast.24, ...), custom_call_target="tpu_custom_call" | custom-call | flops 1415577600 | bytes 12769308 | tf_op jit(solution)/shard_map/five/pallas_call | solution.py:500
  74.6 3.6 %collective-permute-done.7.first_other = bf16[7680,128]{1,0:T(8,128)(2,1)S(1)} collective-permute-done((bf16[7680,128]{1,0:T(8,128)(2,1)S(1)}, bf16[7680,128]{1,0:T(8,128)(2,1)S(1)}, u32[]{:S(2)}, u32[]{:S(2)}) %collective-permute-start.7) | collective-permute-done | bytes 1966112 | tf_op jit(solution)/shard_map/ppermute | solution.py:527
  79.0 57.0 %all_to_all.10.parts = bf16[16,960,128]{2,1,0:T(8,128)(2,1)S(1)} all-to-all(bf16[16,960,128]{2,1,0:T(8,128)(2,1)S(1)} %core_add.1), channel_id=1, replica_groups=mesh['near'=2,'core'=2,'z_high'=4,'z_low'=2,'far'=2,'y'=4] {'z_low','far..., dimensions={0} | all-to-all | bytes 7864320 | tf_op jit(solution)/shard_map/all_to_all | solution.py:536
  136.0 1.4 block_sums.1
  137.4 3.4 %collective-permute-start.9 = (bf16[2,120,128]{2,1,0:T(8,128)(2,1)S(1)}, bf16[2,120,128]{2,1,0:T(8,128)(2,1)S(1)}, u32[]{:S(2)}, u32[]{:S(2)}) collective-permute-start(bf16[2,120,128]{2,1,0:T(8,128)(2,1)S(1)} %get-tuple-element.69), channel_id=1, source_target_pairs={{0,16},{16,32},{32,48},{48,0},{1,17},{17,33},{33,49},{49,1},{2,18}... | collective-permute-start | bytes 184328 | tf_op jit(solution)/shard_map/ppermute | solution.py:541
  140.8 4.5 %collective-permute-start.10 = (bf16[2,120,128]{2,1,0:T(8,128)(2,1)S(1)}, bf16[2,120,128]{2,1,0:T(8,128)(2,1)S(1)}, u32[]{:S(2)}, u32[]{:S(2)}) collective-permute-start(bf16[2,120,128]{2,1,0:T(8,128)(2,1)S(1)} %get-tuple-element.70), channel_id=1, source_target_pairs={{0,32},{16,48},{32,0},{48,16},{1,33},{17,49},{33,1},{49,17},{2,34}... | collective-permute-start | bytes 184328 | tf_op jit(solution)/shard_map/ppermute | solution.py:541
  145.3 2.6 %collective-permute-start.11 = (bf16[2,120,128]{2,1,0:T(8,128)(2,1)S(1)}, bf16[2,120,128]{2,1,0:T(8,128)(2,1)S(1)}, u32[]{:S(2)}, u32[]{:S(2)}) collective-permute-start(bf16[2,120,128]{2,1,0:T(8,128)(2,1)S(1)} %get-tuple-element.71), channel_id=1, source_target_pairs={{0,48},{16,0},{32,16},{48,32},{1,49},{17,1},{33,17},{49,33},{2,50}... | collective-permute-start | bytes 184328 | tf_op jit(solution)/shard_map/ppermute | solution.py:541
  147.9 1.6 collective-permute-done.10.rest_1_
  149.5 1.8 collective-permute-done.11.rest_2_
  151.3 3.7 %collective-permute-start.14 = (bf16[2,120,128]{2,1,0:T(8,128)(2,1)S(1)}, bf16[2,120,128]{2,1,0:T(8,128)(2,1)S(1)}, u32[]{:S(2)}, u32[]{:S(2)}) collective-permute-start(bf16[2,120,128]{2,1,0:T(8,128)(2,1)S(1)} %layer_sums.1.rest_0_), channel_id=1, source_target_pairs={{0,48},{16,0},{32,16},{48,32},{1,49},{17,1},{33,17},{49,33},{2,50}... | collective-permute-start | bytes 184328 | tf_op jit(solution)/shard_map/ppermute | solution.py:541
  155.0 2.1 collective-permute-start.13
  157.7 6.0 %collective-permute-done.13.rest_2_ = bf16[2,120,128]{2,1,0:T(8,128)(2,1)S(1)} collective-permute-done((bf16[2,120,128]{2,1,0:T(8,128)(2,1)S(1)}, bf16[2,120,128]{2,1,0:T(8,128)(2,1)S(1)}, u32[]{:S(2)}, u32[]{:S(2)}) %collective-permute-start.13) | collective-permute-done | bytes 61472 | tf_op jit(solution)/shard_map/ppermute | solution.py:541
  164.0 0.9 assemble.1
  164.9 49.9 %all_to_all.11.packed = bf16[16,960,128]{2,1,0:T(8,128)(2,1)S(1)} all-to-all(bf16[16,960,128]{2,1,0:T(8,128)(2,1)S(1)} %assemble.1), channel_id=1, replica_groups=mesh['near'=2,'core'=2,'z_high'=4,'z_low'=2,'far'=2,'y'=4] {'z_low','far..., dimensions={0} | all-to-all | bytes 7864320 | tf_op jit(solution)/shard_map/all_to_all | solution.py:536
  214.9 3.7 %unpack.1 = (f32[2,1440,320]{2,1,0:T(8,128)}, f32[2,1440,320]{2,1,0:T(8,128)}) custom-call(bf16[16,960,128]{2,1,0:T(8,128)(2,1)S(1)} %all_to_all.11.packed), custom_call_target="tpu_custom_call" | custom-call | tf_op jit(solution)/shard_map/unpack/pallas_call | solution.py:568
  (38 shorter events, 4.9 us)
Async XLA Ops:
  0.6 5.3 %collective-permute-start = (bf16[9,320,320]{2,1,0:T(8,128)(2,1)}, bf16[9,320,320]{2,1,0:T(8,128)(2,1)S(1)}, u32[]{:S(2)}, u32[]{:S(2)}) collective-permute-start(bf16[9,320,320]{2,1,0:T(8,128)(2,1)} %bitcast.10), channel_id=1, source_target_pairs={{0,64},{64,0},{1,65},{65,1},{2,66},{66,2},{3,67},{67,3},{4,68},{68... | collective-permute-start | bytes 5529608 | tf_op jit(solution)/shard_map/ppermute | solution.py:527
  0.7 5.2 %collective-permute-start.1 = (bf16[2,320,320]{2,1,0:T(8,128)(2,1)}, bf16[2,320,320]{2,1,0:T(8,128)(2,1)S(1)}, u32[]{:S(2)}, u32[]{:S(2)}) collective-permute-start(bf16[2,320,320]{2,1,0:T(8,128)(2,1)} %bitcast.19), channel_id=1, source_target_pairs={{0,64},{64,0},{1,65},{65,1},{2,66},{66,2},{3,67},{67,3},{4,68},{68... | collective-permute-start | bytes 1228808 | tf_op jit(solution)/shard_map/ppermute | solution.py:527
  6.0 20.1 %collective-permute-start.3 = (bf16[9,320,320]{2,1,0:T(8,128)(2,1)}, bf16[9,320,320]{2,1,0:T(8,128)(2,1)S(1)}, u32[]{:S(2)}, u32[]{:S(2)}) collective-permute-start(bf16[9,320,320]{2,1,0:T(8,128)(2,1)} %bitcast.15), channel_id=1, source_target_pairs={{0,64},{64,0},{1,65},{65,1},{2,66},{66,2},{3,67},{67,3},{4,68},{68... | collective-permute-start | bytes 5529608 | tf_op jit(solution)/shard_map/ppermute | solution.py:527
  6.1 1.6 copy-start
  7.7 1.0 copy-start.3
  8.8 0.9 copy-start.5
  9.7 1.0 copy-start.7
  10.7 0.7 copy-start.9
  11.4 14.7 %copy-start.1 = (bf16[1,3,3,320,320]{4,3,2,1,0:T(8,128)(2,1)S(1)}, bf16[1,3,3,320,320]{4,3,2,1,0:T(8,128)(2,1)}, u32[]{:S(2)}) copy-start(bf16[1,3,3,320,320]{4,3,2,1,0:T(8,128)(2,1)} %param.12) | copy-start | bytes 5529604
  11.4 14.7 %copy-start.2 = (bf16[1,3,3,320,320]{4,3,2,1,0:T(8,128)(2,1)S(1)}, bf16[1,3,3,320,320]{4,3,2,1,0:T(8,128)(2,1)}, u32[]{:S(2)}) copy-start(bf16[1,3,3,320,320]{4,3,2,1,0:T(8,128)(2,1)} %param.13) | copy-start | bytes 5529604
  11.4 14.7 %copy-start.6 = (bf16[320,320]{1,0:T(8,128)(2,1)S(1)}, bf16[320,320]{1,0:T(8,128)(2,1)}, u32[]{:S(2)}) copy-start(bf16[320,320]{1,0:T(8,128)(2,1)} %constant.26.clone.matrix) | copy-start | bytes 614404
  16.8 23.7 %copy-start.8 = (bf16[2,16,16,320]{3,2,1,0:T(8,128)(2,1)S(1)}, bf16[2,16,16,320]{3,2,1,0:T(8,128)(2,1)}, u32[]{:S(2)}) copy-start(bf16[2,16,16,320]{3,2,1,0:T(8,128)(2,1)} %param.9) | copy-start | bytes 983044
  16.8 9.2 %collective-permute-start.2 = (bf16[256,320]{1,0:T(8,128)(2,1)S(1)}, bf16[256,320]{1,0:T(8,128)(2,1)S(1)}, u32[]{:S(2)}, u32[]{:S(2)}) collective-permute-start(bf16[256,320]{1,0:T(8,128)(2,1)S(1)} %get-tuple-element.44), channel_id=1, source_target_pairs={{0,128},{1,129},{2,130},{3,131},{4,132},{5,133},{6,134},{7,135},{8... | collective-permute-start | bytes 491528 | tf_op jit(solution)/shard_map/ppermute | solution.py:599
  35.1 20.6 %copy-start.10 = (s32[2,2]{1,0:T(2,128)S(1)}, s32[2,2]{1,0:T(2,128)}, u32[]{:S(2)}) copy-start(s32[2,2]{1,0:T(2,128)} %bucket.9) | copy-start | bytes 52
  35.1 5.4 %collective-permute-start.4 = (bf16[256,320]{1,0:T(8,128)(2,1)S(1)}, bf16[256,320]{1,0:T(8,128)(2,1)S(1)}, u32[]{:S(2)}, u32[]{:S(2)}) collective-permute-start(bf16[256,320]{1,0:T(8,128)(2,1)S(1)} %get-tuple-element.46), channel_id=1, source_target_pairs={{128,0},{129,1},{130,2},{131,3},{132,4},{133,5},{134,6},{135,7},{1... | collective-permute-start | bytes 491528 | tf_op jit(solution)/shard_map/ppermute | solution.py:602
  48.0 7.6 %collective-permute-start.5 = (bf16[256,320]{1,0:T(8,128)(2,1)S(1)}, bf16[256,320]{1,0:T(8,128)(2,1)S(1)}, u32[]{:S(2)}, u32[]{:S(2)}) collective-permute-start(bf16[256,320]{1,0:T(8,128)(2,1)S(1)} %get-tuple-element.48), channel_id=1, source_target_pairs={{0,128},{1,129},{2,130},{3,131},{4,132},{5,133},{6,134},{7,135},{8... | collective-permute-start | bytes 491528 | tf_op jit(solution)/shard_map/ppermute | solution.py:599
  55.6 13.7 %copy-start.4 = (bf16[1,2,320,320]{3,2,1,0:T(8,128)(2,1)S(1)}, bf16[1,2,320,320]{3,2,1,0:T(8,128)(2,1)}, u32[]{:S(2)}) copy-start(bf16[1,2,320,320]{3,2,1,0:T(8,128)(2,1)} %param.14) | copy-start | bytes 1228804
  64.3 5.0 %collective-permute-start.6 = (bf16[256,320]{1,0:T(8,128)(2,1)S(1)}, bf16[256,320]{1,0:T(8,128)(2,1)S(1)}, u32[]{:S(2)}, u32[]{:S(2)}) collective-permute-start(bf16[256,320]{1,0:T(8,128)(2,1)S(1)} %get-tuple-element.53), channel_id=1, source_target_pairs={{128,0},{129,1},{130,2},{131,3},{132,4},{133,5},{134,6},{135,7},{1... | collective-permute-start | bytes 491528 | tf_op jit(solution)/shard_map/ppermute | solution.py:602
  69.2 5.4 %collective-permute-start.8 = (bf16[7680,128]{1,0:T(8,128)(2,1)S(1)}, bf16[7680,128]{1,0:T(8,128)(2,1)S(1)}, u32[]{:S(2)}, u32[]{:S(2)}) collective-permute-start(bf16[7680,128]{1,0:T(8,128)(2,1)S(1)} %get-tuple-element.67), channel_id=1, source_target_pairs={{0,64},{64,0},{1,65},{65,1},{2,66},{66,2},{3,67},{67,3},{4,68},{68... | collective-permute-start | bytes 5898248 | tf_op jit(solution)/shard_map/ppermute | solution.py:527
  74.1 4.2 %collective-permute-start.7 = (bf16[7680,128]{1,0:T(8,128)(2,1)S(1)}, bf16[7680,128]{1,0:T(8,128)(2,1)S(1)}, u32[]{:S(2)}, u32[]{:S(2)}) collective-permute-start(bf16[7680,128]{1,0:T(8,128)(2,1)S(1)} %get-tuple-element.61), channel_id=1, source_target_pairs={{0,64},{64,0},{1,65},{65,1},{2,66},{66,2},{3,67},{67,3},{4,68},{68... | collective-permute-start | bytes 5898248 | tf_op jit(solution)/shard_map/ppermute | solution.py:527
  137.4 10.5 %collective-permute-start.9 = (bf16[2,120,128]{2,1,0:T(8,128)(2,1)S(1)}, bf16[2,120,128]{2,1,0:T(8,128)(2,1)S(1)}, u32[]{:S(2)}, u32[]{:S(2)}) collective-permute-start(bf16[2,120,128]{2,1,0:T(8,128)(2,1)S(1)} %get-tuple-element.69), channel_id=1, source_target_pairs={{0,16},{16,32},{32,48},{48,0},{1,17},{17,33},{33,49},{49,1},{2,18}... | collective-permute-start | bytes 184328 | tf_op jit(solution)/shard_map/ppermute | solution.py:541
  140.8 8.8 %collective-permute-start.10 = (bf16[2,120,128]{2,1,0:T(8,128)(2,1)S(1)}, bf16[2,120,128]{2,1,0:T(8,128)(2,1)S(1)}, u32[]{:S(2)}, u32[]{:S(2)}) collective-permute-start(bf16[2,120,128]{2,1,0:T(8,128)(2,1)S(1)} %get-tuple-element.70), channel_id=1, source_target_pairs={{0,32},{16,48},{32,0},{48,16},{1,33},{17,49},{33,1},{49,17},{2,34}... | collective-permute-start | bytes 184328 | tf_op jit(solution)/shard_map/ppermute | solution.py:541
  145.3 6.0 %collective-permute-start.11 = (bf16[2,120,128]{2,1,0:T(8,128)(2,1)S(1)}, bf16[2,120,128]{2,1,0:T(8,128)(2,1)S(1)}, u32[]{:S(2)}, u32[]{:S(2)}) collective-permute-start(bf16[2,120,128]{2,1,0:T(8,128)(2,1)S(1)} %get-tuple-element.71), channel_id=1, source_target_pairs={{0,48},{16,0},{32,16},{48,32},{1,49},{17,1},{33,17},{49,33},{2,50}... | collective-permute-start | bytes 184328 | tf_op jit(solution)/shard_map/ppermute | solution.py:541
  151.3 6.4 %collective-permute-start.14 = (bf16[2,120,128]{2,1,0:T(8,128)(2,1)S(1)}, bf16[2,120,128]{2,1,0:T(8,128)(2,1)S(1)}, u32[]{:S(2)}, u32[]{:S(2)}) collective-permute-start(bf16[2,120,128]{2,1,0:T(8,128)(2,1)S(1)} %layer_sums.1.rest_0_), channel_id=1, source_target_pairs={{0,48},{16,0},{32,16},{48,32},{1,49},{17,1},{33,17},{49,33},{2,50}... | collective-permute-start | bytes 184328 | tf_op jit(solution)/shard_map/ppermute | solution.py:541
  155.0 8.6 %collective-permute-start.13 = (bf16[2,120,128]{2,1,0:T(8,128)(2,1)S(1)}, bf16[2,120,128]{2,1,0:T(8,128)(2,1)S(1)}, u32[]{:S(2)}, u32[]{:S(2)}) collective-permute-start(bf16[2,120,128]{2,1,0:T(8,128)(2,1)S(1)} %layer_sums.1.rest_0_), channel_id=1, source_target_pairs={{0,32},{16,48},{32,0},{48,16},{1,33},{17,49},{33,1},{49,17},{2,34}... | collective-permute-start | bytes 184328 | tf_op jit(solution)/shard_map/ppermute | solution.py:541
  157.1 7.0 %collective-permute-start.12 = (bf16[2,120,128]{2,1,0:T(8,128)(2,1)S(1)}, bf16[2,120,128]{2,1,0:T(8,128)(2,1)S(1)}, u32[]{:S(2)}, u32[]{:S(2)}) collective-permute-start(bf16[2,120,128]{2,1,0:T(8,128)(2,1)S(1)} %layer_sums.1.rest_0_), channel_id=1, source_target_pairs={{0,16},{16,32},{32,48},{48,0},{1,17},{17,33},{33,49},{49,1},{2,18}... | collective-permute-start | bytes 184328 | tf_op jit(solution)/shard_map/ppermute | solution.py:541
